TPU v7x, 512 devices: a whole 4x4x16 slice. The times are simulated.
512 devices in a mesh: tm: 16 (over x, y_lo, core), slab: 32 (over z, y_hi).
Axes of the slice: x: 4, y: 4 (y_hi: 2, y_lo: 2; y = y_hi * 2 + y_lo), z: 16, core: 2. Of those that a mesh axis runs over, the one named last changes fastest.
Arguments:
- node_values: float32 [16, 3, 2, 128, 16, 128], P('tm', None, None, 'slab'), may hold values from 0 to 1
- start_state: float32 [16, 2, 128, 16, 128], P('tm', None, 'slab'), may hold values from 0 to 1
- feed_rate: float32 [128, 16, 128], P('slab'), may hold values from 0.02 to 0.08
- kill_rate: float32 [128, 16, 128], P('slab'), may hold values from 0.03 to 0.1
Outputs:
- swept_nodes: float32 [16, 3, 2, 128, 16, 128], P('tm', None, None, 'slab')
All inputs are finite; a program needn't handle non-finite values.
Results may differ from a plain program's by a relative error of at most 0.0003.
Values sent between devices are 32-bit elements; how exact they have to be, the bound alone decides.
No kernel may reach another device: no remote copies, remote signals or barrier semaphores. Data moves between devices by JAX's collectives and lax.ppermute only.
A program may use at most 64 MiB of HBM per device.

v0:
```python
import jax
import jax.numpy as jnp
from jax import lax
from jax.sharding import PartitionSpec as P

SOLVES = 2


slice_length = 2.0
half_step = 1.0
weights_first = (5.0 / 24.0, 1.0 / 3.0, -1.0 / 24.0)
weights_second = (-1.0 / 24.0, 1.0 / 3.0, 5.0 / 24.0)
diffusion = (0.1, 0.05)


def with_halo(block, sides, width):
    for axis, dim in sides:
        count = lax.axis_size(axis)
        forward = [(i, i + 1) for i in range(count - 1)]
        forward.append((count - 1, 0))
        backward = [(target, source) for source, target in forward]
        low = lax.ppermute(
            lax.slice_in_dim(block, block.shape[dim] - width, None, axis=dim), axis, forward
        )
        high = lax.ppermute(lax.slice_in_dim(block, 0, width, axis=dim), axis, backward)
        block = jnp.concatenate([low, block, high], axis=dim)
    return block


def shifted(value, axis, steps):
    count = lax.axis_size(axis)
    pairs = [(source, (source + steps) % count) for source in range(count)]
    return lax.ppermute(value, axis, pairs)


def partner_2(array, axis, stride):
    return lax.ppermute(array, axis, [(i, i ^ 1 << stride) for i in range(lax.axis_size(axis))])


def from_behind(array, axis, by):
    count = lax.axis_size(axis)
    pairs = [(i, i + by) for i in range(count) if 0 <= i + by < count]
    return lax.ppermute(array, axis, pairs)


def stencil_line(values, dimension):
    nearest = jnp.roll(values, 1, axis=dimension) + jnp.roll(values, -1, axis=dimension)
    farther = jnp.roll(values, 2, axis=dimension) + jnp.roll(values, -2, axis=dimension)
    return (16.0 * nearest - farther - 30.0 * values) / 12.0


def stencil_depth(padded):
    middle = padded[..., 2:-2, :, :]
    nearest = padded[..., 1:-3, :, :] + padded[..., 3:-1, :, :]
    farther = padded[..., :-4, :, :] + padded[..., 4:, :, :]
    return (16.0 * nearest - farther - 30.0 * middle) / 12.0


def explicit_term(padded, spread):
    middle = padded[..., 2:-2, :, :]
    laplace = spread * (stencil_depth(padded) + stencil_line(middle, -2)) + stencil_line(middle, -1)
    coefficient = jnp.array(diffusion, dtype=jnp.float32).reshape(2, 1, 1, 1)
    return coefficient * laplace


def reaction(fields, feed_rate, kill_rate):
    substrate = fields[..., 0, :, :, :]
    catalyst = fields[..., 1, :, :, :]
    growth = substrate * catalyst * catalyst
    return jnp.stack(
        [feed_rate * (1.0 - substrate) - growth, growth - (feed_rate + kill_rate) * catalyst],
        axis=-4,
    )


def node_solve(target, initial, feed_rate, kill_rate):
    substrate = initial[0]
    catalyst = initial[1]
    for repeat_index in range(SOLVES):
        growth = substrate * catalyst * catalyst
        substrate_next = (target[0] + half_step * (feed_rate - growth)) / (
            1.0 + half_step * feed_rate
        )
        catalyst_next = (target[1] + half_step * growth) / (
            1.0 + half_step * (feed_rate + kill_rate)
        )
        substrate, catalyst = (substrate_next, catalyst_next)
    return jnp.stack([substrate, catalyst])


def restrict(values):
    extent = values.shape
    blocks = values.reshape(extent[:-3] + (extent[-3] // 2, 2, extent[-2] // 2, 2, extent[-1]))
    return 0.25 * (
        blocks[..., 0, :, 0, :]
        + blocks[..., 0, :, 1, :]
        + blocks[..., 1, :, 0, :]
        + blocks[..., 1, :, 1, :]
    )


def prolong(values):
    extent = values.shape
    widened = jnp.broadcast_to(
        values[..., :, None, :, None, :], extent[:-3] + (extent[-3], 2, extent[-2], 2, extent[-1])
    )
    return widened.reshape(extent[:-3] + (2 * extent[-3], 2 * extent[-2], extent[-1]))


def weighted(weights, tendency):
    return slice_length * (
        weights[0] * tendency[0] + weights[1] * tendency[1] + weights[2] * tendency[2]
    )


def fine_rims(stacked):
    return with_halo(stacked, (("slab", 2),), 2)


def pair_rim(rim_part, offset):
    return shifted(rim_part, "slab", offset)


def coarse_padded(stacked):
    lower_rim = pair_rim(stacked[:, :, -2:], 2)
    upper_rim = pair_rim(stacked[:, :, :2], -2)
    return jnp.concatenate([lower_rim, stacked, upper_rim], axis=2)


def join_pair(own_part, their_part, parity):
    even_order = jnp.concatenate([own_part, their_part], axis=-3)
    odd_order = jnp.concatenate([their_part, own_part], axis=-3)
    return jnp.where(parity == 0, even_order, odd_order)


def fine_sweep(previous, start, feed_rate, kill_rate):
    padded = fine_rims(jnp.concatenate([previous, start[None]], axis=0))
    explicit_all = explicit_term(padded, 1.0)
    explicit_old = explicit_all[:3]
    explicit_start = explicit_all[3]
    tendency = explicit_old + reaction(previous, feed_rate, kill_rate)
    integral_one = weighted(weights_first, tendency)
    integral_two = weighted(weights_second, tendency)
    target = (
        start
        + half_step * (explicit_start - explicit_old[0])
        - half_step * reaction(previous[1], feed_rate, kill_rate)
        + integral_one
    )
    first_node = node_solve(target, previous[1], feed_rate, kill_rate)
    explicit_first = explicit_term(fine_rims(first_node[None]), 1.0)[0]
    target = (
        first_node
        + half_step * (explicit_first - explicit_old[1])
        - half_step * reaction(previous[2], feed_rate, kill_rate)
        + integral_two
    )
    second_node = node_solve(target, previous[2], feed_rate, kill_rate)
    return (jnp.stack([start, first_node, second_node]), explicit_start, explicit_first)


def body(node_values, start_state, feed_rate, kill_rate):
    previous = node_values[0]
    start = start_state[0]
    tm_index = lax.axis_index("tm")
    swept, explicit_start, explicit_first = fine_sweep(previous, start, feed_rate, kill_rate)
    explicit_last = explicit_term(fine_rims(swept[2:]), 1.0)
    fine_tendency = jnp.concatenate(
        [explicit_start[None], explicit_first[None], explicit_last], axis=0
    ) + reaction(swept, feed_rate, kill_rate)
    fine_integral = jnp.stack(
        [
            restrict(weighted(weights_first, fine_tendency)),
            restrict(weighted(weights_second, fine_tendency)),
        ]
    )
    coarse_old = restrict(swept)
    coarse_start = restrict(start)
    coarse_rates = jnp.stack([restrict(feed_rate), restrict(kill_rate)])
    half_depth = coarse_old.shape[2]
    parity = lax.axis_index("slab") % 2
    partner = partner_2((coarse_old, fine_integral, coarse_start, coarse_rates), "slab", 0)
    coarse_old = join_pair(coarse_old, partner[0], parity)
    fine_integral = join_pair(fine_integral, partner[1], parity)
    coarse_start = join_pair(coarse_start, partner[2], parity)
    coarse_rates = join_pair(coarse_rates, partner[3], parity)
    coarse_feed = coarse_rates[0]
    coarse_kill = coarse_rates[1]
    explicit_coarse = explicit_term(coarse_padded(coarse_old[:2]), 0.25)
    base_one = (
        fine_integral[0]
        - half_step * explicit_coarse[0]
        - half_step * reaction(coarse_old[1], coarse_feed, coarse_kill)
    )
    base_two = (
        fine_integral[1]
        - half_step * explicit_coarse[1]
        - half_step * reaction(coarse_old[2], coarse_feed, coarse_kill)
    )

    def coarse_sweep(begin_state):
        explicit_begin = explicit_term(coarse_padded(begin_state[None]), 0.25)[0]
        first_node = node_solve(
            begin_state + half_step * explicit_begin + base_one,
            coarse_old[1],
            coarse_feed,
            coarse_kill,
        )
        explicit_next = explicit_term(coarse_padded(first_node[None]), 0.25)[0]
        second_node = node_solve(
            first_node + half_step * explicit_next + base_two,
            coarse_old[2],
            coarse_feed,
            coarse_kill,
        )
        return (first_node, second_node)

    first_node, second_node = coarse_sweep(coarse_start)

    def chain_turn(step_index, chain_state):
        incoming = from_behind(chain_state[2], "tm", 1)
        begin_state = jnp.where(tm_index == 0, coarse_start, incoming)
        first_next, second_next = coarse_sweep(begin_state)
        return (begin_state, first_next, second_next)

    chain_state = lax.fori_loop(
        0, lax.axis_size("tm") - 1, chain_turn, (coarse_start, first_node, second_node)
    )
    correction = jnp.stack([chain_state[0], chain_state[1], chain_state[2]]) - coarse_old
    correction = lax.dynamic_slice_in_dim(correction, parity * half_depth, half_depth, 2)
    updated = swept + prolong(correction)
    incoming = from_behind(updated[2], "tm", 1)
    start_again = jnp.where(tm_index == 0, start, incoming)
    result, unused_start, unused_first = fine_sweep(updated, start_again, feed_rate, kill_rate)
    return result[None]


def solution(mesh):
    return jax.shard_map(
        body,
        mesh=mesh,
        in_specs=(
            P("tm", None, None, "slab", None, None),
            P("tm", None, "slab", None, None),
            P("slab", None, None),
            P("slab", None, None),
        ),
        out_specs=P("tm", None, None, "slab", None, None),
        check_vma=False,
    )
```

profile of v0, /device:TPU:6, one launch (start us, length us, event | category | flops | bytes accessed | tf_op | source)
XLA Modules:
  0.0 513.5 jit_solution(16346681686312408613)
XLA Ops:
  1.7 5.1 collective-permute-start.5
  6.8 10.9 %collective-permute-start.6 = (f32[4,2,2,16,128]{4,3,2,1,0:T(8,128)}, f32[4,2,2,16,128]{4,3,2,1,0:T(8,128)}, u32[]{:S(2)}, u32[]{:S(2)}) collective-permute-start(f32[4,2,2,16,128]{4,3,2,1,0:T(8,128)} %get-tuple-element.475), channel_id=1, source_target_pairs={{1,0},{2,1},{3,2},{4,3},{5,4},{6,5},{7,6},{8,7},{9,8},{10,9},{11,1... | collective-permute-start | bytes 393224 | tf_op jit(solution)/shard_map/ppermute | solution.py:25
  20.4 5.4 %collective-permute-start.9 = (f32[2,2,8,128]{3,2,1,0:T(8,128)S(1)}, f32[2,2,8,128]{3,2,1,0:T(8,128)}, u32[]{:S(2)}, u32[]{:S(2)}) collective-permute-start(f32[2,2,8,128]{3,2,1,0:T(8,128)S(1)} %bitcast.546), channel_id=1, source_target_pairs={{0,1},{1,0},{2,3},{3,2},{4,5},{5,4},{6,7},{7,6},{8,9},{9,8},{10,11... | collective-permute-start | bytes 49160 | tf_op jit(solution)/shard_map/ppermute | solution.py:37
  32.9 5.1 collective-permute-start.11
  46.2 6.1 %collective-permute-start.8 = (f32[1,2,2,16,128]{4,3,2,1,0:T(8,128)S(1)}, f32[1,2,2,16,128]{4,3,2,1,0:T(8,128)S(1)}, u32[]{:S(2)}, u32[]{:S(2)}) collective-permute-start(f32[1,2,2,16,128]{4,3,2,1,0:T(8,128)S(1)} %get-tuple-element.558), channel_id=1, source_target_pairs={{1,0},{2,1},{3,2},{4,3},{5,4},{6,5},{7,6},{8,7},{9,8},{10,9},{11,1... | collective-permute-start | bytes 98312 | tf_op jit(solution)/shard_map/ppermute | solution.py:25
  57.4 7.0 %collective-permute-start.13 = (f32[1,2,2,16,128]{4,3,2,1,0:T(8,128)S(1)}, f32[1,2,2,16,128]{4,3,2,1,0:T(8,128)S(1)}, u32[]{:S(2)}, u32[]{:S(2)}) collective-permute-start(f32[1,2,2,16,128]{4,3,2,1,0:T(8,128)S(1)} %get-tuple-element.556), channel_id=1, source_target_pairs={{1,0},{2,1},{3,2},{4,3},{5,4},{6,5},{7,6},{8,7},{9,8},{10,9},{11,1... | collective-permute-start | bytes 98312 | tf_op jit(solution)/shard_map/ppermute | solution.py:25
  68.4 5.4 %collective-permute-start.14 = (f32[2,2,2,8,128]{4,3,2,1,0:T(8,128)S(1)}, f32[2,2,2,8,128]{4,3,2,1,0:T(8,128)S(1)}, u32[]{:S(2)}, u32[]{:S(2)}) collective-permute-start(f32[2,2,2,8,128]{4,3,2,1,0:T(8,128)S(1)} %pad_maximum_fusion.25), channel_id=1, source_target_pairs={{0,1},{1,0},{2,3},{3,2},{4,5},{5,4},{6,7},{7,6},{8,9},{9,8},{10,11... | collective-permute-start | bytes 98312 | tf_op jit(solution)/shard_map/ppermute | solution.py:37
  76.3 5.3 %collective-permute-start.17 = (f32[2,2,2,8,128]{4,3,2,1,0:T(8,128)S(1)}, f32[2,2,2,8,128]{4,3,2,1,0:T(8,128)S(1)}, u32[]{:S(2)}, u32[]{:S(2)}) collective-permute-start(f32[2,2,2,8,128]{4,3,2,1,0:T(8,128)S(1)} %get-tuple-element.512), channel_id=1, source_target_pairs={{0,30},{1,31},{2,0},{3,1},{4,2},{5,3},{6,4},{7,5},{8,6},{9,7},{10,... | collective-permute-start | bytes 98312 | tf_op jit(solution)/shard_map/ppermute | solution.py:33
  87.2 5.4 %collective-permute-start.20 = (f32[1,2,2,8,128]{4,3,2,1,0:T(8,128)S(1)}, f32[1,2,2,8,128]{4,3,2,1,0:T(8,128)S(1)}, u32[]{:S(2)}, u32[]{:S(2)}) collective-permute-start(f32[1,2,2,8,128]{4,3,2,1,0:T(8,128)S(1)} %get-tuple-element.593), channel_id=1, source_target_pairs={{0,30},{1,31},{2,0},{3,1},{4,2},{5,3},{6,4},{7,5},{8,6},{9,7},{10,... | collective-permute-start | bytes 49160 | tf_op jit(solution)/shard_map/ppermute | solution.py:33
  94.9 383.3 %while.19 = (s32[]{:T(128)}, f32[2,4,8,128]{3,2,1,0:T(8,128)}, f32[2,4,8,128]{3,2,1,0:T(8,128)}, f32[2,4,8,128]{3,2,1,0:T(8,128)S(1)}, pred[]{:T(512)}, /*index=...) while((s32[]{:T(128)}, f32[2,4,8,128]{3,2,1,0:T(8,128)}, ...), condition=%wide.region_1.2_spmd.clone.clone, body=%wide.region_0.1_spmd.sunk.clone.clone.sunk | while | flops 753666 | bytes 3277194 | solution.py:226
  97.0 4.2 collective-permute-done
  101.5 5.4 %collective-permute-start.1 = (f32[1,2,2,8,128]{4,3,2,1,0:T(8,128)S(1)}, f32[1,2,2,8,128]{4,3,2,1,0:T(8,128)S(1)}, u32[]{:S(2)}, u32[]{:S(2)}) collective-permute-start(f32[1,2,2,8,128]{4,3,2,1,0:T(8,128)S(1)} %get-tuple-element.747), channel_id=1, source_target_pairs={{0,30},{1,31},{2,0},{3,1},{4,2},{5,3},{6,4},{7,5},{8,6},{9,7},{10,... | collective-permute-start | bytes 49160 | tf_op jit(solution)/shard_map/while/body/eval_jaxpr/ppermute | solution.py:33
  108.9 4.9 collective-permute-done.2
  125.3 4.2 collective-permute-done
  151.6 4.2 collective-permute-done
  202.7 4.2 collective-permute-done
  327.5 4.2 collective-permute-done
  353.8 4.2 collective-permute-done
  430.6 4.2 collective-permute-done
  455.4 4.2 collective-permute-done
  481.1 4.8 collective-permute-done.21
  489.9 6.2 %collective-permute-start.23 = (f32[4,2,2,16,128]{4,3,2,1,0:T(8,128)S(1)}, f32[4,2,2,16,128]{4,3,2,1,0:T(8,128)S(1)}, u32[]{:S(2)}, u32[]{:S(2)}) collective-permute-start(f32[4,2,2,16,128]{4,3,2,1,0:T(8,128)S(1)} %get-tuple-element.455), channel_id=1, source_target_pairs={{1,0},{2,1},{3,2},{4,3},{5,4},{6,5},{7,6},{8,7},{9,8},{10,9},{11,1... | collective-permute-start | bytes 393224 | tf_op jit(solution)/shard_map/ppermute | solution.py:25
  500.4 4.8 collective-permute-start.24
  505.2 5.1 collective-permute-start.25
  (812 shorter events, 388.9 us)
Async XLA Ops:
  1.7 37.2 %collective-permute-start.5 = (f32[4,2,2,16,128]{4,3,2,1,0:T(8,128)}, f32[4,2,2,16,128]{4,3,2,1,0:T(8,128)}, u32[]{:S(2)}, u32[]{:S(2)}) collective-permute-start(f32[4,2,2,16,128]{4,3,2,1,0:T(8,128)} %get-tuple-element.474), channel_id=1, source_target_pairs={{0,1},{1,2},{2,3},{3,4},{4,5},{5,6},{6,7},{7,8},{8,9},{9,10},{10,1... | collective-permute-start | bytes 393224 | tf_op jit(solution)/shard_map/ppermute | solution.py:22
  6.8 32.1 %collective-permute-start.6 = (f32[4,2,2,16,128]{4,3,2,1,0:T(8,128)}, f32[4,2,2,16,128]{4,3,2,1,0:T(8,128)}, u32[]{:S(2)}, u32[]{:S(2)}) collective-permute-start(f32[4,2,2,16,128]{4,3,2,1,0:T(8,128)} %get-tuple-element.475), channel_id=1, source_target_pairs={{1,0},{2,1},{3,2},{4,3},{5,4},{6,5},{7,6},{8,7},{9,8},{10,9},{11,1... | collective-permute-start | bytes 393224 | tf_op jit(solution)/shard_map/ppermute | solution.py:25
  18.4 19.6 %collective-permute-start.18 = (f32[2,2,8,128]{3,2,1,0:T(8,128)}, f32[2,2,8,128]{3,2,1,0:T(8,128)}, u32[]{:S(2)}, u32[]{:S(2)}) collective-permute-start(f32[2,2,8,128]{3,2,1,0:T(8,128)} %pad_maximum_fusion.28), channel_id=1, source_target_pairs={{0,1},{1,0},{2,3},{3,2},{4,5},{5,4},{6,7},{7,6},{8,9},{9,8},{10,11... | collective-permute-start | bytes 49160 | tf_op jit(solution)/shard_map/ppermute | solution.py:37
  20.4 9.3 %collective-permute-start.9 = (f32[2,2,8,128]{3,2,1,0:T(8,128)S(1)}, f32[2,2,8,128]{3,2,1,0:T(8,128)}, u32[]{:S(2)}, u32[]{:S(2)}) collective-permute-start(f32[2,2,8,128]{3,2,1,0:T(8,128)S(1)} %bitcast.546), channel_id=1, source_target_pairs={{0,1},{1,0},{2,3},{3,2},{4,5},{5,4},{6,7},{7,6},{8,9},{9,8},{10,11... | collective-permute-start | bytes 49160 | tf_op jit(solution)/shard_map/ppermute | solution.py:37
  30.9 52.4 %collective-permute-start.10 = (f32[1,2,2,8,128]{4,3,2,1,0:T(8,128)S(1)}, f32[1,2,2,8,128]{4,3,2,1,0:T(8,128)S(1)}, u32[]{:S(2)}, u32[]{:S(2)}) collective-permute-start(f32[1,2,2,8,128]{4,3,2,1,0:T(8,128)S(1)} %get-tuple-element.620), channel_id=1, source_target_pairs={{0,2},{1,3},{2,4},{3,5},{4,6},{5,7},{6,8},{7,9},{8,10},{9,11},{10,... | collective-permute-start | bytes 49160 | tf_op jit(solution)/shard_map/ppermute | solution.py:33
  32.9 50.5 %collective-permute-start.11 = (f32[1,2,2,8,128]{4,3,2,1,0:T(8,128)S(1)}, f32[1,2,2,8,128]{4,3,2,1,0:T(8,128)S(1)}, u32[]{:S(2)}, u32[]{:S(2)}) collective-permute-start(f32[1,2,2,8,128]{4,3,2,1,0:T(8,128)S(1)} %get-tuple-element.621), channel_id=1, source_target_pairs={{0,30},{1,31},{2,0},{3,1},{4,2},{5,3},{6,4},{7,5},{8,6},{9,7},{10,... | collective-permute-start | bytes 49160 | tf_op jit(solution)/shard_map/ppermute | solution.py:33
  42.9 9.5 %collective-permute-start.7 = (f32[1,2,2,16,128]{4,3,2,1,0:T(8,128)S(1)}, f32[1,2,2,16,128]{4,3,2,1,0:T(8,128)S(1)}, u32[]{:S(2)}, u32[]{:S(2)}) collective-permute-start(f32[1,2,2,16,128]{4,3,2,1,0:T(8,128)S(1)} %get-tuple-element.557), channel_id=1, source_target_pairs={{0,1},{1,2},{2,3},{3,4},{4,5},{5,6},{6,7},{7,8},{8,9},{9,10},{10,1... | collective-permute-start | bytes 98312 | tf_op jit(solution)/shard_map/ppermute | solution.py:22
  46.2 7.7 %collective-permute-start.8 = (f32[1,2,2,16,128]{4,3,2,1,0:T(8,128)S(1)}, f32[1,2,2,16,128]{4,3,2,1,0:T(8,128)S(1)}, u32[]{:S(2)}, u32[]{:S(2)}) collective-permute-start(f32[1,2,2,16,128]{4,3,2,1,0:T(8,128)S(1)} %get-tuple-element.558), channel_id=1, source_target_pairs={{1,0},{2,1},{3,2},{4,3},{5,4},{6,5},{7,6},{8,7},{9,8},{10,9},{11,1... | collective-permute-start | bytes 98312 | tf_op jit(solution)/shard_map/ppermute | solution.py:25
  54.7 12.6 %collective-permute-start.12 = (f32[1,2,2,16,128]{4,3,2,1,0:T(8,128)S(1)}, f32[1,2,2,16,128]{4,3,2,1,0:T(8,128)S(1)}, u32[]{:S(2)}, u32[]{:S(2)}) collective-permute-start(f32[1,2,2,16,128]{4,3,2,1,0:T(8,128)S(1)} %get-tuple-element.555), channel_id=1, source_target_pairs={{0,1},{1,2},{2,3},{3,4},{4,5},{5,6},{6,7},{7,8},{8,9},{9,10},{10,1... | collective-permute-start | bytes 98312 | tf_op jit(solution)/shard_map/ppermute | solution.py:22
  57.4 9.8 %collective-permute-start.13 = (f32[1,2,2,16,128]{4,3,2,1,0:T(8,128)S(1)}, f32[1,2,2,16,128]{4,3,2,1,0:T(8,128)S(1)}, u32[]{:S(2)}, u32[]{:S(2)}) collective-permute-start(f32[1,2,2,16,128]{4,3,2,1,0:T(8,128)S(1)} %get-tuple-element.556), channel_id=1, source_target_pairs={{1,0},{2,1},{3,2},{4,3},{5,4},{6,5},{7,6},{8,7},{9,8},{10,9},{11,1... | collective-permute-start | bytes 98312 | tf_op jit(solution)/shard_map/ppermute | solution.py:25
  65.3 8.5 %collective-permute-start.15 = (f32[3,2,2,8,128]{4,3,2,1,0:T(8,128)S(1)}, f32[3,2,2,8,128]{4,3,2,1,0:T(8,128)S(1)}, u32[]{:S(2)}, u32[]{:S(2)}) collective-permute-start(f32[3,2,2,8,128]{4,3,2,1,0:T(8,128)S(1)} %fusion.197), channel_id=1, source_target_pairs={{0,1},{1,0},{2,3},{3,2},{4,5},{5,4},{6,7},{7,6},{8,9},{9,8},{10,11... | collective-permute-start | bytes 147464 | tf_op jit(solution)/shard_map/ppermute | solution.py:37
  68.4 13.2 %collective-permute-start.14 = (f32[2,2,2,8,128]{4,3,2,1,0:T(8,128)S(1)}, f32[2,2,2,8,128]{4,3,2,1,0:T(8,128)S(1)}, u32[]{:S(2)}, u32[]{:S(2)}) collective-permute-start(f32[2,2,2,8,128]{4,3,2,1,0:T(8,128)S(1)} %pad_maximum_fusion.25), channel_id=1, source_target_pairs={{0,1},{1,0},{2,3},{3,2},{4,5},{5,4},{6,7},{7,6},{8,9},{9,8},{10,11... | collective-permute-start | bytes 98312 | tf_op jit(solution)/shard_map/ppermute | solution.py:37
  74.3 7.3 %collective-permute-start.16 = (f32[2,2,2,8,128]{4,3,2,1,0:T(8,128)S(1)}, f32[2,2,2,8,128]{4,3,2,1,0:T(8,128)S(1)}, u32[]{:S(2)}, u32[]{:S(2)}) collective-permute-start(f32[2,2,2,8,128]{4,3,2,1,0:T(8,128)S(1)} %get-tuple-element.511), channel_id=1, source_target_pairs={{0,2},{1,3},{2,4},{3,5},{4,6},{5,7},{6,8},{7,9},{8,10},{9,11},{10,... | collective-permute-start | bytes 98312 | tf_op jit(solution)/shard_map/ppermute | solution.py:33
  76.3 6.8 %collective-permute-start.17 = (f32[2,2,2,8,128]{4,3,2,1,0:T(8,128)S(1)}, f32[2,2,2,8,128]{4,3,2,1,0:T(8,128)S(1)}, u32[]{:S(2)}, u32[]{:S(2)}) collective-permute-start(f32[2,2,2,8,128]{4,3,2,1,0:T(8,128)S(1)} %get-tuple-element.512), channel_id=1, source_target_pairs={{0,30},{1,31},{2,0},{3,1},{4,2},{5,3},{6,4},{7,5},{8,6},{9,7},{10,... | collective-permute-start | bytes 98312 | tf_op jit(solution)/shard_map/ppermute | solution.py:33
  85.3 8.0 %collective-permute-start.19 = (f32[1,2,2,8,128]{4,3,2,1,0:T(8,128)S(1)}, f32[1,2,2,8,128]{4,3,2,1,0:T(8,128)S(1)}, u32[]{:S(2)}, u32[]{:S(2)}) collective-permute-start(f32[1,2,2,8,128]{4,3,2,1,0:T(8,128)S(1)} %get-tuple-element.592), channel_id=1, source_target_pairs={{0,2},{1,3},{2,4},{3,5},{4,6},{5,7},{6,8},{7,9},{8,10},{9,11},{10,... | collective-permute-start | bytes 49160 | tf_op jit(solution)/shard_map/ppermute | solution.py:33
  87.2 6.9 %collective-permute-start.20 = (f32[1,2,2,8,128]{4,3,2,1,0:T(8,128)S(1)}, f32[1,2,2,8,128]{4,3,2,1,0:T(8,128)S(1)}, u32[]{:S(2)}, u32[]{:S(2)}) collective-permute-start(f32[1,2,2,8,128]{4,3,2,1,0:T(8,128)S(1)} %get-tuple-element.593), channel_id=1, source_target_pairs={{0,30},{1,31},{2,0},{3,1},{4,2},{5,3},{6,4},{7,5},{8,6},{9,7},{10,... | collective-permute-start | bytes 49160 | tf_op jit(solution)/shard_map/ppermute | solution.py:33
  101.5 7.4 %collective-permute-start.1 = (f32[1,2,2,8,128]{4,3,2,1,0:T(8,128)S(1)}, f32[1,2,2,8,128]{4,3,2,1,0:T(8,128)S(1)}, u32[]{:S(2)}, u32[]{:S(2)}) collective-permute-start(f32[1,2,2,8,128]{4,3,2,1,0:T(8,128)S(1)} %get-tuple-element.747), channel_id=1, source_target_pairs={{0,30},{1,31},{2,0},{3,1},{4,2},{5,3},{6,4},{7,5},{8,6},{9,7},{10,... | collective-permute-start | bytes 49160 | tf_op jit(solution)/shard_map/while/body/eval_jaxpr/ppermute | solution.py:33
  107.0 6.8 %collective-permute-start.2 = (f32[1,2,2,8,128]{4,3,2,1,0:T(8,128)S(1)}, f32[1,2,2,8,128]{4,3,2,1,0:T(8,128)S(1)}, u32[]{:S(2)}, u32[]{:S(2)}) collective-permute-start(f32[1,2,2,8,128]{4,3,2,1,0:T(8,128)S(1)} %get-tuple-element.748), channel_id=1, source_target_pairs={{0,2},{1,3},{2,4},{3,5},{4,6},{5,7},{6,8},{7,9},{8,10},{9,11},{10,... | collective-permute-start | bytes 49160 | tf_op jit(solution)/shard_map/while/body/eval_jaxpr/ppermute | solution.py:33
  116.3 6.8 %collective-permute-start.4 = (f32[1,2,2,8,128]{4,3,2,1,0:T(8,128)S(1)}, f32[1,2,2,8,128]{4,3,2,1,0:T(8,128)S(1)}, u32[]{:S(2)}, u32[]{:S(2)}) collective-permute-start(f32[1,2,2,8,128]{4,3,2,1,0:T(8,128)S(1)} %get-tuple-element.768), channel_id=1, source_target_pairs={{0,2},{1,3},{2,4},{3,5},{4,6},{5,7},{6,8},{7,9},{8,10},{9,11},{10,... | collective-permute-start | bytes 49160 | tf_op jit(solution)/shard_map/while/body/eval_jaxpr/ppermute | solution.py:33
  131.8 6.8 %collective-permute-start.2 = (f32[1,2,2,8,128]{4,3,2,1,0:T(8,128)S(1)}, f32[1,2,2,8,128]{4,3,2,1,0:T(8,128)S(1)}, u32[]{:S(2)}, u32[]{:S(2)}) collective-permute-start(f32[1,2,2,8,128]{4,3,2,1,0:T(8,128)S(1)} %get-tuple-element.748), channel_id=1, source_target_pairs={{0,2},{1,3},{2,4},{3,5},{4,6},{5,7},{6,8},{7,9},{8,10},{9,11},{10,... | collective-permute-start | bytes 49160 | tf_op jit(solution)/shard_map/while/body/eval_jaxpr/ppermute | solution.py:33
  486.6 10.5 %collective-permute-start.22 = (f32[4,2,2,16,128]{4,3,2,1,0:T(8,128)S(1)}, f32[4,2,2,16,128]{4,3,2,1,0:T(8,128)S(1)}, u32[]{:S(2)}, u32[]{:S(2)}) collective-permute-start(f32[4,2,2,16,128]{4,3,2,1,0:T(8,128)S(1)} %get-tuple-element.454), channel_id=1, source_target_pairs={{0,1},{1,2},{2,3},{3,4},{4,5},{5,6},{6,7},{7,8},{8,9},{9,10},{10,1... | collective-permute-start | bytes 393224 | tf_op jit(solution)/shard_map/ppermute | solution.py:22
  489.9 8.7 %collective-permute-start.23 = (f32[4,2,2,16,128]{4,3,2,1,0:T(8,128)S(1)}, f32[4,2,2,16,128]{4,3,2,1,0:T(8,128)S(1)}, u32[]{:S(2)}, u32[]{:S(2)}) collective-permute-start(f32[4,2,2,16,128]{4,3,2,1,0:T(8,128)S(1)} %get-tuple-element.455), channel_id=1, source_target_pairs={{1,0},{2,1},{3,2},{4,3},{5,4},{6,5},{7,6},{8,7},{9,8},{10,9},{11,1... | collective-permute-start | bytes 393224 | tf_op jit(solution)/shard_map/ppermute | solution.py:25
  500.4 9.9 %collective-permute-start.24 = (f32[1,2,2,16,128]{4,3,2,1,0:T(8,128)S(1)}, f32[1,2,2,16,128]{4,3,2,1,0:T(8,128)S(1)}, u32[]{:S(2)}, u32[]{:S(2)}) collective-permute-start(f32[1,2,2,16,128]{4,3,2,1,0:T(8,128)S(1)} %get-tuple-element.529), channel_id=1, source_target_pairs={{0,1},{1,2},{2,3},{3,4},{4,5},{5,6},{6,7},{7,8},{8,9},{9,10},{10,1... | collective-permute-start | bytes 98312 | tf_op jit(solution)/shard_map/ppermute | solution.py:22
  505.2 7.3 %collective-permute-start.25 = (f32[1,2,2,16,128]{4,3,2,1,0:T(8,128)S(1)}, f32[1,2,2,16,128]{4,3,2,1,0:T(8,128)S(1)}, u32[]{:S(2)}, u32[]{:S(2)}) collective-permute-start(f32[1,2,2,16,128]{4,3,2,1,0:T(8,128)S(1)} %get-tuple-element.530), channel_id=1, source_target_pairs={{1,0},{2,1},{3,2},{4,3},{5,4},{6,5},{7,6},{8,7},{9,8},{10,9},{11,1... | collective-permute-start | bytes 98312 | tf_op jit(solution)/shard_map/ppermute | solution.py:25
  (111 other events, 1084.7 us)
where the time goes:
time: 518 us; the launch traced here: 513 us
  starting transfers between devices  298 us (58%)
  waiting for transfers between devices  164 us (32%)
  other arithmetic  28.3 us (5%)
  local copies, waits for them, and re-layouts  18.6 us (4%)
    ppermute x66, starting transfers between devices, shifted(): return lax.ppermute(value, axis, pairs)  198 us
    ppermute x66, waiting for transfers between devices, shifted(): return lax.ppermute(value, axis, pairs)  90.1 us
    ppermute x16, waiting for transfers between devices, from_behind(): return lax.ppermute(array, axis, pairs)  67.9 us
    ppermute x5, starting transfers between devices, with_halo(): lax.ppermute(lax.slice_in_dim(block, 0, width, axis=dim), axis, backward)  35.3 us
    ppermute x16, starting transfers between devices, from_behind(): return lax.ppermute(array, axis, pairs)  30.8 us
    ppermute x5, starting transfers between devices, with_halo(): lax.ppermute(lax.slice_in_dim(block, block.shape[dim] - width, None, axis...  19.3 us
    ppermute x4, starting transfers between devices, partner_2(): lax.ppermute(array, axis, [(i, i ^ 1 << stride) for i in range(lax.axis_s...  14.7 us
  transfers between devices with their start and end apart: 96, of which 52 were waited for; matrix products, arithmetic and copies ran while one was open for 4% of the time, Pallas kernels for 0%

commit v1 on v0

v1 whole, which is shorter than its diff:
```python
import jax
import jax.numpy as jnp
from jax import lax
from jax.experimental import pallas as pl
from jax.experimental.pallas import tpu as pltpu
from jax.sharding import PartitionSpec as P

AX = ("tm", "slab")
F32 = jnp.float32
W1 = (5.0 / 12.0, 2.0 / 3.0, -1.0 / 12.0)
W2 = (-1.0 / 12.0, 2.0 / 3.0, 5.0 / 12.0)
R1 = (5.0 / 12.0, 2.0 / 3.0 - 1.0, -1.0 / 12.0)
R2 = (-1.0 / 12.0, 2.0 / 3.0, 5.0 / 12.0 - 1.0)
DIFF = (0.1, 0.05)
VM = pl.BlockSpec(memory_space=pltpu.VMEM)
SM = pl.BlockSpec(memory_space=pltpu.SMEM)


def flat(z, yh, chip, core):
    return (2 * chip + core) * 32 + (z % 16) * 2 + yh


def everyone():
    return [(z, yh, chip, core) for z in range(16) for yh in range(2)
            for chip in range(8) for core in range(2)]


def pair_groups():
    return [[flat(z, 0, c, k), flat(z, 1, c, k)] for z in range(16) for c in range(8) for k in range(2)]


def core_groups():
    return [[flat(z, h, c, 0), flat(z, h, c, 1)] for z in range(16) for h in range(2) for c in range(8)]


def z_pairs(step):
    return [(flat(z, h, c, k), flat(z + step, h, c, k)) for z, h, c, k in everyone()]


def split_pairs(step):
    return [(flat(z, h, c, k), flat(z + (step if k == 0 else -step), h, c, k))
            for z, h, c, k in everyone()]


def slice_pairs():
    return [(t * 32 + s, (t + 1) * 32 + s) for t in range(15) for s in range(32)]


def turn_groups(parity):
    groups = []
    for z, h, c, k in everyone():
        if c % 2 == parity:
            groups.append([flat(z, h, c, k), flat(z + (2 if k == 0 else -2), h, (c + 1) % 8, k)])
    return groups


def gather(x, groups):
    return lax.all_gather(x, AX, axis=0, axis_index_groups=groups, tiled=False)


def lane(x, n):
    return pltpu.roll(x, n % 128, x.ndim - 1)


def sub(x, n):
    return pltpu.roll(x, n % 8, x.ndim - 2)


def fine_lap(win, coef):
    n = win.shape[0] - 4
    mid = win[2:n + 2]
    near = win[1:n + 1] + win[3:n + 3]
    far = win[0:n] + win[4:n + 4]
    even = mid[:, 0]
    odd = mid[:, 1]
    even_up, even_dn = sub(even, 1), sub(even, -1)
    odd_up, odd_dn = sub(odd, 1), sub(odd, -1)
    nx = jnp.stack([odd + odd_up, even + even_dn], axis=1)
    fx = jnp.stack([even_up + even_dn, odd_up + odd_dn], axis=1)
    near = near + nx + (lane(mid, 1) + lane(mid, -1))
    far = far + fx + (lane(mid, 2) + lane(mid, -2))
    return (coef * 16.0 / 12.0) * near - (coef / 12.0) * far - (coef * 90.0 / 12.0) * mid


def coarse_lap(win, coef):
    n = win.shape[0] - 4
    mid = win[2:n + 2]
    near = win[1:n + 1] + win[3:n + 3] + (sub(mid, 1) + sub(mid, -1))
    far = win[0:n] + win[4:n + 4] + (sub(mid, 2) + sub(mid, -2))
    near_y = lane(mid, 1) + lane(mid, -1)
    far_y = lane(mid, 2) + lane(mid, -2)
    c = coef / 12.0
    return (4.0 * c) * near - (0.25 * c) * far + (16.0 * c) * near_y - c * far_y - (45.0 * c) * mid


def solve(bu, bv, g, ru, rv):
    u = (bu - g) * ru
    v = (bv + g) * rv
    g = u * v * v
    return (bu - g) * ru, (bv + g) * rv


def comb(w, xs):
    return w[0] * xs[0] + w[1] * xs[1] + w[2] * xs[2]


def pack_kernel(nv, st, fr, kr, out):
    for p in range(4):
        for par in range(2):
            rows = pl.ds(par, 8, stride=2)
            for j in range(3):
                for s in range(2):
                    out[p, 2 * j + s, par] = nv[0, j, s, p, rows, :]
            for s in range(2):
                out[p, 6 + s, par] = st[0, s, p, rows, :]
            out[p, 8, par] = fr[p, rows, :]
            out[p, 9, par] = kr[p, rows, :]


def first_combo(w, start):
    return start + (5.0 / 12.0 - 1.0) * w[0] + (2.0 / 3.0) * w[1] - (1.0 / 12.0) * w[2]


def sweep_kernel(pair, lo, hi, big, unit, aux, v1, v2, b2, xs, xp, cs):
    segs = ((lo, 2, 6), (pair, 8, 8), (hi, 16, 6))

    def raw(ref, i, f):
        if ref is pair:
            return ref[pl.ds(i, 2), f]
        return jnp.stack([ref[i * 10 + f], ref[i * 10 + 10 + f]])

    for s in range(2):
        v1[0, s] = lo[60 + s]
        v1[1, s] = lo[62 + s]
        v1[22, s] = hi[60 + s]
        v1[23, s] = hi[62 + s]

    for ref, base, count in segs:
        def load_v1(n, _, ref=ref, base=base):
            i = 2 * n
            for s in range(2):
                w = [raw(ref, i, 2 * j + s) for j in range(3)]
                start = raw(ref, i, 6 + s)
                v1[pl.ds(base + i, 2), s] = first_combo(w, start)
            return 0
        lax.fori_loop(0, count // 2, load_v1, 0)

    for ref, base, count in segs:
        def node_one(n, _, ref=ref, base=base):
            i = 2 * n
            p = base + i
            q = p - 2
            u = [raw(ref, i, 2 * j) for j in range(3)]
            v = [raw(ref, i, 2 * j + 1) for j in range(3)]
            su, sv = raw(ref, i, 6), raw(ref, i, 7)
            f = raw(ref, i, 8)
            fk = f + raw(ref, i, 9)
            ru = 1.0 / (1.0 + f)
            rv = 1.0 / (1.0 + fk)
            g = [u[j] * v[j] * v[j] for j in range(3)]
            gq = comb(R1, g)
            bu = su + f - f * comb(R1, u) - gq + fine_lap(v1[pl.ds(p - 2, 6), 0], DIFF[0])
            bv = sv + gq - fk * comb(R1, v) + fine_lap(v1[pl.ds(p - 2, 6), 1], DIFF[1])
            nu, nv = solve(bu, bv, g[1], ru, rv)
            at = pl.ds(q, 2)
            big[at, 0] = su
            big[at, 1] = sv
            big[at, 2] = nu
            big[at, 3] = nv
            big[at, 6] = f
            big[at, 7] = fk
            big[at, 8] = ru
            big[at, 9] = rv
            qu, qv = comb(R2, u), comb(R2, v)
            gq = comb(R2, g)
            v2[at, 0] = nu + qu + (u[2] - u[1])
            v2[at, 1] = nv + qv + (v[2] - v[1])
            b2[at, 0] = nu + f - f * qu - gq
            b2[at, 1] = nv + gq - fk * qv
            b2[at, 2] = g[2]
            return 0
        lax.fori_loop(0, count // 2, node_one, 0)

    def node_two(n, _):
        q = 2 + 2 * n
        at = pl.ds(q, 2)
        bu = b2[at, 0] + fine_lap(v2[pl.ds(q - 2, 6), 0], DIFF[0])
        bv = b2[at, 1] + fine_lap(v2[pl.ds(q - 2, 6), 1], DIFF[1])
        nu, nv = solve(bu, bv, b2[at, 2], big[at, 8], big[at, 9])
        big[at, 4] = nu
        big[at, 5] = nv
        return 0
    lax.fori_loop(0, 8, node_two, 0)

    def integrals(n, _):
        q = 4 + 2 * n
        at = pl.ds(q, 2)
        u = [big[at, 2 * j] for j in range(3)]
        v = [big[at, 2 * j + 1] for j in range(3)]
        f, fk = big[at, 6], big[at, 7]
        g = [u[j] * v[j] * v[j] for j in range(3)]
        to = pl.ds(2 * n, 2)
        for m, w in enumerate((W1, W2)):
            xu, xv, gx = comb(w, u), comb(w, v), comb(w, g)
            xs[to, 2 * m] = xu
            xs[to, 2 * m + 1] = xv
            xp[to, 2 * m] = f - f * xu - gx
            xp[to, 2 * m + 1] = gx - fk * xv
        return 0
    lax.fori_loop(0, 6, integrals, 0)

    def restrict(x):
        return 0.25 * (x[0, 0] + x[0, 1] + x[1, 0] + x[1, 1])

    def coarsen(n, _):
        at = pl.ds(2 * n, 2)
        for f in range(6):
            cs[n, f] = restrict(big[at, f])
        f = restrict(big[at, 6])
        k = restrict(big[at, 7])
        cs[n, 6] = f
        cs[n, 7] = k
        aux[n, 0] = cs[n, 0]
        aux[n, 1] = cs[n, 1]
        aux[n, 2] = 1.0 / (1.0 + f)
        aux[n, 3] = 1.0 / (1.0 + k)
        return 0
    lax.fori_loop(0, 10, coarsen, 0)

    def make_unit(n, _):
        for m in range(2):
            cu, cv = cs[3 + n, 2 * m + 2], cs[3 + n, 2 * m + 3]
            f, fk = cs[3 + n, 6], cs[3 + n, 7]
            g = cu * cv * cv
            for s in range(2):
                fl = fine_lap(xs[pl.ds(2 * n, 6), 2 * m + s], DIFF[s]) + xp[pl.ds(2 * n + 2, 2), 2 * m + s]
                val = restrict(fl) - coarse_lap(cs[pl.ds(n + 1, 5), 2 * m + s], DIFF[s])[0]
                if s == 0:
                    val = val + f * cu + g
                else:
                    val = val - g + fk * cv
                unit[n, 3 * m + s] = val
            unit[n, 3 * m + 2] = g
        return 0
    lax.fori_loop(0, 4, make_unit, 0)


def coarse_node(src, src_off, prm, prm_off, m, rates, rate_off, dst, dst_off, count):
    def step(n, _):
        i = 4 * n
        at = pl.ds(prm_off + i, 4)
        ra = pl.ds(rate_off + i, 4)
        wu = src[pl.ds(src_off + i, 8), 0]
        wv = src[pl.ds(src_off + i, 8), 1]
        bu = wu[2:6] + coarse_lap(wu, DIFF[0]) + prm[at, 3 * m]
        bv = wv[2:6] + coarse_lap(wv, DIFF[1]) + prm[at, 3 * m + 1]
        nu, nv = solve(bu, bv, prm[at, 3 * m + 2], rates[ra, 2], rates[ra, 3])
        dst[pl.ds(dst_off + i, 4), 0] = nu
        dst[pl.ds(dst_off + i, 4), 1] = nv
        return 0
    lax.fori_loop(0, count // 4, step, 0)


def two_slices(a, pa, pb, aux, n1, n2, n3, out):
    coarse_node(a, 0, pa, 0, 0, aux, 2, n1, 0, 28)
    coarse_node(n1, 0, pa, 2, 1, aux, 4, n2, 0, 24)
    coarse_node(n2, 0, pb, 0, 0, aux, 6, n3, 0, 20)
    coarse_node(n3, 0, pb, 2, 1, aux, 8, out, 0, 16)


def chain_kernel(a, pa, pb, aux, out, n1, n2, n3):
    two_slices(a, pa, pb, aux, n1, n2, n3, out)


def last_kernel(sc, a, pa, pb, aux, big, prev, res, n1, n2, n3, n4, gs, v1, tp):
    two_slices(a, pa, pb, aux, n1, n2, n3, n4)
    core = sc[0]
    yh = sc[1]

    @pl.when(core == 0)
    def _():
        for s in range(2):
            gs[:, s] = a[12:20, s]
            gs[:, 2 + s] = n1[10:18, s]
            gs[:, 4 + s] = n2[8:16, s]

    @pl.when(core != 0)
    def _():
        for s in range(2):
            gs[:, s] = n2[8:16, s]
            gs[:, 2 + s] = n3[6:14, s]
            gs[:, 4 + s] = n4[4:12, s]

    def restrict(x):
        return 0.25 * (x[0, 0] + x[0, 1] + x[1, 0] + x[1, 1])

    def update(i, _):
        row = 2 * yh + i
        at = pl.ds(2 + 4 * yh + 2 * i, 2)
        to = pl.ds(2 * i, 2)
        new = []
        for f in range(6):
            x = big[at, f]
            new.append(x + (gs[row, f] - restrict(x))[None, None])
        u, v = new[0::2], new[1::2]
        bu = prev[to, 0]
        bv = prev[to, 1]
        bu = bu + (gs[row, 0] - restrict(bu))[None, None]
        bv = bv + (gs[row, 1] - restrict(bv))[None, None]
        f, fk = big[at, 6], big[at, 7]
        g = [u[j] * v[j] * v[j] for j in range(3)]
        qu, qv, gq = comb(R1, u), comb(R1, v), comb(R1, g)
        v1[to, 0] = bu + qu + (u[1] - u[0])
        v1[to, 1] = bv + qv + (v[1] - v[0])
        tp[to, 0] = bu + f - f * qu - gq
        tp[to, 1] = bv + gq - fk * qv
        tp[to, 2] = g[1]
        qu, qv, gq = comb(R2, u), comb(R2, v), comb(R2, g)
        tp[to, 3] = qu + (u[2] - u[1])
        tp[to, 4] = qv + (v[2] - v[1])
        tp[to, 5] = f - f * qu - gq
        tp[to, 6] = gq - fk * qv
        tp[to, 7] = g[2]
        tp[to, 8] = bu
        tp[to, 9] = bv
        return 0
    lax.fori_loop(0, 6, update, 0)

    def put(node, s, plane, x):
        res[0, node, s, plane, pl.ds(0, 8, stride=2), :] = x[0]
        res[0, node, s, plane, pl.ds(1, 8, stride=2), :] = x[1]

    def node_one(n, _):
        i = 2 + 2 * n
        at = pl.ds(i, 2)
        br = pl.ds(2 + 4 * yh + i, 2)
        bu = tp[at, 0] + fine_lap(v1[pl.ds(i - 2, 6), 0], DIFF[0])
        bv = tp[at, 1] + fine_lap(v1[pl.ds(i - 2, 6), 1], DIFF[1])
        nu, nv = solve(bu, bv, tp[at, 2], big[br, 8], big[br, 9])
        tp[at, 3] = tp[at, 3] + nu
        tp[at, 4] = tp[at, 4] + nv
        tp[at, 5] = tp[at, 5] + nu
        tp[at, 6] = tp[at, 6] + nv
        tp[at, 10] = nu
        tp[at, 11] = nv
        return 0
    lax.fori_loop(0, 4, node_one, 0)

    for n in range(2):
        i = 4 + 2 * n
        at = pl.ds(i, 2)
        br = pl.ds(2 + 4 * yh + i, 2)
        bu = tp[at, 5] + fine_lap(tp[pl.ds(i - 2, 6), 3], DIFF[0])
        bv = tp[at, 6] + fine_lap(tp[pl.ds(i - 2, 6), 4], DIFF[1])
        nu, nv = solve(bu, bv, tp[at, 7], big[br, 8], big[br, 9])
        for d in range(2):
            p = 2 * n + d
            put(2, 0, p, nu[d])
            put(2, 1, p, nv[d])
            for s in range(2):
                put(0, s, p, tp[i + d, 8 + s])
                put(1, s, p, tp[i + d, 10 + s])


def vmem(*shape):
    return pltpu.VMEM(shape, F32)


def shape(*dims):
    return jax.ShapeDtypeStruct(dims, F32)


def body(node_values, start_state, feed_rate, kill_rate):
    t = lax.axis_index("tm")
    core = t % 2
    chip = t // 2
    yh = lax.axis_index("slab") % 2
    left = core == 0
    own = pl.pallas_call(
        pack_kernel, out_shape=shape(4, 10, 2, 8, 128), in_specs=[VM] * 4, out_specs=VM,
        name="pack",
    )(node_values, start_state, feed_rate, kill_rate)
    pair = gather(own, pair_groups()).reshape(8, 10, 2, 8, 128)

    def edge(planes, far):
        w = [far[:, 2 * j:2 * j + 2] for j in range(3)]
        v = first_combo(w, far[:, 6:8])
        return jnp.concatenate([planes.reshape(60, 2, 8, 128), v.reshape(4, 2, 8, 128)])

    lo = lax.ppermute(edge(pair[2:8], pair[0:2]), AX, z_pairs(1))
    hi = lax.ppermute(edge(pair[0:6], pair[6:8]), AX, z_pairs(-1))
    big, unit, aux = pl.pallas_call(
        sweep_kernel,
        out_shape=(shape(20, 10, 2, 8, 128), shape(4, 6, 8, 128), shape(10, 4, 8, 128)),
        in_specs=[VM] * 3, out_specs=(VM, VM, VM),
        scratch_shapes=[vmem(24, 2, 2, 8, 128), vmem(20, 2, 2, 8, 128), vmem(20, 3, 2, 8, 128),
                        vmem(12, 4, 2, 8, 128), vmem(12, 4, 2, 8, 128), vmem(10, 8, 8, 128)],
        name="sweep",
    )(pair, lo, hi)

    mine = lax.dynamic_slice_in_dim(big, 2 + 4 * yh, 12, 0)
    prev = lax.ppermute(mine[:, 4:6], AX, slice_pairs())
    prev = jnp.where(t == 0, mine[:, 0:2], prev)

    both = gather(jnp.concatenate([unit.reshape(24, 8, 128), aux.reshape(40, 8, 128)]), core_groups())
    units = both[:, :24].reshape(2, 4, 6, 8, 128)
    aux = both[0, 24:].reshape(10, 4, 8, 128)

    def send(parts, step):
        rows = [x.reshape(-1, 8, 128) for x in parts]
        return lax.ppermute(jnp.concatenate(rows), AX, split_pairs(step))

    got1 = send([units, jnp.where(left, aux[0:4], aux[6:10])], 1)
    aux1 = got1[48:].reshape(4, 4, 8, 128)
    got2 = send([units, got1[0:24],
                 jnp.where(left, jnp.concatenate([aux1[1:4], aux[0:4]]),
                           jnp.concatenate([aux[6:10], aux1[0:3]]))], 2)
    sides = gather(jnp.concatenate([got1, got2]), core_groups())

    def pick(side, start, planes, fields):
        return sides[side, start:start + planes * fields].reshape(planes, fields, 8, 128)

    pa = jnp.concatenate([pick(0, 64 + 48, 4, 6), pick(0, 64, 4, 6), pick(0, 0, 4, 6), units[0],
                          pick(1, 0, 4, 6), pick(1, 64, 4, 6), pick(1, 64 + 48, 4, 6)])
    pb = jnp.concatenate([pick(0, 64 + 24, 4, 6), pick(0, 24, 4, 6), units[1],
                          pick(1, 24, 4, 6), pick(1, 64 + 24, 4, 6)])
    aux = jnp.concatenate([pick(0, 64 + 72, 7, 4), pick(0, 48, 4, 4), aux,
                           pick(1, 48, 4, 4), pick(1, 64 + 72, 7, 4)])
    state = aux[:, 0:2]

    scratch = [vmem(28, 2, 8, 128), vmem(24, 2, 8, 128), vmem(20, 2, 8, 128)]
    for turn in range(7):
        out = pl.pallas_call(
            chain_kernel, out_shape=shape(16, 2, 8, 128), in_specs=[VM] * 4, out_specs=VM,
            scratch_shapes=scratch, name="chain",
        )(state, pa, pb, aux)
        moved = gather(out, turn_groups(turn % 2))[0]
        moved = gather(moved, core_groups()).reshape(32, 2, 8, 128)
        takes = jnp.logical_and(chip % 2 == (turn + 1) % 2, chip > 0)
        state = jnp.where(takes, moved, state)

    scalars = jnp.stack([core, yh]).astype(jnp.int32)
    return pl.pallas_call(
        last_kernel, out_shape=shape(1, 3, 2, 4, 16, 128), in_specs=[SM] + [VM] * 6, out_specs=VM,
        scratch_shapes=scratch + [vmem(16, 2, 8, 128), vmem(8, 6, 8, 128),
                                  vmem(12, 2, 2, 8, 128), vmem(12, 12, 2, 8, 128)],
        name="last",
    )(scalars, state, pa, pb, aux, big, prev)


def solution(mesh):
    return jax.shard_map(
        body,
        mesh=mesh,
        in_specs=(
            P("tm", None, None, "slab", None, None),
            P("tm", None, "slab", None, None),
            P("slab", None, None),
            P("slab", None, None),
        ),
        out_specs=P("tm", None, None, "slab", None, None),
        check_vma=False,
    )
```

time: 518 us -> 245 us (0.47)
  starting transfers between devices: 298 us -> 19.1 us
  waiting for transfers between devices: 164 us -> 45.5 us
  blocking collectives: 0 us -> 99.1 us
  Pallas kernels: 0 us -> 46.2 us
  other arithmetic: 28.3 us -> 9.53 us
  between operations: 1.22 us -> 13.8 us
  local copies, waits for them, and re-layouts: 18.6 us -> 7.8 us
    ppermute x96 -> x5, starting transfers between devices: 298 us -> 19.1 us  [the longest x1 9.5 us: body(): hi = lax.ppermute(edge(pair[0:6], pair[6:8]), AX, z_pairs(-1))]
    ppermute x96 -> x5, waiting for transfers between devices: 164 us -> 38.3 us  [the longest x2 22 us: send(): return lax.ppermute(jnp.concatenate(rows), AX, split_pairs(step))]
    all_gather x0 -> x16, blocking collectives: none -> 99.1 us  [gather(): return lax.all_gather(x, AX, axis=0, axis_index_groups=groups, tiled=False)]
    pallas_call x0 -> x10, Pallas kernels: none -> 46.2 us  [the longest x7 32.7 us: body(): pl.pallas_call(chain_kernel, out_shape=shape(16, 2, 8, 128), in_specs=[VM...]
    another operation x47 -> x1, other arithmetic: 11.2 us -> 0.58 us  [body(): scalars = jnp.stack([core, yh]).astype(jnp.int32)]
    all_gather x0 -> x1, waiting for transfers between devices: none -> 7.25 us  [gather(): return lax.all_gather(x, AX, axis=0, axis_index_groups=groups, tiled=False)]
  transfers between devices with their start and end apart: 96 -> 6, of which waited for: 52 -> 6; matrix products, arithmetic and copies ran while one was open for 4% -> 1% of each run, Pallas kernels for 0% -> 0%
where the time goes in v1:
time: 245 us; the launch traced here: 241 us
  blocking collectives  99.1 us (40%)
  Pallas kernels  46.2 us (19%)
  waiting for transfers between devices  45.5 us (19%)
  starting transfers between devices  19.1 us (8%)
  between operations  13.8 us (6%)
  other arithmetic  9.53 us (4%)
  local copies, waits for them, and re-layouts  7.8 us (3%)
    all_gather x16, blocking collectives, gather(): return lax.all_gather(x, AX, axis=0, axis_index_groups=groups, tiled=False)  99.1 us
    pallas_call x7, Pallas kernels, body(): pl.pallas_call(chain_kernel, out_shape=shape(16, 2, 8, 128), in_specs=[VM...  32.7 us
    ppermute x2, waiting for transfers between devices, send(): return lax.ppermute(jnp.concatenate(rows), AX, split_pairs(step))  22 us
    ppermute x1, starting transfers between devices, body(): hi = lax.ppermute(edge(pair[0:6], pair[6:8]), AX, z_pairs(-1))  9.5 us
    ppermute x1, waiting for transfers between devices, body(): lo = lax.ppermute(edge(pair[2:8], pair[0:2]), AX, z_pairs(1))  9.06 us
    all_gather x1, waiting for transfers between devices, gather(): return lax.all_gather(x, AX, axis=0, axis_index_groups=groups, tiled=False)  7.25 us
    pallas_call x1, Pallas kernels, body(): pl.pallas_call(last_kernel, out_shape=shape(1, 3, 2, 4, 16, 128), in_spec...  6.13 us
    ppermute x1, waiting for transfers between devices, body(): prev = lax.ppermute(mine[:, 4:6], AX, slice_pairs())  5.94 us
  transfers between devices with their start and end apart: 6, of which 6 were waited for; matrix products, arithmetic and copies ran while one was open for 1% of the time, Pallas kernels for 0%

profile of v1, /device:TPU:6, one launch (start us, length us, event | category | flops | bytes accessed | tf_op | source)
XLA Modules:
  0.0 241.1 jit_solution(3781477566867964803)
XLA Ops:
  8.3 11.8 %all-gather.pair = f32[8,10,2,8,128]{4,3,2,1,0:T(8,128)S(1)} all-gather(f32[4,10,2,8,128]{4,3,2,1,0:T(8,128)} %pack.1), channel_id=2, replica_groups={{0,1},{32,33},{64,65},{96,97},{128,129},{160,161},{192,193},{224,225},{..., dimensions={0}, use_global_device_ids=true | all-gather | bytes 983040 | tf_op jit(solution)/shard_map/all_gather | solution.py:58
  20.9 3.8 %collective-permute-start = (f32[64,2,8,128]{3,2,1,0:T(8,128)S(1)}, f32[64,2,8,128]{3,2,1,0:T(8,128)S(1)}, u32[]{:S(2)}, u32[]{:S(2)}) collective-permute-start(f32[64,2,8,128]{3,2,1,0:T(8,128)S(1)} %pad_maximum_fusion.1), channel_id=1, source_target_pairs={{0,2},{32,34},{64,66},{96,98},{128,130},{160,162},{192,194},{224,2... | collective-permute-start | bytes 1572872 | tf_op jit(solution)/shard_map/ppermute | solution.py:390
  24.8 9.5 %collective-permute-start.1 = (f32[64,2,8,128]{3,2,1,0:T(8,128)S(1)}, f32[64,2,8,128]{3,2,1,0:T(8,128)S(1)}, u32[]{:S(2)}, u32[]{:S(2)}) collective-permute-start(f32[64,2,8,128]{3,2,1,0:T(8,128)S(1)} %pad_maximum_fusion.2), channel_id=1, source_target_pairs={{0,30},{32,62},{64,94},{96,126},{128,158},{160,190},{192,222},{224... | collective-permute-start | bytes 1572872 | tf_op jit(solution)/shard_map/ppermute | solution.py:391
  34.3 9.1 %collective-permute-done.lo = f32[64,2,8,128]{3,2,1,0:T(8,128)S(1)} collective-permute-done((f32[64,2,8,128]{3,2,1,0:T(8,128)S(1)}, f32[64,2,8,128]{3,2,1,0:T(8,128)S(1)}, u32[]{:S(2)}, u32[]{:S(2)}) %collective-permute-start) | collective-permute-done | bytes 524320 | tf_op jit(solution)/shard_map/ppermute | solution.py:390
  45.4 5.7 %sweep.1 = (f32[20,10,2,8,128]{4,3,2,1,0:T(8,128)}, f32[4,6,8,128]{3,2,1,0:T(8,128)}, f32[10,4,8,128]{3,2,1,0:T(8,128)}) custom-call(f32[8,10,2,8,128]{4,3,2,1,0:T(8,128)} %copy-done.4, f32[64,2,8,128]{3,2,1,0:T(8,128)} %copy-done.11, f32[64,2,8,128]{3,2,1,0:T(8,128)} %copy-done.12), custom_call_target="tpu_custom_call" | custom-call | tf_op jit(solution)/shard_map/sweep/pallas_call | solution.py:392
  56.3 8.0 %collective-permute-done.2 = f32[64,8,128]{2,1,0:T(8,128)S(1)} collective-permute-done((f32[64,8,128]{2,1,0:T(8,128)S(1)}, f32[64,8,128]{2,1,0:T(8,128)S(1)}, u32[]{:S(2)}, u32[]{:S(2)}) %collective-permute-start.2) | collective-permute-done | bytes 262176 | tf_op jit(solution)/shard_map/ppermute | solution.py:411
  66.3 14.0 %collective-permute-done.3 = f32[100,8,128]{2,1,0:T(8,128)S(1)} collective-permute-done((f32[100,8,128]{2,1,0:T(8,128)S(1)}, f32[100,8,128]{2,1,0:T(8,128)S(1)}, u32[]{:S(2)}, u32[]{:S(2)}) %collective-permute-start.3) | collective-permute-done | bytes 409632 | tf_op jit(solution)/shard_map/ppermute | solution.py:411
  84.9 5.9 %collective-permute-done.4 = f32[12,2,2,8,128]{4,3,2,1,0:T(8,128)S(1)} collective-permute-done((f32[12,2,2,8,128]{4,3,2,1,0:T(8,128)S(1)}, f32[12,2,2,8,128]{4,3,2,1,0:T(8,128)S(1)}, u32[]{:S(2)}, u32[]{:S(2)}) %collective-permute-start.4) | collective-permute-done | bytes 196640 | tf_op jit(solution)/shard_map/ppermute | solution.py:402
  92.4 7.3 %all-gather.19.cloned.1.call-done = f32[328,8,128]{2,1,0:T(8,128)} async-done(((f32[164,8,128]{2,1,0:T(8,128)}), f32[328,8,128]{2,1,0:T(8,128)}) %all-gather.19.cloned.1.call-update) | async-done | bytes 1343504 | tf_op jit(solution)/shard_map/all_gather | solution.py:58
  105.0 4.7 %chain.7 = f32[16,2,8,128]{3,2,1,0:T(8,128)} custom-call(f32[32,2,8,128]{3,2,1,0:T(8,128)} %slice.237.a, f32[28,6,8,128]{3,2,1,0:T(8,128)} %copy-done, f32[20,6,8,128]{3,2,1,0:T(8,128)} %copy-done.3, f32[32,4,8,128]{3,2,1,0:T(8,128)} %copy-done.1), custom_call_target="tpu_custom_call" | custom-call | tf_op jit(solution)/shard_map/chain/pallas_call | solution.py:433
  109.6 9.4 %all-gather.3 = f32[32,2,8,128]{3,2,1,0:T(8,128)S(1)} all-gather(f32[16,2,8,128]{3,2,1,0:T(8,128)} %chain.7), channel_id=5, replica_groups={{0,68},{32,124},{128,196},{160,252},{256,324},{288,380},{384,452},{416,..., dimensions={0}, use_global_device_ids=true | all-gather | bytes 393216 | tf_op jit(solution)/shard_map/all_gather | solution.py:58
  122.1 4.7 %chain.8 = f32[16,2,8,128]{3,2,1,0:T(8,128)} custom-call(f32[32,2,8,128]{3,2,1,0:T(8,128)} %broadcast_select_fusion.6.a, f32[28,6,8,128]{3,2,1,0:T(8,128)} %copy-done, f32[20,6,8,128]{3,2,1,0:T(8,128)} %copy-done.3, f32[32,4,8,128]{3,2,1,0:T(8,128)} %copy-done.1), custom_call_target="tpu_custom_call" | custom-call | tf_op jit(solution)/shard_map/chain/pallas_call | solution.py:433
  126.7 10.7 %all-gather.4 = f32[32,2,8,128]{3,2,1,0:T(8,128)S(1)} all-gather(f32[16,2,8,128]{3,2,1,0:T(8,128)} %chain.8), channel_id=6, replica_groups={{64,132},{96,188},{192,260},{224,316},{320,388},{352,444},{448,4},{480,..., dimensions={0}, use_global_device_ids=true | all-gather | bytes 393216 | tf_op jit(solution)/shard_map/all_gather | solution.py:58
  140.2 4.7 %chain.9 = f32[16,2,8,128]{3,2,1,0:T(8,128)} custom-call(f32[32,2,8,128]{3,2,1,0:T(8,128)} %broadcast_select_fusion.2.a, f32[28,6,8,128]{3,2,1,0:T(8,128)} %copy-done, f32[20,6,8,128]{3,2,1,0:T(8,128)} %copy-done.3, f32[32,4,8,128]{3,2,1,0:T(8,128)} %copy-done.1), custom_call_target="tpu_custom_call" | custom-call | tf_op jit(solution)/shard_map/chain/pallas_call | solution.py:433
  144.9 9.5 %all-gather.5 = f32[32,2,8,128]{3,2,1,0:T(8,128)S(1)} all-gather(f32[16,2,8,128]{3,2,1,0:T(8,128)} %chain.9), channel_id=7, replica_groups={{0,68},{32,124},{128,196},{160,252},{256,324},{288,380},{384,452},{416,..., dimensions={0}, use_global_device_ids=true | all-gather | bytes 393216 | tf_op jit(solution)/shard_map/all_gather | solution.py:58
  158.5 4.7 %chain.10 = f32[16,2,8,128]{3,2,1,0:T(8,128)} custom-call(f32[32,2,8,128]{3,2,1,0:T(8,128)} %broadcast_select_fusion.5.a, f32[28,6,8,128]{3,2,1,0:T(8,128)} %copy-done, f32[20,6,8,128]{3,2,1,0:T(8,128)} %copy-done.3, f32[32,4,8,128]{3,2,1,0:T(8,128)} %copy-done.1), custom_call_target="tpu_custom_call" | custom-call | tf_op jit(solution)/shard_map/chain/pallas_call | solution.py:433
  163.2 11.0 %all-gather.6 = f32[32,2,8,128]{3,2,1,0:T(8,128)S(1)} all-gather(f32[16,2,8,128]{3,2,1,0:T(8,128)} %chain.10), channel_id=8, replica_groups={{64,132},{96,188},{192,260},{224,316},{320,388},{352,444},{448,4},{480,..., dimensions={0}, use_global_device_ids=true | all-gather | bytes 393216 | tf_op jit(solution)/shard_map/all_gather | solution.py:58
  176.9 4.7 %chain.11 = f32[16,2,8,128]{3,2,1,0:T(8,128)} custom-call(f32[32,2,8,128]{3,2,1,0:T(8,128)} %broadcast_select_fusion.1.a, f32[28,6,8,128]{3,2,1,0:T(8,128)} %copy-done, f32[20,6,8,128]{3,2,1,0:T(8,128)} %copy-done.3, f32[32,4,8,128]{3,2,1,0:T(8,128)} %copy-done.1), custom_call_target="tpu_custom_call" | custom-call | tf_op jit(solution)/shard_map/chain/pallas_call | solution.py:433
  181.6 8.6 %all-gather.7 = f32[32,2,8,128]{3,2,1,0:T(8,128)S(1)} all-gather(f32[16,2,8,128]{3,2,1,0:T(8,128)} %chain.11), channel_id=9, replica_groups={{0,68},{32,124},{128,196},{160,252},{256,324},{288,380},{384,452},{416,..., dimensions={0}, use_global_device_ids=true | all-gather | bytes 393216 | tf_op jit(solution)/shard_map/all_gather | solution.py:58
  193.5 4.7 %chain.12 = f32[16,2,8,128]{3,2,1,0:T(8,128)} custom-call(f32[32,2,8,128]{3,2,1,0:T(8,128)} %broadcast_select_fusion.4.a, f32[28,6,8,128]{3,2,1,0:T(8,128)} %copy-done, f32[20,6,8,128]{3,2,1,0:T(8,128)} %copy-done.3, f32[32,4,8,128]{3,2,1,0:T(8,128)} %copy-done.1), custom_call_target="tpu_custom_call" | custom-call | tf_op jit(solution)/shard_map/chain/pallas_call | solution.py:433
  198.2 10.3 %all-gather.8 = f32[32,2,8,128]{3,2,1,0:T(8,128)S(1)} all-gather(f32[16,2,8,128]{3,2,1,0:T(8,128)} %chain.12), channel_id=10, replica_groups={{64,132},{96,188},{192,260},{224,316},{320,388},{352,444},{448,4},{480,..., dimensions={0}, use_global_device_ids=true | all-gather | bytes 393216 | tf_op jit(solution)/shard_map/all_gather | solution.py:58
  211.3 4.7 %chain.13 = f32[16,2,8,128]{3,2,1,0:T(8,128)} custom-call(f32[32,2,8,128]{3,2,1,0:T(8,128)} %broadcast_select_fusion.a, f32[28,6,8,128]{3,2,1,0:T(8,128)} %copy-done, f32[20,6,8,128]{3,2,1,0:T(8,128)} %copy-done.3, f32[32,4,8,128]{3,2,1,0:T(8,128)} %copy-done.1), custom_call_target="tpu_custom_call" | custom-call | tf_op jit(solution)/shard_map/chain/pallas_call | solution.py:433
  215.9 8.9 %all-gather.9 = f32[32,2,8,128]{3,2,1,0:T(8,128)S(1)} all-gather(f32[16,2,8,128]{3,2,1,0:T(8,128)} %chain.13), channel_id=11, replica_groups={{0,68},{32,124},{128,196},{160,252},{256,324},{288,380},{384,452},{416,..., dimensions={0}, use_global_device_ids=true | all-gather | bytes 393216 | tf_op jit(solution)/shard_map/all_gather | solution.py:58
  228.1 6.1 %last.1 = f32[1,3,2,4,16,128]{5,4,3,2,1,0:T(8,128)} custom-call(s32[2]{0:T(128)} %pad_add_fusion.sc, f32[32,2,8,128]{3,2,1,0:T(8,128)} %broadcast_select_fusion.3.a, f32[28,6,8,128]{3,2,1,0:T(8,128)} %copy-done, f32[20,6,8,128]{3,2,1,0:T(8,128)} %copy-done.3, f32[32,4,8,128]{3,2,1,0:T(8,128)} %copy-done.1, f32[20,10,2,8,128]{4,3,2,1,0:T(8,128)} %get-tuple-element.10.big, ...), custom_call_target="tpu_custom_call" | custom-call | tf_op jit(solution)/shard_map/last/pallas_call | solution.py:443
  (93 shorter events, 45.0 us)
Async XLA Ops:
  6.5 93.1 %all-gather.19.cloned.1.call-start = ((), (), s32[]{:S(2)}) async-start(), calls=%async_computation | async-start | bytes 2015232 | tf_op jit(solution)/shard_map/all_gather | solution.py:58
  20.1 0.8 copy-start.4
  20.9 22.4 %collective-permute-start = (f32[64,2,8,128]{3,2,1,0:T(8,128)S(1)}, f32[64,2,8,128]{3,2,1,0:T(8,128)S(1)}, u32[]{:S(2)}, u32[]{:S(2)}) collective-permute-start(f32[64,2,8,128]{3,2,1,0:T(8,128)S(1)} %pad_maximum_fusion.1), channel_id=1, source_target_pairs={{0,2},{32,34},{64,66},{96,98},{128,130},{160,162},{192,194},{224,2... | collective-permute-start | bytes 1572872 | tf_op jit(solution)/shard_map/ppermute | solution.py:390
  24.8 19.8 %collective-permute-start.1 = (f32[64,2,8,128]{3,2,1,0:T(8,128)S(1)}, f32[64,2,8,128]{3,2,1,0:T(8,128)S(1)}, u32[]{:S(2)}, u32[]{:S(2)}) collective-permute-start(f32[64,2,8,128]{3,2,1,0:T(8,128)S(1)} %pad_maximum_fusion.2), channel_id=1, source_target_pairs={{0,30},{32,62},{64,94},{96,126},{128,158},{160,190},{192,222},{224... | collective-permute-start | bytes 1572872 | tf_op jit(solution)/shard_map/ppermute | solution.py:391
  43.4 1.2 copy-start.11
  44.6 0.8 copy-start.12
  54.4 9.9 %collective-permute-start.2 = (f32[64,8,128]{2,1,0:T(8,128)S(1)}, f32[64,8,128]{2,1,0:T(8,128)S(1)}, u32[]{:S(2)}, u32[]{:S(2)}) collective-permute-start(f32[64,8,128]{2,1,0:T(8,128)S(1)} %pad_maximum_fusion.5), channel_id=1, source_target_pairs={{0,2},{32,62},{64,66},{96,126},{128,130},{160,190},{192,194},{224,... | collective-permute-start | bytes 786440 | tf_op jit(solution)/shard_map/ppermute | solution.py:411
  64.4 16.0 %collective-permute-start.3 = (f32[100,8,128]{2,1,0:T(8,128)S(1)}, f32[100,8,128]{2,1,0:T(8,128)S(1)}, u32[]{:S(2)}, u32[]{:S(2)}) collective-permute-start(f32[100,8,128]{2,1,0:T(8,128)S(1)} %pad_maximum_fusion.3), channel_id=1, source_target_pairs={{0,4},{32,60},{64,68},{96,124},{128,132},{160,188},{192,196},{224,... | collective-permute-start | bytes 1228808 | tf_op jit(solution)/shard_map/ppermute | solution.py:411
  82.9 7.9 %collective-permute-start.4 = (f32[12,2,2,8,128]{4,3,2,1,0:T(8,128)S(1)}, f32[12,2,2,8,128]{4,3,2,1,0:T(8,128)S(1)}, u32[]{:S(2)}, u32[]{:S(2)}) collective-permute-start(f32[12,2,2,8,128]{4,3,2,1,0:T(8,128)S(1)} %constant_dynamic-slice_fusion), channel_id=1, source_target_pairs={{0,32},{1,33},{2,34},{3,35},{4,36},{5,37},{6,38},{7,39},{8,40},{9,... | collective-permute-start | bytes 589832 | tf_op jit(solution)/shard_map/ppermute | solution.py:402
  103.0 1.0 copy-start.1
  103.9 0.9 copy-start
  103.9 1.0 copy-start.3
  105.0 16.3 %copy-start.2 = (f32[32,4,8,128]{3,2,1,0:T(8,128)S(1)}, f32[32,4,8,128]{3,2,1,0:T(8,128)}, u32[]{:S(2)}) copy-start(f32[32,4,8,128]{3,2,1,0:T(8,128)} %copy-done.1) | copy-start | bytes 1572868
  122.0 17.4 %copy-start.10 = (f32[32,2,8,128]{3,2,1,0:T(8,128)S(1)}, f32[32,2,8,128]{3,2,1,0:T(8,128)}, u32[]{:S(2)}) copy-start(f32[32,2,8,128]{3,2,1,0:T(8,128)} %broadcast_select_fusion.6.a) | copy-start | bytes 786436
  140.2 17.6 %copy-start.7 = (f32[32,2,8,128]{3,2,1,0:T(8,128)S(1)}, f32[32,2,8,128]{3,2,1,0:T(8,128)}, u32[]{:S(2)}) copy-start(f32[32,2,8,128]{3,2,1,0:T(8,128)} %broadcast_select_fusion.2.a) | copy-start | bytes 786436
  158.5 17.7 %copy-start.8 = (f32[32,2,8,128]{3,2,1,0:T(8,128)S(1)}, f32[32,2,8,128]{3,2,1,0:T(8,128)}, u32[]{:S(2)}) copy-start(f32[32,2,8,128]{3,2,1,0:T(8,128)} %broadcast_select_fusion.5.a) | copy-start | bytes 786436
  176.9 15.8 %copy-start.9 = (f32[32,2,8,128]{3,2,1,0:T(8,128)S(1)}, f32[32,2,8,128]{3,2,1,0:T(8,128)}, u32[]{:S(2)}) copy-start(f32[32,2,8,128]{3,2,1,0:T(8,128)} %broadcast_select_fusion.1.a) | copy-start | bytes 786436
  193.5 17.0 %copy-start.6 = (f32[32,2,8,128]{3,2,1,0:T(8,128)S(1)}, f32[32,2,8,128]{3,2,1,0:T(8,128)}, u32[]{:S(2)}) copy-start(f32[32,2,8,128]{3,2,1,0:T(8,128)} %broadcast_select_fusion.4.a) | copy-start | bytes 786436
  211.3 16.1 %copy-start.5 = (f32[32,2,8,128]{3,2,1,0:T(8,128)S(1)}, f32[32,2,8,128]{3,2,1,0:T(8,128)}, u32[]{:S(2)}) copy-start(f32[32,2,8,128]{3,2,1,0:T(8,128)} %broadcast_select_fusion.a) | copy-start | bytes 786436
Sparse Core Ops, SparseCore 0:
  81.4 18.2 all-gather.18

commit v2 on v1

--- a/solution.py
+++ b/solution.py
@@ -104,6 +104,11 @@
     return w[0] * xs[0] + w[1] * xs[1] + w[2] * xs[2]
 
 
+def unrolled(count, step):
+    for n in range(count):
+        step(n, 0)
+
+
 def pack_kernel(nv, st, fr, kr, out):
     for p in range(4):
         for par in range(2):
@@ -143,7 +148,7 @@
                 start = raw(ref, i, 6 + s)
                 v1[pl.ds(base + i, 2), s] = first_combo(w, start)
             return 0
-        lax.fori_loop(0, count // 2, load_v1, 0)
+        unrolled(count // 2, load_v1)
 
     for ref, base, count in segs:
         def node_one(n, _, ref=ref, base=base):
@@ -179,7 +184,7 @@
             b2[at, 1] = nv + gq - fk * qv
             b2[at, 2] = g[2]
             return 0
-        lax.fori_loop(0, count // 2, node_one, 0)
+        unrolled(count // 2, node_one)
 
     def node_two(n, _):
         q = 2 + 2 * n
@@ -190,7 +195,7 @@
         big[at, 4] = nu
         big[at, 5] = nv
         return 0
-    lax.fori_loop(0, 8, node_two, 0)
+    unrolled(8, node_two)
 
     def integrals(n, _):
         q = 4 + 2 * n
@@ -207,7 +212,7 @@
             xp[to, 2 * m] = f - f * xu - gx
             xp[to, 2 * m + 1] = gx - fk * xv
         return 0
-    lax.fori_loop(0, 6, integrals, 0)
+    unrolled(6, integrals)
 
     def restrict(x):
         return 0.25 * (x[0, 0] + x[0, 1] + x[1, 0] + x[1, 1])
@@ -225,7 +230,7 @@
         aux[n, 2] = 1.0 / (1.0 + f)
         aux[n, 3] = 1.0 / (1.0 + k)
         return 0
-    lax.fori_loop(0, 10, coarsen, 0)
+    unrolled(10, coarsen)
 
     def make_unit(n, _):
         for m in range(2):
@@ -242,7 +247,7 @@
                 unit[n, 3 * m + s] = val
             unit[n, 3 * m + 2] = g
         return 0
-    lax.fori_loop(0, 4, make_unit, 0)
+    unrolled(4, make_unit)
 
 
 def coarse_node(src, src_off, prm, prm_off, m, rates, rate_off, dst, dst_off, count):
@@ -258,7 +263,7 @@
         dst[pl.ds(dst_off + i, 4), 0] = nu
         dst[pl.ds(dst_off + i, 4), 1] = nv
         return 0
-    lax.fori_loop(0, count // 4, step, 0)
+    unrolled(count // 4, step)
 
 
 def two_slices(a, pa, pb, aux, n1, n2, n3, out):
@@ -268,14 +273,31 @@
     coarse_node(n3, 0, pb, 2, 1, aux, 8, out, 0, 16)
 
 
-def chain_kernel(a, pa, pb, aux, out, n1, n2, n3):
+def take(flag, moved, a_in, a):
+    @pl.when(flag != 0)
+    def _():
+        for side in range(2):
+            a[pl.ds(16 * side, 16)] = moved[side]
+
+    @pl.when(flag == 0)
+    def _():
+        a[...] = a_in[...]
+
+
+def first_chain_kernel(a, pa, pb, aux, out, n1, n2, n3):
     two_slices(a, pa, pb, aux, n1, n2, n3, out)
 
 
-def last_kernel(sc, a, pa, pb, aux, big, prev, res, n1, n2, n3, n4, gs, v1, tp):
+def chain_kernel(sc, moved, a_in, pa, pb, aux, a, out, n1, n2, n3):
+    take(sc[0], moved, a_in, a)
+    two_slices(a, pa, pb, aux, n1, n2, n3, out)
+
+
+def last_kernel(sc, moved, a_in, pa, pb, aux, big, prev, res, a, n1, n2, n3, n4, gs, v1, tp):
+    take(sc[0], moved, a_in, a)
     two_slices(a, pa, pb, aux, n1, n2, n3, n4)
-    core = sc[0]
-    yh = sc[1]
+    core = sc[1]
+    yh = sc[2]
 
     @pl.when(core == 0)
     def _():
@@ -324,7 +346,7 @@
         tp[to, 8] = bu
         tp[to, 9] = bv
         return 0
-    lax.fori_loop(0, 6, update, 0)
+    unrolled(6, update)
 
     def put(node, s, plane, x):
         res[0, node, s, plane, pl.ds(0, 8, stride=2), :] = x[0]
@@ -344,7 +366,7 @@
         tp[at, 10] = nu
         tp[at, 11] = nv
         return 0
-    lax.fori_loop(0, 4, node_one, 0)
+    unrolled(4, node_one)
 
     for n in range(2):
         i = 4 + 2 * n
@@ -415,37 +437,49 @@
     got2 = send([units, got1[0:24],
                  jnp.where(left, jnp.concatenate([aux1[1:4], aux[0:4]]),
                            jnp.concatenate([aux[6:10], aux1[0:3]]))], 2)
-    sides = gather(jnp.concatenate([got1, got2]), core_groups())
-
-    def pick(side, start, planes, fields):
-        return sides[side, start:start + planes * fields].reshape(planes, fields, 8, 128)
-
-    pa = jnp.concatenate([pick(0, 64 + 48, 4, 6), pick(0, 64, 4, 6), pick(0, 0, 4, 6), units[0],
-                          pick(1, 0, 4, 6), pick(1, 64, 4, 6), pick(1, 64 + 48, 4, 6)])
-    pb = jnp.concatenate([pick(0, 64 + 24, 4, 6), pick(0, 24, 4, 6), units[1],
-                          pick(1, 24, 4, 6), pick(1, 64 + 24, 4, 6)])
-    aux = jnp.concatenate([pick(0, 64 + 72, 7, 4), pick(0, 48, 4, 4), aux,
-                           pick(1, 48, 4, 4), pick(1, 64 + 72, 7, 4)])
+    near = gather(got1, core_groups())
+    far = gather(got2[:48], core_groups())
+    edge2 = gather(got2[48:], core_groups())
+
+    def pick(rows, side, start, planes, fields):
+        return rows[side, start:start + planes * fields].reshape(planes, fields, 8, 128)
+
+    pa = jnp.concatenate([pick(edge2, 0, 0, 4, 6), pick(far, 0, 0, 4, 6), pick(near, 0, 0, 4, 6), units[0],
+                          pick(near, 1, 0, 4, 6), pick(far, 1, 0, 4, 6), pick(edge2, 1, 0, 4, 6)])
+    pb = jnp.concatenate([pick(far, 0, 24, 4, 6), pick(near, 0, 24, 4, 6), units[1],
+                          pick(near, 1, 24, 4, 6), pick(far, 1, 24, 4, 6)])
+    aux = jnp.concatenate([pick(edge2, 0, 24, 7, 4), pick(near, 0, 48, 4, 4), aux,
+                           pick(near, 1, 48, 4, 4), pick(edge2, 1, 24, 7, 4)])
     state = aux[:, 0:2]
 
     scratch = [vmem(28, 2, 8, 128), vmem(24, 2, 8, 128), vmem(20, 2, 8, 128)]
-    for turn in range(7):
-        out = pl.pallas_call(
-            chain_kernel, out_shape=shape(16, 2, 8, 128), in_specs=[VM] * 4, out_specs=VM,
+
+    def exchange(out, turn):
+        moved = gather(out, turn_groups(turn % 2))[0]
+        moved = gather(moved, core_groups())
+        takes = jnp.logical_and(chip % 2 == (turn + 1) % 2, chip > 0)
+        return moved, takes.astype(jnp.int32)
+
+    out = pl.pallas_call(
+        first_chain_kernel, out_shape=shape(16, 2, 8, 128), in_specs=[VM] * 4, out_specs=VM,
+        scratch_shapes=scratch, name="chain",
+    )(state, pa, pb, aux)
+    for turn in range(6):
+        moved, takes = exchange(out, turn)
+        state, out = pl.pallas_call(
+            chain_kernel, out_shape=(shape(32, 2, 8, 128), shape(16, 2, 8, 128)),
+            in_specs=[SM] + [VM] * 5, out_specs=(VM, VM),
             scratch_shapes=scratch, name="chain",
-        )(state, pa, pb, aux)
-        moved = gather(out, turn_groups(turn % 2))[0]
-        moved = gather(moved, core_groups()).reshape(32, 2, 8, 128)
-        takes = jnp.logical_and(chip % 2 == (turn + 1) % 2, chip > 0)
-        state = jnp.where(takes, moved, state)
-
-    scalars = jnp.stack([core, yh]).astype(jnp.int32)
+        )(takes.reshape(1), moved, state, pa, pb, aux)
+    moved, takes = exchange(out, 6)
+
+    scalars = jnp.stack([takes, core, yh]).astype(jnp.int32)
     return pl.pallas_call(
-        last_kernel, out_shape=shape(1, 3, 2, 4, 16, 128), in_specs=[SM] + [VM] * 6, out_specs=VM,
-        scratch_shapes=scratch + [vmem(16, 2, 8, 128), vmem(8, 6, 8, 128),
+        last_kernel, out_shape=shape(1, 3, 2, 4, 16, 128), in_specs=[SM] + [VM] * 7, out_specs=VM,
+        scratch_shapes=[vmem(32, 2, 8, 128)] + scratch + [vmem(16, 2, 8, 128), vmem(8, 6, 8, 128),
                                   vmem(12, 2, 2, 8, 128), vmem(12, 12, 2, 8, 128)],
         name="last",
-    )(scalars, state, pa, pb, aux, big, prev)
+    )(scalars, moved, state, pa, pb, aux, big, prev)
 
 
 def solution(mesh):

time: 245 us -> 194 us (0.79)
  waiting for transfers between devices: 45.5 us -> 26.9 us
  Pallas kernels: 46.2 us -> 30.6 us
  between operations: 13.8 us -> 0.44 us
  blocking collectives: 99.1 us -> 106 us
  other arithmetic: 9.53 us -> 3.43 us
  local copies, waits for them, and re-layouts: 7.8 us -> 4.67 us
    pallas_call x7, Pallas kernels: 32.7 us -> 21.4 us  [the longest x6 18.4 us: body(): pl.pallas_call(chain_kernel, out_shape=(shape(32, 2, 8, 128), shape(16, 2...]
    all_gather x1 -> x0, waiting for transfers between devices: 7.25 us -> none  [gather(): return lax.all_gather(x, AX, axis=0, axis_index_groups=groups, tiled=False)]
    all_gather x16 -> x19, blocking collectives: 99.1 us -> 106 us  [gather(): return lax.all_gather(x, AX, axis=0, axis_index_groups=groups, tiled=False)]
    ppermute x1, waiting for transfers between devices: 5.94 us -> 0.01 us  [body(): prev = lax.ppermute(mine[:, 4:6], AX, slice_pairs())]
    select_n x7 -> x0, other arithmetic: 5.25 us -> none  [body(): state = jnp.where(takes, moved, state)]
    ppermute x2, waiting for transfers between devices: 22 us -> 17.3 us  [send(): return lax.ppermute(jnp.concatenate(rows), AX, split_pairs(step))]
    slice x10 -> x14, local copies, waits for them, and re-layouts: 3.27 us -> 0.19 us  [the longest x5 0.1 us: pick(): rows[side, start:start + planes * fields].reshape(planes, fields, 8, 128)]
  transfers between devices with their start and end apart: 6 -> 5, of which waited for: 6 -> 4; matrix products, arithmetic and copies ran while one was open for 1% -> 2% of each run, Pallas kernels for 0% -> 0%
where the time goes in v2:
time: 194 us; the launch traced here: 191 us
  blocking collectives  106 us (55%)
  Pallas kernels  30.6 us (16%)
  waiting for transfers between devices  26.9 us (14%)
  starting transfers between devices  19.1 us (10%)
  local copies, waits for them, and re-layouts  4.67 us (2%)
  other arithmetic  3.43 us (2%)
    all_gather x19, blocking collectives, gather(): return lax.all_gather(x, AX, axis=0, axis_index_groups=groups, tiled=False)  106 us
    pallas_call x6, Pallas kernels, body(): pl.pallas_call(chain_kernel, out_shape=(shape(32, 2, 8, 128), shape(16, 2...  18.4 us
    ppermute x2, waiting for transfers between devices, send(): return lax.ppermute(jnp.concatenate(rows), AX, split_pairs(step))  17.3 us
    ppermute x1, starting transfers between devices, body(): hi = lax.ppermute(edge(pair[0:6], pair[6:8]), AX, z_pairs(-1))  9.5 us
    ppermute x1, waiting for transfers between devices, body(): lo = lax.ppermute(edge(pair[2:8], pair[0:2]), AX, z_pairs(1))  8.41 us
    pallas_call x1, Pallas kernels, body(): pl.pallas_call(last_kernel, out_shape=shape(1, 3, 2, 4, 16, 128), in_spec...  3.98 us
  transfers between devices with their start and end apart: 5, of which 4 were waited for; matrix products, arithmetic and copies ran while one was open for 2% of the time, Pallas kernels for 0%

profile of v2, /device:TPU:6, one launch (start us, length us, event | category | flops | bytes accessed | tf_op | source)
XLA Modules:
  0.0 190.8 jit_solution(14798522622107256392)
XLA Ops:
  1.7 11.8 %all-gather.pair = f32[8,10,2,8,128]{4,3,2,1,0:T(8,128)S(1)} all-gather(f32[4,10,2,8,128]{4,3,2,1,0:T(8,128)} %pack.1), channel_id=2, replica_groups={{0,1},{32,33},{64,65},{96,97},{128,129},{160,161},{192,193},{224,225},{..., dimensions={0}, use_global_device_ids=true | all-gather | bytes 983040 | tf_op jit(solution)/shard_map/all_gather | solution.py:58
  14.4 3.8 %collective-permute-start = (f32[64,2,8,128]{3,2,1,0:T(8,128)S(1)}, f32[64,2,8,128]{3,2,1,0:T(8,128)S(1)}, u32[]{:S(2)}, u32[]{:S(2)}) collective-permute-start(f32[64,2,8,128]{3,2,1,0:T(8,128)S(1)} %pad_maximum_fusion), channel_id=1, source_target_pairs={{0,2},{32,34},{64,66},{96,98},{128,130},{160,162},{192,194},{224,2... | collective-permute-start | bytes 1572872 | tf_op jit(solution)/shard_map/ppermute | solution.py:412
  18.3 9.5 %collective-permute-start.1 = (f32[64,2,8,128]{3,2,1,0:T(8,128)S(1)}, f32[64,2,8,128]{3,2,1,0:T(8,128)S(1)}, u32[]{:S(2)}, u32[]{:S(2)}) collective-permute-start(f32[64,2,8,128]{3,2,1,0:T(8,128)S(1)} %pad_maximum_fusion.1), channel_id=1, source_target_pairs={{0,30},{32,62},{64,94},{96,126},{128,158},{160,190},{192,222},{224... | collective-permute-start | bytes 1572872 | tf_op jit(solution)/shard_map/ppermute | solution.py:413
  28.4 8.4 %collective-permute-done.lo = f32[64,2,8,128]{3,2,1,0:T(8,128)S(1)} collective-permute-done((f32[64,2,8,128]{3,2,1,0:T(8,128)S(1)}, f32[64,2,8,128]{3,2,1,0:T(8,128)S(1)}, u32[]{:S(2)}, u32[]{:S(2)}) %collective-permute-start) | collective-permute-done | bytes 524320 | tf_op jit(solution)/shard_map/ppermute | solution.py:412
  38.9 3.6 %sweep.1 = (f32[20,10,2,8,128]{4,3,2,1,0:T(8,128)}, f32[4,6,8,128]{3,2,1,0:T(8,128)}, f32[10,4,8,128]{3,2,1,0:T(8,128)}) custom-call(f32[8,10,2,8,128]{4,3,2,1,0:T(8,128)} %copy-done.3, f32[64,2,8,128]{3,2,1,0:T(8,128)} %copy-done.4, f32[64,2,8,128]{3,2,1,0:T(8,128)} %copy-done.5), custom_call_target="tpu_custom_call" | custom-call | tf_op jit(solution)/shard_map/sweep/pallas_call | solution.py:414
  46.3 3.5 %all-gather.1 = f32[128,8,128]{2,1,0:T(8,128)S(1)} all-gather(f32[64,8,128]{2,1,0:T(8,128)S(1)} %pad_maximum_fusion.3), channel_id=3, replica_groups={{0,32},{64,96},{128,160},{192,224},{256,288},{320,352},{384,416},{448,4..., dimensions={0}, use_global_device_ids=true | all-gather | bytes 786432 | tf_op jit(solution)/shard_map/all_gather | solution.py:58
  53.5 6.3 %collective-permute-done.2 = f32[64,8,128]{2,1,0:T(8,128)S(1)} collective-permute-done((f32[64,8,128]{2,1,0:T(8,128)S(1)}, f32[64,8,128]{2,1,0:T(8,128)S(1)}, u32[]{:S(2)}, u32[]{:S(2)}) %collective-permute-start.2) | collective-permute-done | bytes 262176 | tf_op jit(solution)/shard_map/ppermute | solution.py:433
  61.8 3.0 %all-gather.3 = f32[128,8,128]{2,1,0:T(8,128)S(1)} all-gather(f32[64,8,128]{2,1,0:T(8,128)S(1)} %collective-permute-done.2), channel_id=5, replica_groups={{0,32},{64,96},{128,160},{192,224},{256,288},{320,352},{384,416},{448,4..., dimensions={0}, use_global_device_ids=true | all-gather | bytes 786432 | tf_op jit(solution)/shard_map/all_gather | solution.py:58
  64.9 11.0 %collective-permute-done.3 = f32[100,8,128]{2,1,0:T(8,128)S(1)} collective-permute-done((f32[100,8,128]{2,1,0:T(8,128)S(1)}, f32[100,8,128]{2,1,0:T(8,128)S(1)}, u32[]{:S(2)}, u32[]{:S(2)}) %collective-permute-start.3) | collective-permute-done | bytes 409632 | tf_op jit(solution)/shard_map/ppermute | solution.py:433
  85.2 8.5 %all-gather.5 = f32[32,2,8,128]{3,2,1,0:T(8,128)S(1)} all-gather(f32[16,2,8,128]{3,2,1,0:T(8,128)} %chain.7), channel_id=7, replica_groups={{0,68},{32,124},{128,196},{160,252},{256,324},{288,380},{384,452},{416,..., dimensions={0}, use_global_device_ids=true | all-gather | bytes 393216 | tf_op jit(solution)/shard_map/all_gather | solution.py:58
  95.9 3.1 %chain.8 = (f32[32,2,8,128]{3,2,1,0:T(8,128)}, f32[16,2,8,128]{3,2,1,0:T(8,128)}) custom-call(s32[1]{0:T(128)} %bitcast.sc, f32[2,16,2,8,128]{4,3,2,1,0:T(8,128)} %bitcast.65, f32[32,2,8,128]{3,2,1,0:T(8,128)} %slice.246.a.a_in, f32[28,6,8,128]{3,2,1,0:T(8,128)} %copy-done, f32[20,6,8,128]{3,2,1,0:T(8,128)} %copy-done.2, f32[32,4,8,128]{3,2,1,0:T(8,128)} %copy-done.1), custom_call_target="tpu_custom_call" | custom-call | tf_op jit(solution)/shard_map/chain/pallas_call | solution.py:469
  99.0 10.6 %all-gather.6 = f32[32,2,8,128]{3,2,1,0:T(8,128)S(1)} all-gather(f32[16,2,8,128]{3,2,1,0:T(8,128)} %get-tuple-element.22), channel_id=8, replica_groups={{64,132},{96,188},{192,260},{224,316},{320,388},{352,444},{448,4},{480,..., dimensions={0}, use_global_device_ids=true | all-gather | bytes 393216 | tf_op jit(solution)/shard_map/all_gather | solution.py:58
  111.8 3.1 %chain.9 = (f32[32,2,8,128]{3,2,1,0:T(8,128)}, f32[16,2,8,128]{3,2,1,0:T(8,128)}) custom-call(s32[1]{0:T(128)} %bitcast.3.sc, f32[2,16,2,8,128]{4,3,2,1,0:T(8,128)} %bitcast.62, f32[32,2,8,128]{3,2,1,0:T(8,128)} %get-tuple-element.23.a_in, f32[28,6,8,128]{3,2,1,0:T(8,128)} %copy-done, f32[20,6,8,128]{3,2,1,0:T(8,128)} %copy-done.2, f32[32,4,8,128]{3,2,1,0:T(8,128)} %copy-done.1), custom_call_target="tpu_custom_call" | custom-call | tf_op jit(solution)/shard_map/chain/pallas_call | solution.py:469
  114.8 8.6 %all-gather.7 = f32[32,2,8,128]{3,2,1,0:T(8,128)S(1)} all-gather(f32[16,2,8,128]{3,2,1,0:T(8,128)} %get-tuple-element.24), channel_id=9, replica_groups={{0,68},{32,124},{128,196},{160,252},{256,324},{288,380},{384,452},{416,..., dimensions={0}, use_global_device_ids=true | all-gather | bytes 393216 | tf_op jit(solution)/shard_map/all_gather | solution.py:58
  125.6 3.1 %chain.10 = (f32[32,2,8,128]{3,2,1,0:T(8,128)}, f32[16,2,8,128]{3,2,1,0:T(8,128)}) custom-call(s32[1]{0:T(128)} %bitcast.sc, f32[2,16,2,8,128]{4,3,2,1,0:T(8,128)} %bitcast.63, f32[32,2,8,128]{3,2,1,0:T(8,128)} %get-tuple-element.25.a_in, f32[28,6,8,128]{3,2,1,0:T(8,128)} %copy-done, f32[20,6,8,128]{3,2,1,0:T(8,128)} %copy-done.2, f32[32,4,8,128]{3,2,1,0:T(8,128)} %copy-done.1), custom_call_target="tpu_custom_call" | custom-call | tf_op jit(solution)/shard_map/chain/pallas_call | solution.py:469
  128.7 10.9 %all-gather.8 = f32[32,2,8,128]{3,2,1,0:T(8,128)S(1)} all-gather(f32[16,2,8,128]{3,2,1,0:T(8,128)} %get-tuple-element.26), channel_id=10, replica_groups={{64,132},{96,188},{192,260},{224,316},{320,388},{352,444},{448,4},{480,..., dimensions={0}, use_global_device_ids=true | all-gather | bytes 393216 | tf_op jit(solution)/shard_map/all_gather | solution.py:58
  141.8 3.1 %chain.11 = (f32[32,2,8,128]{3,2,1,0:T(8,128)}, f32[16,2,8,128]{3,2,1,0:T(8,128)}) custom-call(s32[1]{0:T(128)} %bitcast.3.sc, f32[2,16,2,8,128]{4,3,2,1,0:T(8,128)} %bitcast.64, f32[32,2,8,128]{3,2,1,0:T(8,128)} %get-tuple-element.27.a_in, f32[28,6,8,128]{3,2,1,0:T(8,128)} %copy-done, f32[20,6,8,128]{3,2,1,0:T(8,128)} %copy-done.2, f32[32,4,8,128]{3,2,1,0:T(8,128)} %copy-done.1), custom_call_target="tpu_custom_call" | custom-call | tf_op jit(solution)/shard_map/chain/pallas_call | solution.py:469
  144.8 8.4 %all-gather.9 = f32[32,2,8,128]{3,2,1,0:T(8,128)S(1)} all-gather(f32[16,2,8,128]{3,2,1,0:T(8,128)} %get-tuple-element.28), channel_id=11, replica_groups={{0,68},{32,124},{128,196},{160,252},{256,324},{288,380},{384,452},{416,..., dimensions={0}, use_global_device_ids=true | all-gather | bytes 393216 | tf_op jit(solution)/shard_map/all_gather | solution.py:58
  156.1 3.1 %chain.12 = (f32[32,2,8,128]{3,2,1,0:T(8,128)}, f32[16,2,8,128]{3,2,1,0:T(8,128)}) custom-call(s32[1]{0:T(128)} %bitcast.sc, f32[2,16,2,8,128]{4,3,2,1,0:T(8,128)} %bitcast.60, f32[32,2,8,128]{3,2,1,0:T(8,128)} %get-tuple-element.29.a_in, f32[28,6,8,128]{3,2,1,0:T(8,128)} %copy-done, f32[20,6,8,128]{3,2,1,0:T(8,128)} %copy-done.2, f32[32,4,8,128]{3,2,1,0:T(8,128)} %copy-done.1), custom_call_target="tpu_custom_call" | custom-call | tf_op jit(solution)/shard_map/chain/pallas_call | solution.py:469
  159.2 10.2 %all-gather.10 = f32[32,2,8,128]{3,2,1,0:T(8,128)S(1)} all-gather(f32[16,2,8,128]{3,2,1,0:T(8,128)} %get-tuple-element.30), channel_id=12, replica_groups={{64,132},{96,188},{192,260},{224,316},{320,388},{352,444},{448,4},{480,..., dimensions={0}, use_global_device_ids=true | all-gather | bytes 393216 | tf_op jit(solution)/shard_map/all_gather | solution.py:58
  171.5 3.1 %chain.13 = (f32[32,2,8,128]{3,2,1,0:T(8,128)}, f32[16,2,8,128]{3,2,1,0:T(8,128)}) custom-call(s32[1]{0:T(128)} %bitcast.3.sc, f32[2,16,2,8,128]{4,3,2,1,0:T(8,128)} %bitcast.61, f32[32,2,8,128]{3,2,1,0:T(8,128)} %get-tuple-element.31.a_in, f32[28,6,8,128]{3,2,1,0:T(8,128)} %copy-done, f32[20,6,8,128]{3,2,1,0:T(8,128)} %copy-done.2, f32[32,4,8,128]{3,2,1,0:T(8,128)} %copy-done.1), custom_call_target="tpu_custom_call" | custom-call | tf_op jit(solution)/shard_map/chain/pallas_call | solution.py:469
  174.6 9.0 %all-gather.11 = f32[32,2,8,128]{3,2,1,0:T(8,128)S(1)} all-gather(f32[16,2,8,128]{3,2,1,0:T(8,128)} %get-tuple-element.32), channel_id=13, replica_groups={{0,68},{32,124},{128,196},{160,252},{256,324},{288,380},{384,452},{416,..., dimensions={0}, use_global_device_ids=true | all-gather | bytes 393216 | tf_op jit(solution)/shard_map/all_gather | solution.py:58
  183.6 3.3 %all-gather.18 = f32[32,2,8,128]{3,2,1,0:T(8,128)} all-gather(f32[16,2,8,128]{3,2,1,0:T(8,128)S(1)} %slice.266), channel_id=20, replica_groups={{0,32},{64,96},{128,160},{192,224},{256,288},{320,352},{384,416},{448,4..., dimensions={0}, use_global_device_ids=true | all-gather | bytes 393216 | tf_op jit(solution)/shard_map/all_gather | solution.py:58
  186.9 4.0 %last.1 = f32[1,3,2,4,16,128]{5,4,3,2,1,0:T(8,128)} custom-call(s32[3]{0:T(128)} %pad_add_fusion.sc, f32[2,16,2,8,128]{4,3,2,1,0:T(8,128)} %bitcast.59, f32[32,2,8,128]{3,2,1,0:T(8,128)} %get-tuple-element.33.a_in, f32[28,6,8,128]{3,2,1,0:T(8,128)} %copy-done, f32[20,6,8,128]{3,2,1,0:T(8,128)} %copy-done.2, f32[32,4,8,128]{3,2,1,0:T(8,128)} %copy-done.1, ...), custom_call_target="tpu_custom_call" | custom-call | tf_op jit(solution)/shard_map/last/pallas_call | solution.py:477
  (75 shorter events, 37.6 us)
Async XLA Ops:
  13.5 0.9 copy-start.3
  14.4 22.4 %collective-permute-start = (f32[64,2,8,128]{3,2,1,0:T(8,128)S(1)}, f32[64,2,8,128]{3,2,1,0:T(8,128)S(1)}, u32[]{:S(2)}, u32[]{:S(2)}) collective-permute-start(f32[64,2,8,128]{3,2,1,0:T(8,128)S(1)} %pad_maximum_fusion), channel_id=1, source_target_pairs={{0,2},{32,34},{64,66},{96,98},{128,130},{160,162},{192,194},{224,2... | collective-permute-start | bytes 1572872 | tf_op jit(solution)/shard_map/ppermute | solution.py:412
  18.3 19.8 %collective-permute-start.1 = (f32[64,2,8,128]{3,2,1,0:T(8,128)S(1)}, f32[64,2,8,128]{3,2,1,0:T(8,128)S(1)}, u32[]{:S(2)}, u32[]{:S(2)}) collective-permute-start(f32[64,2,8,128]{3,2,1,0:T(8,128)S(1)} %pad_maximum_fusion.1), channel_id=1, source_target_pairs={{0,30},{32,62},{64,94},{96,126},{128,158},{160,190},{192,222},{224... | collective-permute-start | bytes 1572872 | tf_op jit(solution)/shard_map/ppermute | solution.py:413
  36.8 1.2 copy-start.4
  38.1 0.8 copy-start.5
  43.4 8.5 %collective-permute-start.4 = (f32[12,2,2,8,128]{4,3,2,1,0:T(8,128)S(1)}, f32[12,2,2,8,128]{4,3,2,1,0:T(8,128)S(1)}, u32[]{:S(2)}, u32[]{:S(2)}) collective-permute-start(f32[12,2,2,8,128]{4,3,2,1,0:T(8,128)S(1)} %constant_dynamic-slice_fusion), channel_id=1, source_target_pairs={{0,32},{1,33},{2,34},{3,35},{4,36},{5,37},{6,38},{7,39},{8,40},{9,... | collective-permute-start | bytes 589832 | tf_op jit(solution)/shard_map/ppermute | solution.py:424
  49.9 9.9 %collective-permute-start.2 = (f32[64,8,128]{2,1,0:T(8,128)S(1)}, f32[64,8,128]{2,1,0:T(8,128)S(1)}, u32[]{:S(2)}, u32[]{:S(2)}) collective-permute-start(f32[64,8,128]{2,1,0:T(8,128)S(1)} %pad_maximum_fusion.4), channel_id=1, source_target_pairs={{0,2},{32,62},{64,66},{96,126},{128,130},{160,190},{192,194},{224,... | collective-permute-start | bytes 786440 | tf_op jit(solution)/shard_map/ppermute | solution.py:433
  59.9 16.0 %collective-permute-start.3 = (f32[100,8,128]{2,1,0:T(8,128)S(1)}, f32[100,8,128]{2,1,0:T(8,128)S(1)}, u32[]{:S(2)}, u32[]{:S(2)}) collective-permute-start(f32[100,8,128]{2,1,0:T(8,128)S(1)} %pad_maximum_fusion.2), channel_id=1, source_target_pairs={{0,4},{32,60},{64,68},{96,124},{128,132},{160,188},{192,196},{224,... | collective-permute-start | bytes 1228808 | tf_op jit(solution)/shard_map/ppermute | solution.py:433
  80.3 1.0 copy-start.1
  81.2 0.9 copy-start
  81.2 1.0 copy-start.2

commit v3 on v2

--- a/solution.py
+++ b/solution.py
@@ -14,6 +14,7 @@
 DIFF = (0.1, 0.05)
 VM = pl.BlockSpec(memory_space=pltpu.VMEM)
 SM = pl.BlockSpec(memory_space=pltpu.SMEM)
+SMALL = pltpu.CompilerParams(vmem_limit_bytes=16 * 1024 * 1024)
 
 
 def flat(z, yh, chip, core):
@@ -400,7 +401,7 @@
     left = core == 0
     own = pl.pallas_call(
         pack_kernel, out_shape=shape(4, 10, 2, 8, 128), in_specs=[VM] * 4, out_specs=VM,
-        name="pack",
+        name="pack", compiler_params=SMALL,
     )(node_values, start_state, feed_rate, kill_rate)
     pair = gather(own, pair_groups()).reshape(8, 10, 2, 8, 128)
 
@@ -417,7 +418,7 @@
         in_specs=[VM] * 3, out_specs=(VM, VM, VM),
         scratch_shapes=[vmem(24, 2, 2, 8, 128), vmem(20, 2, 2, 8, 128), vmem(20, 3, 2, 8, 128),
                         vmem(12, 4, 2, 8, 128), vmem(12, 4, 2, 8, 128), vmem(10, 8, 8, 128)],
-        name="sweep",
+        name="sweep", compiler_params=SMALL,
     )(pair, lo, hi)
 
     mine = lax.dynamic_slice_in_dim(big, 2 + 4 * yh, 12, 0)
@@ -462,14 +463,14 @@
 
     out = pl.pallas_call(
         first_chain_kernel, out_shape=shape(16, 2, 8, 128), in_specs=[VM] * 4, out_specs=VM,
-        scratch_shapes=scratch, name="chain",
+        scratch_shapes=scratch, name="chain", compiler_params=SMALL,
     )(state, pa, pb, aux)
     for turn in range(6):
         moved, takes = exchange(out, turn)
         state, out = pl.pallas_call(
             chain_kernel, out_shape=(shape(32, 2, 8, 128), shape(16, 2, 8, 128)),
             in_specs=[SM] + [VM] * 5, out_specs=(VM, VM),
-            scratch_shapes=scratch, name="chain",
+            scratch_shapes=scratch, name="chain", compiler_params=SMALL,
         )(takes.reshape(1), moved, state, pa, pb, aux)
     moved, takes = exchange(out, 6)
 
@@ -478,7 +479,7 @@
         last_kernel, out_shape=shape(1, 3, 2, 4, 16, 128), in_specs=[SM] + [VM] * 7, out_specs=VM,
         scratch_shapes=[vmem(32, 2, 8, 128)] + scratch + [vmem(16, 2, 8, 128), vmem(8, 6, 8, 128),
                                   vmem(12, 2, 2, 8, 128), vmem(12, 12, 2, 8, 128)],
-        name="last",
+        name="last", compiler_params=SMALL,
     )(scalars, moved, state, pa, pb, aux, big, prev)
 
 

time: 194 us -> 169 us (0.87)
  Pallas kernels: 30.6 us -> 10.1 us
  other arithmetic: 3.43 us -> 0.3 us
  waiting for transfers between devices: 26.9 us -> 29.1 us
  blocking collectives: 106 us -> 104 us
    pallas_call x6, Pallas kernels: 18.4 us -> 5.4 us  [body(): pl.pallas_call(chain_kernel, out_shape=(shape(32, 2, 8, 128), shape(16, 2...]
    pallas_call x1, Pallas kernels: 3.57 us -> 1.35 us  [body(): pl.pallas_call(sweep_kernel, out_shape=(shape(20, 10, 2, 8, 128), shape(4...]
    pallas_call x1, Pallas kernels: 2.96 us -> 0.88 us  [body(): pl.pallas_call(first_chain_kernel, out_shape=shape(16, 2, 8, 128), in_spe...]
  transfers between devices with their start and end apart: 5 -> 5, of which waited for: 4 -> 5; matrix products, arithmetic and copies ran while one was open for 2% -> 0% of each run, Pallas kernels for 0% -> 0%
where the time goes in v3:
time: 169 us; the launch traced here: 167 us
  blocking collectives  104 us (62%)
  waiting for transfers between devices  29.1 us (17%)
  starting transfers between devices  19.1 us (11%)
  Pallas kernels  10.1 us (6%)
  local copies, waits for them, and re-layouts  3.81 us (2%)
    all_gather x19, blocking collectives, gather(): return lax.all_gather(x, AX, axis=0, axis_index_groups=groups, tiled=False)  104 us
    ppermute x2, waiting for transfers between devices, send(): return lax.ppermute(jnp.concatenate(rows), AX, split_pairs(step))  18.5 us
    ppermute x1, starting transfers between devices, body(): hi = lax.ppermute(edge(pair[0:6], pair[6:8]), AX, z_pairs(-1))  9.5 us
    ppermute x1, waiting for transfers between devices, body(): lo = lax.ppermute(edge(pair[2:8], pair[0:2]), AX, z_pairs(1))  8.94 us
    pallas_call x6, Pallas kernels, body(): pl.pallas_call(chain_kernel, out_shape=(shape(32, 2, 8, 128), shape(16, 2...  5.4 us
    ppermute x2, starting transfers between devices, send(): return lax.ppermute(jnp.concatenate(rows), AX, split_pairs(step))  3.84 us
    ppermute x1, starting transfers between devices, body(): lo = lax.ppermute(edge(pair[2:8], pair[0:2]), AX, z_pairs(1))  3.83 us
    unnamed x22, local copies, waits for them, and re-layouts  3.41 us
  transfers between devices with their start and end apart: 5, of which 5 were waited for; matrix products, arithmetic and copies ran while one was open for 0% of the time, Pallas kernels for 0%

profile of v3, /device:TPU:6, one launch (start us, length us, event | category | flops | bytes accessed | tf_op | source)
XLA Modules:
  0.0 166.9 jit_solution(1473422224582985996)
XLA Ops:
  3.3 11.6 %all-gather.pair = f32[8,10,2,8,128]{4,3,2,1,0:T(8,128)S(1)} all-gather(f32[4,10,2,8,128]{4,3,2,1,0:T(8,128)S(1)} %pack.1), channel_id=2, replica_groups={{0,1},{32,33},{64,65},{96,97},{128,129},{160,161},{192,193},{224,225},{..., dimensions={0}, use_global_device_ids=true | all-gather | bytes 983040 | tf_op jit(solution)/shard_map/all_gather | solution.py:59
  15.1 3.8 %collective-permute-start = (f32[64,2,8,128]{3,2,1,0:T(8,128)S(1)}, f32[64,2,8,128]{3,2,1,0:T(8,128)S(1)}, u32[]{:S(2)}, u32[]{:S(2)}) collective-permute-start(f32[64,2,8,128]{3,2,1,0:T(8,128)S(1)} %pad_maximum_fusion), channel_id=1, source_target_pairs={{0,2},{32,34},{64,66},{96,98},{128,130},{160,162},{192,194},{224,2... | collective-permute-start | bytes 1572872 | tf_op jit(solution)/shard_map/ppermute | solution.py:413
  19.0 9.5 %collective-permute-start.1 = (f32[64,2,8,128]{3,2,1,0:T(8,128)S(1)}, f32[64,2,8,128]{3,2,1,0:T(8,128)S(1)}, u32[]{:S(2)}, u32[]{:S(2)}) collective-permute-start(f32[64,2,8,128]{3,2,1,0:T(8,128)S(1)} %pad_maximum_fusion.1), channel_id=1, source_target_pairs={{0,30},{32,62},{64,94},{96,126},{128,158},{160,190},{192,222},{224... | collective-permute-start | bytes 1572872 | tf_op jit(solution)/shard_map/ppermute | solution.py:414
  28.6 8.9 %collective-permute-done.lo = f32[64,2,8,128]{3,2,1,0:T(8,128)S(1)} collective-permute-done((f32[64,2,8,128]{3,2,1,0:T(8,128)S(1)}, f32[64,2,8,128]{3,2,1,0:T(8,128)S(1)}, u32[]{:S(2)}, u32[]{:S(2)}) %collective-permute-start) | collective-permute-done | bytes 524320 | tf_op jit(solution)/shard_map/ppermute | solution.py:413
  42.1 3.5 %all-gather.1 = f32[128,8,128]{2,1,0:T(8,128)S(1)} all-gather(f32[64,8,128]{2,1,0:T(8,128)S(1)} %pad_maximum_fusion.3), channel_id=3, replica_groups={{0,32},{64,96},{128,160},{192,224},{256,288},{320,352},{384,416},{448,4..., dimensions={0}, use_global_device_ids=true | all-gather | bytes 786432 | tf_op jit(solution)/shard_map/all_gather | solution.py:59
  48.1 7.5 %collective-permute-done.2 = f32[64,8,128]{2,1,0:T(8,128)S(1)} collective-permute-done((f32[64,8,128]{2,1,0:T(8,128)S(1)}, f32[64,8,128]{2,1,0:T(8,128)S(1)}, u32[]{:S(2)}, u32[]{:S(2)}) %collective-permute-start.2) | collective-permute-done | bytes 262176 | tf_op jit(solution)/shard_map/ppermute | solution.py:434
  57.6 3.0 %all-gather.3 = f32[128,8,128]{2,1,0:T(8,128)S(1)} all-gather(f32[64,8,128]{2,1,0:T(8,128)S(1)} %collective-permute-done.2), channel_id=5, replica_groups={{0,32},{64,96},{128,160},{192,224},{256,288},{320,352},{384,416},{448,4..., dimensions={0}, use_global_device_ids=true | all-gather | bytes 786432 | tf_op jit(solution)/shard_map/all_gather | solution.py:59
  60.7 11.0 %collective-permute-done.3 = f32[100,8,128]{2,1,0:T(8,128)S(1)} collective-permute-done((f32[100,8,128]{2,1,0:T(8,128)S(1)}, f32[100,8,128]{2,1,0:T(8,128)S(1)}, u32[]{:S(2)}, u32[]{:S(2)}) %collective-permute-start.3) | collective-permute-done | bytes 409632 | tf_op jit(solution)/shard_map/ppermute | solution.py:434
  71.7 2.1 %all-gather.2 = f32[104,8,128]{2,1,0:T(8,128)S(1)} all-gather(f32[52,8,128]{2,1,0:T(8,128)S(1)} %slice.240), channel_id=4, replica_groups={{0,32},{64,96},{128,160},{192,224},{256,288},{320,352},{384,416},{448,4..., dimensions={0}, use_global_device_ids=true | all-gather | bytes 638976 | tf_op jit(solution)/shard_map/all_gather | solution.py:59
  73.9 2.1 %all-gather.4 = f32[96,8,128]{2,1,0:T(8,128)S(1)} all-gather(f32[48,8,128]{2,1,0:T(8,128)S(1)} %slice.248), channel_id=6, replica_groups={{0,32},{64,96},{128,160},{192,224},{256,288},{320,352},{384,416},{448,4..., dimensions={0}, use_global_device_ids=true | all-gather | bytes 589824 | tf_op jit(solution)/shard_map/all_gather | solution.py:59
  77.2 8.3 %all-gather.5 = f32[32,2,8,128]{3,2,1,0:T(8,128)S(1)} all-gather(f32[16,2,8,128]{3,2,1,0:T(8,128)S(1)} %chain.7), channel_id=7, replica_groups={{0,68},{32,124},{128,196},{160,252},{256,324},{288,380},{384,452},{416,..., dimensions={0}, use_global_device_ids=true | all-gather | bytes 393216 | tf_op jit(solution)/shard_map/all_gather | solution.py:59
  85.5 2.1 %all-gather.12 = f32[32,2,8,128]{3,2,1,0:T(8,128)S(1)} all-gather(f32[16,2,8,128]{3,2,1,0:T(8,128)S(1)} %slice.260), channel_id=14, replica_groups={{0,32},{64,96},{128,160},{192,224},{256,288},{320,352},{384,416},{448,4..., dimensions={0}, use_global_device_ids=true | all-gather | bytes 393216 | tf_op jit(solution)/shard_map/all_gather | solution.py:59
  88.5 10.4 %all-gather.6 = f32[32,2,8,128]{3,2,1,0:T(8,128)S(1)} all-gather(f32[16,2,8,128]{3,2,1,0:T(8,128)S(1)} %get-tuple-element.22), channel_id=8, replica_groups={{64,132},{96,188},{192,260},{224,316},{320,388},{352,444},{448,4},{480,..., dimensions={0}, use_global_device_ids=true | all-gather | bytes 393216 | tf_op jit(solution)/shard_map/all_gather | solution.py:59
  98.9 2.0 %all-gather.13 = f32[32,2,8,128]{3,2,1,0:T(8,128)S(1)} all-gather(f32[16,2,8,128]{3,2,1,0:T(8,128)S(1)} %slice.261), channel_id=15, replica_groups={{0,32},{64,96},{128,160},{192,224},{256,288},{320,352},{384,416},{448,4..., dimensions={0}, use_global_device_ids=true | all-gather | bytes 393216 | tf_op jit(solution)/shard_map/all_gather | solution.py:59
  101.8 8.4 %all-gather.7 = f32[32,2,8,128]{3,2,1,0:T(8,128)S(1)} all-gather(f32[16,2,8,128]{3,2,1,0:T(8,128)S(1)} %get-tuple-element.24), channel_id=9, replica_groups={{0,68},{32,124},{128,196},{160,252},{256,324},{288,380},{384,452},{416,..., dimensions={0}, use_global_device_ids=true | all-gather | bytes 393216 | tf_op jit(solution)/shard_map/all_gather | solution.py:59
  113.2 10.8 %all-gather.8 = f32[32,2,8,128]{3,2,1,0:T(8,128)S(1)} all-gather(f32[16,2,8,128]{3,2,1,0:T(8,128)S(1)} %get-tuple-element.26), channel_id=10, replica_groups={{64,132},{96,188},{192,260},{224,316},{320,388},{352,444},{448,4},{480,..., dimensions={0}, use_global_device_ids=true | all-gather | bytes 393216 | tf_op jit(solution)/shard_map/all_gather | solution.py:59
  124.0 2.0 %all-gather.15 = f32[32,2,8,128]{3,2,1,0:T(8,128)S(1)} all-gather(f32[16,2,8,128]{3,2,1,0:T(8,128)S(1)} %slice.263), channel_id=17, replica_groups={{0,32},{64,96},{128,160},{192,224},{256,288},{320,352},{384,416},{448,4..., dimensions={0}, use_global_device_ids=true | all-gather | bytes 393216 | tf_op jit(solution)/shard_map/all_gather | solution.py:59
  126.9 8.2 %all-gather.9 = f32[32,2,8,128]{3,2,1,0:T(8,128)S(1)} all-gather(f32[16,2,8,128]{3,2,1,0:T(8,128)S(1)} %get-tuple-element.28), channel_id=11, replica_groups={{0,68},{32,124},{128,196},{160,252},{256,324},{288,380},{384,452},{416,..., dimensions={0}, use_global_device_ids=true | all-gather | bytes 393216 | tf_op jit(solution)/shard_map/all_gather | solution.py:59
  135.1 2.6 %all-gather.16 = f32[32,2,8,128]{3,2,1,0:T(8,128)S(1)} all-gather(f32[16,2,8,128]{3,2,1,0:T(8,128)S(1)} %slice.264), channel_id=18, replica_groups={{0,32},{64,96},{128,160},{192,224},{256,288},{320,352},{384,416},{448,4..., dimensions={0}, use_global_device_ids=true | all-gather | bytes 393216 | tf_op jit(solution)/shard_map/all_gather | solution.py:59
  138.6 10.3 %all-gather.10 = f32[32,2,8,128]{3,2,1,0:T(8,128)S(1)} all-gather(f32[16,2,8,128]{3,2,1,0:T(8,128)S(1)} %get-tuple-element.30), channel_id=12, replica_groups={{64,132},{96,188},{192,260},{224,316},{320,388},{352,444},{448,4},{480,..., dimensions={0}, use_global_device_ids=true | all-gather | bytes 393216 | tf_op jit(solution)/shard_map/all_gather | solution.py:59
  148.9 2.0 %all-gather.17 = f32[32,2,8,128]{3,2,1,0:T(8,128)S(1)} all-gather(f32[16,2,8,128]{3,2,1,0:T(8,128)S(1)} %slice.265), channel_id=19, replica_groups={{0,32},{64,96},{128,160},{192,224},{256,288},{320,352},{384,416},{448,4..., dimensions={0}, use_global_device_ids=true | all-gather | bytes 393216 | tf_op jit(solution)/shard_map/all_gather | solution.py:59
  151.8 8.9 %all-gather.11 = f32[32,2,8,128]{3,2,1,0:T(8,128)S(1)} all-gather(f32[16,2,8,128]{3,2,1,0:T(8,128)S(1)} %get-tuple-element.32), channel_id=13, replica_groups={{0,68},{32,124},{128,196},{160,252},{256,324},{288,380},{384,452},{416,..., dimensions={0}, use_global_device_ids=true | all-gather | bytes 393216 | tf_op jit(solution)/shard_map/all_gather | solution.py:59
  160.6 3.8 %all-gather.18 = f32[32,2,8,128]{3,2,1,0:T(8,128)S(1)} all-gather(f32[16,2,8,128]{3,2,1,0:T(8,128)S(1)} %slice.266), channel_id=20, replica_groups={{0,32},{64,96},{128,160},{192,224},{256,288},{320,352},{384,416},{448,4..., dimensions={0}, use_global_device_ids=true | all-gather | bytes 393216 | tf_op jit(solution)/shard_map/all_gather | solution.py:59
  164.4 2.5 %last.1 = f32[1,3,2,4,16,128]{5,4,3,2,1,0:T(8,128)} custom-call(s32[3]{0:T(128)S(1)} %pad_add_fusion.sc, f32[2,16,2,8,128]{4,3,2,1,0:T(8,128)S(1)} %bitcast.46, f32[32,2,8,128]{3,2,1,0:T(8,128)S(1)} %get-tuple-element.33.a_in, f32[28,6,8,128]{3,2,1,0:T(8,128)S(1)} %get-tuple-element.60.pa, f32[20,6,8,128]{3,2,1,0:T(8,128)S(1)} %get-tuple-element.61.pb, ...), custom_call_target="tpu_custom_call" | custom-call | tf_op jit(solution)/shard_map/last/pallas_call | solution.py:478
  (71 shorter events, 21.2 us)
Async XLA Ops:
  0.0 0.9 copy-start
  0.9 0.8 copy-start.1
  1.8 0.8 copy-start.2
  2.5 0.8 copy-start.3
  15.1 22.5 %collective-permute-start = (f32[64,2,8,128]{3,2,1,0:T(8,128)S(1)}, f32[64,2,8,128]{3,2,1,0:T(8,128)S(1)}, u32[]{:S(2)}, u32[]{:S(2)}) collective-permute-start(f32[64,2,8,128]{3,2,1,0:T(8,128)S(1)} %pad_maximum_fusion), channel_id=1, source_target_pairs={{0,2},{32,34},{64,66},{96,98},{128,130},{160,162},{192,194},{224,2... | collective-permute-start | bytes 1572872 | tf_op jit(solution)/shard_map/ppermute | solution.py:413
  19.0 19.8 %collective-permute-start.1 = (f32[64,2,8,128]{3,2,1,0:T(8,128)S(1)}, f32[64,2,8,128]{3,2,1,0:T(8,128)S(1)}, u32[]{:S(2)}, u32[]{:S(2)}) collective-permute-start(f32[64,2,8,128]{3,2,1,0:T(8,128)S(1)} %pad_maximum_fusion.1), channel_id=1, source_target_pairs={{0,30},{32,62},{64,94},{96,126},{128,158},{160,190},{192,222},{224... | collective-permute-start | bytes 1572872 | tf_op jit(solution)/shard_map/ppermute | solution.py:414
  40.2 7.9 %collective-permute-start.4 = (f32[12,2,2,8,128]{4,3,2,1,0:T(8,128)S(1)}, f32[12,2,2,8,128]{4,3,2,1,0:T(8,128)S(1)}, u32[]{:S(2)}, u32[]{:S(2)}) collective-permute-start(f32[12,2,2,8,128]{4,3,2,1,0:T(8,128)S(1)} %constant_dynamic-slice_fusion), channel_id=1, source_target_pairs={{0,32},{1,33},{2,34},{3,35},{4,36},{5,37},{6,38},{7,39},{8,40},{9,... | collective-permute-start | bytes 589832 | tf_op jit(solution)/shard_map/ppermute | solution.py:425
  45.7 9.9 %collective-permute-start.2 = (f32[64,8,128]{2,1,0:T(8,128)S(1)}, f32[64,8,128]{2,1,0:T(8,128)S(1)}, u32[]{:S(2)}, u32[]{:S(2)}) collective-permute-start(f32[64,8,128]{2,1,0:T(8,128)S(1)} %pad_maximum_fusion.4), channel_id=1, source_target_pairs={{0,2},{32,62},{64,66},{96,126},{128,130},{160,190},{192,194},{224,... | collective-permute-start | bytes 786440 | tf_op jit(solution)/shard_map/ppermute | solution.py:434
  55.7 16.0 %collective-permute-start.3 = (f32[100,8,128]{2,1,0:T(8,128)S(1)}, f32[100,8,128]{2,1,0:T(8,128)S(1)}, u32[]{:S(2)}, u32[]{:S(2)}) collective-permute-start(f32[100,8,128]{2,1,0:T(8,128)S(1)} %pad_maximum_fusion.2), channel_id=1, source_target_pairs={{0,4},{32,60},{64,68},{96,124},{128,132},{160,188},{192,196},{224,... | collective-permute-start | bytes 1228808 | tf_op jit(solution)/shard_map/ppermute | solution.py:434

commit v4 on v3

--- a/solution.py
+++ b/solution.py
@@ -4,6 +4,7 @@
 from jax.experimental import pallas as pl
 from jax.experimental.pallas import tpu as pltpu
 from jax.sharding import PartitionSpec as P
+
 
 AX = ("tm", "slab")
 F32 = jnp.float32
@@ -47,12 +48,9 @@
     return [(t * 32 + s, (t + 1) * 32 + s) for t in range(15) for s in range(32)]
 
 
-def turn_groups(parity):
-    groups = []
-    for z, h, c, k in everyone():
-        if c % 2 == parity:
-            groups.append([flat(z, h, c, k), flat(z + (2 if k == 0 else -2), h, (c + 1) % 8, k)])
-    return groups
+def turn_pairs(turn):
+    return [(flat(z, h, turn, k), flat(z + (2 if k == 0 else -2), h, turn + 1, k))
+            for z in range(16) for h in range(2) for k in range(2)]
 
 
 def gather(x, groups):
@@ -127,7 +125,7 @@
     return start + (5.0 / 12.0 - 1.0) * w[0] + (2.0 / 3.0) * w[1] - (1.0 / 12.0) * w[2]
 
 
-def sweep_kernel(pair, lo, hi, big, unit, aux, v1, v2, b2, xs, xp, cs):
+def sweep_kernel(pair, lo, hi, big, unit, start, rates, v1, v2, b2, xs, xp, cs):
     segs = ((lo, 2, 6), (pair, 8, 8), (hi, 16, 6))
 
     def raw(ref, i, f):
@@ -149,6 +147,7 @@
                 start = raw(ref, i, 6 + s)
                 v1[pl.ds(base + i, 2), s] = first_combo(w, start)
             return 0
+
         unrolled(count // 2, load_v1)
 
     for ref, base, count in segs:
@@ -185,6 +184,7 @@
             b2[at, 1] = nv + gq - fk * qv
             b2[at, 2] = g[2]
             return 0
+
         unrolled(count // 2, node_one)
 
     def node_two(n, _):
@@ -196,6 +196,7 @@
         big[at, 4] = nu
         big[at, 5] = nv
         return 0
+
     unrolled(8, node_two)
 
     def integrals(n, _):
@@ -213,6 +214,7 @@
             xp[to, 2 * m] = f - f * xu - gx
             xp[to, 2 * m + 1] = gx - fk * xv
         return 0
+
     unrolled(6, integrals)
 
     def restrict(x):
@@ -226,11 +228,12 @@
         k = restrict(big[at, 7])
         cs[n, 6] = f
         cs[n, 7] = k
-        aux[n, 0] = cs[n, 0]
-        aux[n, 1] = cs[n, 1]
-        aux[n, 2] = 1.0 / (1.0 + f)
-        aux[n, 3] = 1.0 / (1.0 + k)
+        start[n, 0] = cs[n, 0]
+        start[n, 1] = cs[n, 1]
+        rates[n, 0] = 1.0 / (1.0 + f)
+        rates[n, 1] = 1.0 / (1.0 + k)
         return 0
+
     unrolled(10, coarsen)
 
     def make_unit(n, _):
@@ -245,33 +248,35 @@
                     val = val + f * cu + g
                 else:
                     val = val - g + fk * cv
-                unit[n, 3 * m + s] = val
-            unit[n, 3 * m + 2] = g
+                unit[m, n, s] = val
+            unit[m, n, 2] = g
         return 0
+
     unrolled(4, make_unit)
 
 
-def coarse_node(src, src_off, prm, prm_off, m, rates, rate_off, dst, dst_off, count):
+def coarse_node(src, prm, rates, rate_off, dst, count):
     def step(n, _):
         i = 4 * n
-        at = pl.ds(prm_off + i, 4)
+        at = pl.ds(i, 4)
         ra = pl.ds(rate_off + i, 4)
-        wu = src[pl.ds(src_off + i, 8), 0]
-        wv = src[pl.ds(src_off + i, 8), 1]
-        bu = wu[2:6] + coarse_lap(wu, DIFF[0]) + prm[at, 3 * m]
-        bv = wv[2:6] + coarse_lap(wv, DIFF[1]) + prm[at, 3 * m + 1]
-        nu, nv = solve(bu, bv, prm[at, 3 * m + 2], rates[ra, 2], rates[ra, 3])
-        dst[pl.ds(dst_off + i, 4), 0] = nu
-        dst[pl.ds(dst_off + i, 4), 1] = nv
-        return 0
+        wu = src[pl.ds(i, 8), 0]
+        wv = src[pl.ds(i, 8), 1]
+        bu = wu[2:6] + coarse_lap(wu, DIFF[0]) + prm[at, 0]
+        bv = wv[2:6] + coarse_lap(wv, DIFF[1]) + prm[at, 1]
+        nu, nv = solve(bu, bv, prm[at, 2], rates[ra, 0], rates[ra, 1])
+        dst[at, 0] = nu
+        dst[at, 1] = nv
+
     unrolled(count // 4, step)
 
 
-def two_slices(a, pa, pb, aux, n1, n2, n3, out):
-    coarse_node(a, 0, pa, 0, 0, aux, 2, n1, 0, 28)
-    coarse_node(n1, 0, pa, 2, 1, aux, 4, n2, 0, 24)
-    coarse_node(n2, 0, pb, 0, 0, aux, 6, n3, 0, 20)
-    coarse_node(n3, 0, pb, 2, 1, aux, 8, out, 0, 16)
+def two_slices(a, prm, n1, n2, n3, out):
+    p1a, p2a, p1b, p2b, rates = prm
+    coarse_node(a, p1a, rates, 0, n1, 28)
+    coarse_node(n1, p2a, rates, 2, n2, 24)
+    coarse_node(n2, p1b, rates, 4, n3, 20)
+    coarse_node(n3, p2b, rates, 6, out, 16)
 
 
 def take(flag, moved, a_in, a):
@@ -285,18 +290,18 @@
         a[...] = a_in[...]
 
 
-def first_chain_kernel(a, pa, pb, aux, out, n1, n2, n3):
-    two_slices(a, pa, pb, aux, n1, n2, n3, out)
-
-
-def chain_kernel(sc, moved, a_in, pa, pb, aux, a, out, n1, n2, n3):
+def first_chain_kernel(a, p1a, p2a, p1b, p2b, rates, out, n1, n2, n3):
+    two_slices(a, (p1a, p2a, p1b, p2b, rates), n1, n2, n3, out)
+
+
+def chain_kernel(sc, moved, a_in, p1a, p2a, p1b, p2b, rates, a, out, n1, n2, n3):
     take(sc[0], moved, a_in, a)
-    two_slices(a, pa, pb, aux, n1, n2, n3, out)
-
-
-def last_kernel(sc, moved, a_in, pa, pb, aux, big, prev, res, a, n1, n2, n3, n4, gs, v1, tp):
+    two_slices(a, (p1a, p2a, p1b, p2b, rates), n1, n2, n3, out)
+
+
+def last_kernel(sc, moved, a_in, p1a, p2a, p1b, p2b, rates, big, prev, res, a, n1, n2, n3, n4, gs, v1, tp):
     take(sc[0], moved, a_in, a)
-    two_slices(a, pa, pb, aux, n1, n2, n3, n4)
+    two_slices(a, (p1a, p2a, p1b, p2b, rates), n1, n2, n3, n4)
     core = sc[1]
     yh = sc[2]
 
@@ -347,6 +352,7 @@
         tp[to, 8] = bu
         tp[to, 9] = bv
         return 0
+
     unrolled(6, update)
 
     def put(node, s, plane, x):
@@ -367,6 +373,7 @@
         tp[at, 10] = nu
         tp[at, 11] = nv
         return 0
+
     unrolled(4, node_one)
 
     for n in range(2):
@@ -393,7 +400,7 @@
     return jax.ShapeDtypeStruct(dims, F32)
 
 
-def body(node_values, start_state, feed_rate, kill_rate):
+def program(node_values, start_state, feed_rate, kill_rate):
     t = lax.axis_index("tm")
     core = t % 2
     chip = t // 2
@@ -401,7 +408,7 @@
     left = core == 0
     own = pl.pallas_call(
         pack_kernel, out_shape=shape(4, 10, 2, 8, 128), in_specs=[VM] * 4, out_specs=VM,
-        name="pack", compiler_params=SMALL,
+        name="pack",
     )(node_values, start_state, feed_rate, kill_rate)
     pair = gather(own, pair_groups()).reshape(8, 10, 2, 8, 128)
 
@@ -412,80 +419,92 @@
 
     lo = lax.ppermute(edge(pair[2:8], pair[0:2]), AX, z_pairs(1))
     hi = lax.ppermute(edge(pair[0:6], pair[6:8]), AX, z_pairs(-1))
-    big, unit, aux = pl.pallas_call(
+    big, unit, start, rates = pl.pallas_call(
         sweep_kernel,
-        out_shape=(shape(20, 10, 2, 8, 128), shape(4, 6, 8, 128), shape(10, 4, 8, 128)),
-        in_specs=[VM] * 3, out_specs=(VM, VM, VM),
+        out_shape=(shape(20, 10, 2, 8, 128), shape(2, 4, 3, 8, 128), shape(10, 2, 8, 128),
+                   shape(10, 2, 8, 128)),
+        in_specs=[VM] * 3, out_specs=(VM, VM, VM, VM),
         scratch_shapes=[vmem(24, 2, 2, 8, 128), vmem(20, 2, 2, 8, 128), vmem(20, 3, 2, 8, 128),
                         vmem(12, 4, 2, 8, 128), vmem(12, 4, 2, 8, 128), vmem(10, 8, 8, 128)],
         name="sweep", compiler_params=SMALL,
     )(pair, lo, hi)
 
+    def rows(parts):
+        return jnp.concatenate([x.reshape(-1, 8, 128) for x in parts])
+
+    both = gather(rows([unit, start]), core_groups())
+    units = both[:, :24].reshape(2, 2, 4, 3, 8, 128)
+    start = both[0, 24:].reshape(10, 2, 8, 128)
+    (p1a, p2a), (p1b, p2b) = units
+
+    def near_planes(x, n):
+        return jnp.where(left, x[4 - n:], x[:n])
+
+    def send(parts, step):
+        message = rows(parts)
+        return lax.ppermute(message, AX, split_pairs(step))
+
+    start4 = jnp.where(left, start[0:4], start[6:10])
+    rates4 = jnp.where(left, rates[0:4], rates[6:10])
+    near = send([p1a, p2a, p1b, p2b, start4, rates4], 1)
+    mid = send([p1a, p2a, p1b, near_planes(p2b, 2), start4, rates4], 2)
+    far = send([p1a, near_planes(p2a, 2), jnp.where(left, start[1:4], start[6:9]),
+                jnp.where(left, rates[3:4], rates[6:7])], 3)
+    nears = gather(near, core_groups())
+    fars = gather(jnp.concatenate([mid, far]), core_groups())
+
+    def pick(part, side, first, planes, fields):
+        return part[side, first:first + planes * fields].reshape(planes, fields, 8, 128)
+
+    def window(own, *pieces):
+        below = [pick(part, 0, first, planes, own.shape[1]) for part, first, planes in pieces]
+        above = [pick(part, 1, first, planes, own.shape[1]) for part, first, planes in pieces]
+        return jnp.concatenate(below[::-1] + [own] + above)
+
+    p1a = window(p1a, (nears, 0, 4), (fars, 0, 4), (fars, 58, 4))
+    p2a = window(p2a, (nears, 12, 4), (fars, 12, 4), (fars, 70, 2))
+    p1b = window(p1b, (nears, 24, 4), (fars, 24, 4))
+    p2b = window(p2b, (nears, 36, 4), (fars, 36, 2))
+    state = window(start, (nears, 48, 4), (fars, 42, 4), (fars, 76, 3))
+    rates = window(rates, (nears, 56, 4), (fars, 50, 4), (fars, 82, 1))
+    prm = (p1a, p2a, p1b, p2b, rates)
+
     mine = lax.dynamic_slice_in_dim(big, 2 + 4 * yh, 12, 0)
     prev = lax.ppermute(mine[:, 4:6], AX, slice_pairs())
     prev = jnp.where(t == 0, mine[:, 0:2], prev)
 
-    both = gather(jnp.concatenate([unit.reshape(24, 8, 128), aux.reshape(40, 8, 128)]), core_groups())
-    units = both[:, :24].reshape(2, 4, 6, 8, 128)
-    aux = both[0, 24:].reshape(10, 4, 8, 128)
-
-    def send(parts, step):
-        rows = [x.reshape(-1, 8, 128) for x in parts]
-        return lax.ppermute(jnp.concatenate(rows), AX, split_pairs(step))
-
-    got1 = send([units, jnp.where(left, aux[0:4], aux[6:10])], 1)
-    aux1 = got1[48:].reshape(4, 4, 8, 128)
-    got2 = send([units, got1[0:24],
-                 jnp.where(left, jnp.concatenate([aux1[1:4], aux[0:4]]),
-                           jnp.concatenate([aux[6:10], aux1[0:3]]))], 2)
-    near = gather(got1, core_groups())
-    far = gather(got2[:48], core_groups())
-    edge2 = gather(got2[48:], core_groups())
-
-    def pick(rows, side, start, planes, fields):
-        return rows[side, start:start + planes * fields].reshape(planes, fields, 8, 128)
-
-    pa = jnp.concatenate([pick(edge2, 0, 0, 4, 6), pick(far, 0, 0, 4, 6), pick(near, 0, 0, 4, 6), units[0],
-                          pick(near, 1, 0, 4, 6), pick(far, 1, 0, 4, 6), pick(edge2, 1, 0, 4, 6)])
-    pb = jnp.concatenate([pick(far, 0, 24, 4, 6), pick(near, 0, 24, 4, 6), units[1],
-                          pick(near, 1, 24, 4, 6), pick(far, 1, 24, 4, 6)])
-    aux = jnp.concatenate([pick(edge2, 0, 24, 7, 4), pick(near, 0, 48, 4, 4), aux,
-                           pick(near, 1, 48, 4, 4), pick(edge2, 1, 24, 7, 4)])
-    state = aux[:, 0:2]
-
     scratch = [vmem(28, 2, 8, 128), vmem(24, 2, 8, 128), vmem(20, 2, 8, 128)]
 
     def exchange(out, turn):
-        moved = gather(out, turn_groups(turn % 2))[0]
+        moved = lax.ppermute(out, AX, turn_pairs(turn))
         moved = gather(moved, core_groups())
-        takes = jnp.logical_and(chip % 2 == (turn + 1) % 2, chip > 0)
-        return moved, takes.astype(jnp.int32)
+        return moved, (chip == turn + 1).astype(jnp.int32)
 
     out = pl.pallas_call(
-        first_chain_kernel, out_shape=shape(16, 2, 8, 128), in_specs=[VM] * 4, out_specs=VM,
+        first_chain_kernel, out_shape=shape(16, 2, 8, 128), in_specs=[VM] * 6, out_specs=VM,
         scratch_shapes=scratch, name="chain", compiler_params=SMALL,
-    )(state, pa, pb, aux)
+    )(state, *prm)
     for turn in range(6):
         moved, takes = exchange(out, turn)
         state, out = pl.pallas_call(
             chain_kernel, out_shape=(shape(32, 2, 8, 128), shape(16, 2, 8, 128)),
-            in_specs=[SM] + [VM] * 5, out_specs=(VM, VM),
+            in_specs=[SM] + [VM] * 7, out_specs=(VM, VM),
             scratch_shapes=scratch, name="chain", compiler_params=SMALL,
-        )(takes.reshape(1), moved, state, pa, pb, aux)
+        )(takes.reshape(1), moved, state, *prm)
     moved, takes = exchange(out, 6)
 
     scalars = jnp.stack([takes, core, yh]).astype(jnp.int32)
     return pl.pallas_call(
-        last_kernel, out_shape=shape(1, 3, 2, 4, 16, 128), in_specs=[SM] + [VM] * 7, out_specs=VM,
-        scratch_shapes=[vmem(32, 2, 8, 128)] + scratch + [vmem(16, 2, 8, 128), vmem(8, 6, 8, 128),
-                                  vmem(12, 2, 2, 8, 128), vmem(12, 12, 2, 8, 128)],
+        last_kernel, out_shape=shape(1, 3, 2, 4, 16, 128), in_specs=[SM] + [VM] * 9, out_specs=VM,
+        scratch_shapes=[vmem(32, 2, 8, 128)] + scratch + [
+            vmem(16, 2, 8, 128), vmem(8, 6, 8, 128), vmem(12, 2, 2, 8, 128), vmem(12, 12, 2, 8, 128)],
         name="last", compiler_params=SMALL,
-    )(scalars, moved, state, pa, pb, aux, big, prev)
+    )(scalars, moved, state, *prm, big, prev)
 
 
 def solution(mesh):
     return jax.shard_map(
-        body,
+        program,
         mesh=mesh,
         in_specs=(
             P("tm", None, None, "slab", None, None),

time: 169 us -> 149 us (0.88)
  the two profiles are of different devices: /device:TPU:6 before, /device:TPU:63 now
where the time goes in v4:
time: 149 us
  waiting for transfers between devices  62.7 us (42%)
  blocking collectives  38.3 us (26%)
  starting transfers between devices  30.8 us (21%)
  Pallas kernels  14.7 us (10%)
    ppermute x7, waiting for transfers between devices, exchange(): moved = lax.ppermute(out, AX, turn_pairs(turn))  48.7 us
    all_gather x11, blocking collectives, gather(): return lax.all_gather(x, AX, axis=0, axis_index_groups=groups, tiled=False)  38.3 us
    ppermute x3, starting transfers between devices, send(): return lax.ppermute(message, AX, split_pairs(step))  18.2 us
    pallas_call x6, Pallas kernels, program(): pl.pallas_call(chain_kernel, out_shape=(shape(32, 2, 8, 128), shape(16, 2...  8.42 us
    ppermute x1, waiting for transfers between devices, program(): lo = lax.ppermute(edge(pair[2:8], pair[0:2]), AX, z_pairs(1))  8.3 us
    ppermute x7, starting transfers between devices, exchange(): moved = lax.ppermute(out, AX, turn_pairs(turn))  5.89 us
    ppermute x1, waiting for transfers between devices, program(): hi = lax.ppermute(edge(pair[0:6], pair[6:8]), AX, z_pairs(-1))  3.68 us
    ppermute x1, starting transfers between devices, program(): lo = lax.ppermute(edge(pair[2:8], pair[0:2]), AX, z_pairs(1))  3.55 us
  transfers between devices with their start and end apart: 13, of which 4 were waited for; matrix products, arithmetic and copies ran while one was open for 1% of the time, Pallas kernels for 1%

profile of v4, /device:TPU:63, one launch (start us, length us, event | category | flops | bytes accessed | tf_op | source)
XLA Modules:
  0.0 148.9 jit_solution(9343965576723223647)
XLA Ops:
  0.0 1.7 %pack.1 = f32[4,10,2,8,128]{4,3,2,1,0:T(8,128)} custom-call(f32[1,3,2,4,16,128]{5,4,3,2,1,0:T(8,128)} %nv.1, f32[1,2,4,16,128]{4,3,2,1,0:T(8,128)} %st.1, f32[4,16,128]{2,1,0:T(8,128)} %fr.1, f32[4,16,128]{2,1,0:T(8,128)} %kr.1), custom_call_target="tpu_custom_call" | custom-call | tf_op jit(solution)/shard_map/pack/pallas_call | solution.py:409
  1.7 11.0 %all-gather.pair = f32[8,10,2,8,128]{4,3,2,1,0:T(8,128)S(1)} all-gather(f32[4,10,2,8,128]{4,3,2,1,0:T(8,128)} %pack.1), channel_id=2, replica_groups={{0,1},{32,33},{64,65},{96,97},{128,129},{160,161},{192,193},{224,225},{..., dimensions={0}, use_global_device_ids=true | all-gather | bytes 983040 | tf_op jit(solution)/shard_map/all_gather | solution.py:57
  12.8 3.5 %collective-permute-start = (f32[64,2,8,128]{3,2,1,0:T(8,128)S(1)}, f32[64,2,8,128]{3,2,1,0:T(8,128)S(1)}, u32[]{:S(2)}, u32[]{:S(2)}) collective-permute-start(f32[64,2,8,128]{3,2,1,0:T(8,128)S(1)} %pad_maximum_fusion), channel_id=1, source_target_pairs={{0,2},{32,34},{64,66},{96,98},{128,130},{160,162},{192,194},{224,2... | collective-permute-start | bytes 1572872 | tf_op jit(solution)/shard_map/ppermute | solution.py:420
  16.4 1.9 %collective-permute-start.1 = (f32[64,2,8,128]{3,2,1,0:T(8,128)S(1)}, f32[64,2,8,128]{3,2,1,0:T(8,128)S(1)}, u32[]{:S(2)}, u32[]{:S(2)}) collective-permute-start(f32[64,2,8,128]{3,2,1,0:T(8,128)S(1)} %pad_maximum_fusion.1), channel_id=1, source_target_pairs={{0,30},{32,62},{64,94},{96,126},{128,158},{160,190},{192,222},{224... | collective-permute-start | bytes 1572872 | tf_op jit(solution)/shard_map/ppermute | solution.py:421
  18.4 8.3 %collective-permute-done.lo = f32[64,2,8,128]{3,2,1,0:T(8,128)S(1)} collective-permute-done((f32[64,2,8,128]{3,2,1,0:T(8,128)S(1)}, f32[64,2,8,128]{3,2,1,0:T(8,128)S(1)}, u32[]{:S(2)}, u32[]{:S(2)}) %collective-permute-start) | collective-permute-done | bytes 524320 | tf_op jit(solution)/shard_map/ppermute | solution.py:420
  26.7 3.7 %collective-permute-done.1.hi = f32[64,2,8,128]{3,2,1,0:T(8,128)S(1)} collective-permute-done((f32[64,2,8,128]{3,2,1,0:T(8,128)S(1)}, f32[64,2,8,128]{3,2,1,0:T(8,128)S(1)}, u32[]{:S(2)}, u32[]{:S(2)}) %collective-permute-start.1) | collective-permute-done | bytes 524320 | tf_op jit(solution)/shard_map/ppermute | solution.py:421
  31.7 4.2 %all-gather.1 = f32[88,8,128]{2,1,0:T(8,128)S(1)} all-gather(f32[44,8,128]{2,1,0:T(8,128)S(1)} %pad_maximum_fusion.3), channel_id=3, replica_groups={{0,32},{64,96},{128,160},{192,224},{256,288},{320,352},{384,416},{448,4..., dimensions={0}, use_global_device_ids=true | all-gather | bytes 540672 | tf_op jit(solution)/shard_map/all_gather | solution.py:57
  36.0 10.1 %collective-permute-start.2 = (f32[58,8,128]{2,1,0:T(8,128)S(1)}, f32[58,8,128]{2,1,0:T(8,128)S(1)}, u32[]{:S(2)}, u32[]{:S(2)}) collective-permute-start(f32[58,8,128]{2,1,0:T(8,128)S(1)} %get-tuple-element.83), channel_id=1, source_target_pairs={{0,4},{32,60},{64,68},{96,124},{128,132},{160,188},{192,196},{224,... | collective-permute-start | bytes 712712 | tf_op jit(solution)/shard_map/ppermute | solution.py:445
  46.2 3.0 %collective-permute-start.3 = (f32[26,8,128]{2,1,0:T(8,128)S(1)}, f32[26,8,128]{2,1,0:T(8,128)S(1)}, u32[]{:S(2)}, u32[]{:S(2)}) collective-permute-start(f32[26,8,128]{2,1,0:T(8,128)S(1)} %pad_maximum_fusion.4), channel_id=1, source_target_pairs={{0,6},{32,58},{64,70},{96,122},{128,134},{160,186},{192,198},{224,... | collective-permute-start | bytes 319496 | tf_op jit(solution)/shard_map/ppermute | solution.py:445
  49.2 5.1 %collective-permute-start.4 = (f32[64,8,128]{2,1,0:T(8,128)S(1)}, f32[64,8,128]{2,1,0:T(8,128)S(1)}, u32[]{:S(2)}, u32[]{:S(2)}) collective-permute-start(f32[64,8,128]{2,1,0:T(8,128)S(1)} %get-tuple-element.82), channel_id=1, source_target_pairs={{0,2},{32,62},{64,66},{96,126},{128,130},{160,190},{192,194},{224,... | collective-permute-start | bytes 786440 | tf_op jit(solution)/shard_map/ppermute | solution.py:445
  54.3 1.9 %collective-permute-done.3 = f32[26,8,128]{2,1,0:T(8,128)S(1)} collective-permute-done((f32[26,8,128]{2,1,0:T(8,128)S(1)}, f32[26,8,128]{2,1,0:T(8,128)S(1)}, u32[]{:S(2)}, u32[]{:S(2)}) %collective-permute-start.3) | collective-permute-done | bytes 106528 | tf_op jit(solution)/shard_map/ppermute | solution.py:445
  56.2 3.7 %all-gather.2 = f32[168,8,128]{2,1,0:T(8,128)S(1)} all-gather(f32[84,8,128]{2,1,0:T(8,128)S(1)} %pad_maximum_fusion.2), channel_id=4, replica_groups={{0,32},{64,96},{128,160},{192,224},{256,288},{320,352},{384,416},{448,4..., dimensions={0}, use_global_device_ids=true | all-gather | bytes 1032192 | tf_op jit(solution)/shard_map/all_gather | solution.py:57
  60.1 2.2 %all-gather.3 = f32[128,8,128]{2,1,0:T(8,128)S(1)} all-gather(f32[64,8,128]{2,1,0:T(8,128)S(1)} %collective-permute-done.4), channel_id=5, replica_groups={{0,32},{64,96},{128,160},{192,224},{256,288},{320,352},{384,416},{448,4..., dimensions={0}, use_global_device_ids=true | all-gather | bytes 786432 | tf_op jit(solution)/shard_map/all_gather | solution.py:57
  64.3 2.0 %all-gather.4 = f32[32,2,8,128]{3,2,1,0:T(8,128)S(1)} all-gather(f32[16,2,8,128]{3,2,1,0:T(8,128)S(1)} %collective-permute-done.5), channel_id=6, replica_groups={{0,32},{64,96},{128,160},{192,224},{256,288},{320,352},{384,416},{448,4..., dimensions={0}, use_global_device_ids=true | all-gather | bytes 393216 | tf_op jit(solution)/shard_map/all_gather | solution.py:57
  66.3 1.5 %chain.8 = (f32[32,2,8,128]{3,2,1,0:T(8,128)S(1)}, f32[16,2,8,128]{3,2,1,0:T(8,128)}) custom-call(s32[1]{0:T(128)} %bitcast.8.sc, f32[2,16,2,8,128]{4,3,2,1,0:T(8,128)S(1)} %bitcast.95, f32[32,2,8,128]{3,2,1,0:T(8,128)S(1)} %constant_dynamic-update-slice_fusion.12.a.a_in, f32[28,3,8,128]{3,2,1,0:T(8,128)S(1)} %get-tuple-element.84.p1a, ...), custom_call_target="tpu_custom_call" | custom-call | tf_op jit(solution)/shard_map/chain/pallas_call | solution.py:489
  68.5 2.0 %all-gather.5 = f32[32,2,8,128]{3,2,1,0:T(8,128)S(1)} all-gather(f32[16,2,8,128]{3,2,1,0:T(8,128)S(1)} %collective-permute-done.6), channel_id=7, replica_groups={{0,32},{64,96},{128,160},{192,224},{256,288},{320,352},{384,416},{448,4..., dimensions={0}, use_global_device_ids=true | all-gather | bytes 393216 | tf_op jit(solution)/shard_map/all_gather | solution.py:57
  70.5 1.5 %chain.9 = (f32[32,2,8,128]{3,2,1,0:T(8,128)S(1)}, f32[16,2,8,128]{3,2,1,0:T(8,128)}) custom-call(s32[1]{0:T(128)} %bitcast.7.sc, f32[2,16,2,8,128]{4,3,2,1,0:T(8,128)S(1)} %bitcast.90, f32[32,2,8,128]{3,2,1,0:T(8,128)S(1)} %get-tuple-element.25.a_in, f32[28,3,8,128]{3,2,1,0:T(8,128)S(1)} %get-tuple-element.84.p1a, ...), custom_call_target="tpu_custom_call" | custom-call | tf_op jit(solution)/shard_map/chain/pallas_call | solution.py:489
  72.7 2.0 %all-gather.6 = f32[32,2,8,128]{3,2,1,0:T(8,128)S(1)} all-gather(f32[16,2,8,128]{3,2,1,0:T(8,128)S(1)} %collective-permute-done.7), channel_id=8, replica_groups={{0,32},{64,96},{128,160},{192,224},{256,288},{320,352},{384,416},{448,4..., dimensions={0}, use_global_device_ids=true | all-gather | bytes 393216 | tf_op jit(solution)/shard_map/all_gather | solution.py:57
  76.8 2.0 %all-gather.7 = f32[32,2,8,128]{3,2,1,0:T(8,128)S(1)} all-gather(f32[16,2,8,128]{3,2,1,0:T(8,128)S(1)} %collective-permute-done.8), channel_id=9, replica_groups={{0,32},{64,96},{128,160},{192,224},{256,288},{320,352},{384,416},{448,4..., dimensions={0}, use_global_device_ids=true | all-gather | bytes 393216 | tf_op jit(solution)/shard_map/all_gather | solution.py:57
  81.0 2.0 %all-gather.8 = f32[32,2,8,128]{3,2,1,0:T(8,128)S(1)} all-gather(f32[16,2,8,128]{3,2,1,0:T(8,128)S(1)} %collective-permute-done.9), channel_id=10, replica_groups={{0,32},{64,96},{128,160},{192,224},{256,288},{320,352},{384,416},{448,4..., dimensions={0}, use_global_device_ids=true | all-gather | bytes 393216 | tf_op jit(solution)/shard_map/all_gather | solution.py:57
  87.3 3.0 %all-gather.9 = f32[32,2,8,128]{3,2,1,0:T(8,128)S(1)} all-gather(f32[16,2,8,128]{3,2,1,0:T(8,128)} %collective-permute-done.10), channel_id=11, replica_groups={{0,32},{64,96},{128,160},{192,224},{256,288},{320,352},{384,416},{448,4..., dimensions={0}, use_global_device_ids=true | all-gather | bytes 393216 | tf_op jit(solution)/shard_map/all_gather | solution.py:57
  93.4 48.7 %collective-permute-done.11 = f32[16,2,8,128]{3,2,1,0:T(8,128)S(1)} collective-permute-done((f32[16,2,8,128]{3,2,1,0:T(8,128)S(1)}, f32[16,2,8,128]{3,2,1,0:T(8,128)S(1)}, u32[]{:S(2)}, u32[]{:S(2)}) %collective-permute-start.11) | collective-permute-done | bytes 131104 | tf_op jit(solution)/shard_map/ppermute | solution.py:479
  142.1 4.3 %all-gather.10 = f32[32,2,8,128]{3,2,1,0:T(8,128)S(1)} all-gather(f32[16,2,8,128]{3,2,1,0:T(8,128)S(1)} %collective-permute-done.11), channel_id=12, replica_groups={{0,32},{64,96},{128,160},{192,224},{256,288},{320,352},{384,416},{448,4..., dimensions={0}, use_global_device_ids=true | all-gather | bytes 393216 | tf_op jit(solution)/shard_map/all_gather | solution.py:57
  146.4 2.4 %last.1 = f32[1,3,2,4,16,128]{5,4,3,2,1,0:T(8,128)} custom-call(s32[3]{0:T(128)S(1)} %pad_add_fusion.sc, f32[2,16,2,8,128]{4,3,2,1,0:T(8,128)S(1)} %bitcast.89, f32[32,2,8,128]{3,2,1,0:T(8,128)S(1)} %get-tuple-element.35.a_in, f32[28,3,8,128]{3,2,1,0:T(8,128)S(1)} %get-tuple-element.84.p1a, f32[24,3,8,128]{3,2,1,0:T(8,128)S(1)} %get-tuple-element.86.p2a, ...), custom_call_target="tpu_custom_call" | custom-call | tf_op jit(solution)/shard_map/last/pallas_call | solution.py:497
  (88 shorter events, 16.4 us)
Async XLA Ops:
  12.8 13.8 %collective-permute-start = (f32[64,2,8,128]{3,2,1,0:T(8,128)S(1)}, f32[64,2,8,128]{3,2,1,0:T(8,128)S(1)}, u32[]{:S(2)}, u32[]{:S(2)}) collective-permute-start(f32[64,2,8,128]{3,2,1,0:T(8,128)S(1)} %pad_maximum_fusion), channel_id=1, source_target_pairs={{0,2},{32,34},{64,66},{96,98},{128,130},{160,162},{192,194},{224,2... | collective-permute-start | bytes 1572872 | tf_op jit(solution)/shard_map/ppermute | solution.py:420
  16.4 13.9 %collective-permute-start.1 = (f32[64,2,8,128]{3,2,1,0:T(8,128)S(1)}, f32[64,2,8,128]{3,2,1,0:T(8,128)S(1)}, u32[]{:S(2)}, u32[]{:S(2)}) collective-permute-start(f32[64,2,8,128]{3,2,1,0:T(8,128)S(1)} %pad_maximum_fusion.1), channel_id=1, source_target_pairs={{0,30},{32,62},{64,94},{96,126},{128,158},{160,190},{192,222},{224... | collective-permute-start | bytes 1572872 | tf_op jit(solution)/shard_map/ppermute | solution.py:421
  36.0 20.2 %collective-permute-start.2 = (f32[58,8,128]{2,1,0:T(8,128)S(1)}, f32[58,8,128]{2,1,0:T(8,128)S(1)}, u32[]{:S(2)}, u32[]{:S(2)}) collective-permute-start(f32[58,8,128]{2,1,0:T(8,128)S(1)} %get-tuple-element.83), channel_id=1, source_target_pairs={{0,4},{32,60},{64,68},{96,124},{128,132},{160,188},{192,196},{224,... | collective-permute-start | bytes 712712 | tf_op jit(solution)/shard_map/ppermute | solution.py:445
  46.2 10.1 %collective-permute-start.3 = (f32[26,8,128]{2,1,0:T(8,128)S(1)}, f32[26,8,128]{2,1,0:T(8,128)S(1)}, u32[]{:S(2)}, u32[]{:S(2)}) collective-permute-start(f32[26,8,128]{2,1,0:T(8,128)S(1)} %pad_maximum_fusion.4), channel_id=1, source_target_pairs={{0,6},{32,58},{64,70},{96,122},{128,134},{160,186},{192,198},{224,... | collective-permute-start | bytes 319496 | tf_op jit(solution)/shard_map/ppermute | solution.py:445
  49.2 10.9 %collective-permute-start.4 = (f32[64,8,128]{2,1,0:T(8,128)S(1)}, f32[64,8,128]{2,1,0:T(8,128)S(1)}, u32[]{:S(2)}, u32[]{:S(2)}) collective-permute-start(f32[64,8,128]{2,1,0:T(8,128)S(1)} %get-tuple-element.82), channel_id=1, source_target_pairs={{0,2},{32,62},{64,66},{96,126},{128,130},{160,190},{192,194},{224,... | collective-permute-start | bytes 786440 | tf_op jit(solution)/shard_map/ppermute | solution.py:445
  63.6 0.7 collective-permute-start.5
  67.8 0.7 collective-permute-start.6
  72.0 0.7 collective-permute-start.7
  76.2 0.7 collective-permute-start.8
  80.3 0.7 collective-permute-start.9
  84.5 2.7 %collective-permute-start.10 = (f32[16,2,8,128]{3,2,1,0:T(8,128)}, f32[16,2,8,128]{3,2,1,0:T(8,128)}, u32[]{:S(2)}, u32[]{:S(2)}) collective-permute-start(f32[16,2,8,128]{3,2,1,0:T(8,128)} %get-tuple-element.32), channel_id=1, source_target_pairs={{320,388},{352,444},{321,389},{353,445},{322,390},{354,446},{323,3... | collective-permute-start | bytes 393224 | tf_op jit(solution)/shard_map/ppermute | solution.py:479
  85.9 6.5 %collective-permute-start.12 = (f32[12,2,2,8,128]{4,3,2,1,0:T(8,128)S(1)}, f32[12,2,2,8,128]{4,3,2,1,0:T(8,128)}, u32[]{:S(2)}, u32[]{:S(2)}) collective-permute-start(f32[12,2,2,8,128]{4,3,2,1,0:T(8,128)S(1)} %constant_dynamic-slice_fusion), channel_id=1, source_target_pairs={{0,32},{1,33},{2,34},{3,35},{4,36},{5,37},{6,38},{7,39},{8,40},{9,... | collective-permute-start | bytes 589832 | tf_op jit(solution)/shard_map/ppermute | solution.py:473
  91.1 51.0 %collective-permute-start.11 = (f32[16,2,8,128]{3,2,1,0:T(8,128)S(1)}, f32[16,2,8,128]{3,2,1,0:T(8,128)S(1)}, u32[]{:S(2)}, u32[]{:S(2)}) collective-permute-start(f32[16,2,8,128]{3,2,1,0:T(8,128)S(1)} %get-tuple-element.34), channel_id=1, source_target_pairs={{384,452},{416,508},{385,453},{417,509},{386,454},{418,510},{387,4... | collective-permute-start | bytes 393224 | tf_op jit(solution)/shard_map/ppermute | solution.py:479

commit v5 on v4

--- a/solution.py
+++ b/solution.py
@@ -49,7 +49,7 @@
 
 
 def turn_pairs(turn):
-    return [(flat(z, h, turn, k), flat(z + (2 if k == 0 else -2), h, turn + 1, k))
+    return [(flat(z, h, turn, k), flat(z + (2 if k == 0 else -2), h ^ k, turn + 1, k))
             for z in range(16) for h in range(2) for k in range(2)]
 
 
@@ -279,31 +279,14 @@
     coarse_node(n3, p2b, rates, 6, out, 16)
 
 
-def take(flag, moved, a_in, a):
-    @pl.when(flag != 0)
-    def _():
-        for side in range(2):
-            a[pl.ds(16 * side, 16)] = moved[side]
-
-    @pl.when(flag == 0)
-    def _():
-        a[...] = a_in[...]
-
-
-def first_chain_kernel(a, p1a, p2a, p1b, p2b, rates, out, n1, n2, n3):
+def chain_kernel(a, p1a, p2a, p1b, p2b, rates, out, n1, n2, n3):
     two_slices(a, (p1a, p2a, p1b, p2b, rates), n1, n2, n3, out)
 
 
-def chain_kernel(sc, moved, a_in, p1a, p2a, p1b, p2b, rates, a, out, n1, n2, n3):
-    take(sc[0], moved, a_in, a)
-    two_slices(a, (p1a, p2a, p1b, p2b, rates), n1, n2, n3, out)
-
-
-def last_kernel(sc, moved, a_in, p1a, p2a, p1b, p2b, rates, big, prev, res, a, n1, n2, n3, n4, gs, v1, tp):
-    take(sc[0], moved, a_in, a)
+def last_kernel(sc, a, p1a, p2a, p1b, p2b, rates, big, prev, res, n1, n2, n3, n4, gs, v1, tp):
     two_slices(a, (p1a, p2a, p1b, p2b, rates), n1, n2, n3, n4)
-    core = sc[1]
-    yh = sc[2]
+    core = sc[0]
+    yh = sc[1]
 
     @pl.when(core == 0)
     def _():
@@ -475,31 +458,22 @@
 
     scratch = [vmem(28, 2, 8, 128), vmem(24, 2, 8, 128), vmem(20, 2, 8, 128)]
 
-    def exchange(out, turn):
+    for turn in range(7):
+        out = pl.pallas_call(
+            chain_kernel, out_shape=shape(16, 2, 8, 128), in_specs=[VM] * 6, out_specs=VM,
+            scratch_shapes=scratch, name="chain", compiler_params=SMALL,
+        )(state, *prm)
         moved = lax.ppermute(out, AX, turn_pairs(turn))
-        moved = gather(moved, core_groups())
-        return moved, (chip == turn + 1).astype(jnp.int32)
-
-    out = pl.pallas_call(
-        first_chain_kernel, out_shape=shape(16, 2, 8, 128), in_specs=[VM] * 6, out_specs=VM,
-        scratch_shapes=scratch, name="chain", compiler_params=SMALL,
-    )(state, *prm)
-    for turn in range(6):
-        moved, takes = exchange(out, turn)
-        state, out = pl.pallas_call(
-            chain_kernel, out_shape=(shape(32, 2, 8, 128), shape(16, 2, 8, 128)),
-            in_specs=[SM] + [VM] * 7, out_specs=(VM, VM),
-            scratch_shapes=scratch, name="chain", compiler_params=SMALL,
-        )(takes.reshape(1), moved, state, *prm)
-    moved, takes = exchange(out, 6)
-
-    scalars = jnp.stack([takes, core, yh]).astype(jnp.int32)
+        moved = gather(moved, core_groups()).reshape(32, 2, 8, 128)
+        state = jnp.where(chip == turn + 1, moved, state)
+
+    scalars = jnp.stack([core, yh]).astype(jnp.int32)
     return pl.pallas_call(
-        last_kernel, out_shape=shape(1, 3, 2, 4, 16, 128), in_specs=[SM] + [VM] * 9, out_specs=VM,
-        scratch_shapes=[vmem(32, 2, 8, 128)] + scratch + [
+        last_kernel, out_shape=shape(1, 3, 2, 4, 16, 128), in_specs=[SM] + [VM] * 8, out_specs=VM,
+        scratch_shapes=scratch + [
             vmem(16, 2, 8, 128), vmem(8, 6, 8, 128), vmem(12, 2, 2, 8, 128), vmem(12, 12, 2, 8, 128)],
         name="last", compiler_params=SMALL,
-    )(scalars, moved, state, *prm, big, prev)
+    )(scalars, state, *prm, big, prev)
 
 
 def solution(mesh):

time: 149 us -> 146 us (0.980)
  the two profiles are of different devices: /device:TPU:63 before, /device:TPU:47 now
where the time goes in v5:
time: 146 us
  waiting for transfers between devices  62 us (42%)
  blocking collectives  38.7 us (27%)
  starting transfers between devices  30.2 us (21%)
  Pallas kernels  11.3 us (8%)
  other arithmetic  1.49 us (1%)
    ppermute x7, waiting for transfers between devices, program(): moved = lax.ppermute(out, AX, turn_pairs(turn))  48 us
    all_gather x11, blocking collectives, gather(): return lax.all_gather(x, AX, axis=0, axis_index_groups=groups, tiled=False)  38.7 us
    ppermute x3, starting transfers between devices, send(): return lax.ppermute(message, AX, split_pairs(step))  18.2 us
    ppermute x1, waiting for transfers between devices, program(): lo = lax.ppermute(edge(pair[2:8], pair[0:2]), AX, z_pairs(1))  8.3 us
    pallas_call x7, Pallas kernels, program(): pl.pallas_call(chain_kernel, out_shape=shape(16, 2, 8, 128), in_specs=[VM...  5.85 us
    ppermute x7, starting transfers between devices, program(): moved = lax.ppermute(out, AX, turn_pairs(turn))  5.29 us
    ppermute x1, waiting for transfers between devices, program(): hi = lax.ppermute(edge(pair[0:6], pair[6:8]), AX, z_pairs(-1))  3.68 us
    ppermute x1, starting transfers between devices, program(): lo = lax.ppermute(edge(pair[2:8], pair[0:2]), AX, z_pairs(1))  3.55 us
  transfers between devices with their start and end apart: 13, of which 4 were waited for; matrix products, arithmetic and copies ran while one was open for 0% of the time, Pallas kernels for 1%

profile of v5, /device:TPU:47, one launch (start us, length us, event | category | flops | bytes accessed | tf_op | source)
XLA Modules:
  0.0 145.6 jit_solution(654212873788524056)
XLA Ops:
  0.0 1.7 %pack.1 = f32[4,10,2,8,128]{4,3,2,1,0:T(8,128)} custom-call(f32[1,3,2,4,16,128]{5,4,3,2,1,0:T(8,128)} %nv.1, f32[1,2,4,16,128]{4,3,2,1,0:T(8,128)} %st.1, f32[4,16,128]{2,1,0:T(8,128)} %fr.1, f32[4,16,128]{2,1,0:T(8,128)} %kr.1), custom_call_target="tpu_custom_call" | custom-call | tf_op jit(solution)/shard_map/pack/pallas_call | solution.py:392
  1.7 11.0 %all-gather.pair = f32[8,10,2,8,128]{4,3,2,1,0:T(8,128)S(1)} all-gather(f32[4,10,2,8,128]{4,3,2,1,0:T(8,128)} %pack.1), channel_id=2, replica_groups={{0,1},{32,33},{64,65},{96,97},{128,129},{160,161},{192,193},{224,225},{..., dimensions={0}, use_global_device_ids=true | all-gather | bytes 983040 | tf_op jit(solution)/shard_map/all_gather | solution.py:57
  12.8 3.5 %collective-permute-start = (f32[64,2,8,128]{3,2,1,0:T(8,128)S(1)}, f32[64,2,8,128]{3,2,1,0:T(8,128)S(1)}, u32[]{:S(2)}, u32[]{:S(2)}) collective-permute-start(f32[64,2,8,128]{3,2,1,0:T(8,128)S(1)} %pad_maximum_fusion), channel_id=1, source_target_pairs={{0,2},{32,34},{64,66},{96,98},{128,130},{160,162},{192,194},{224,2... | collective-permute-start | bytes 1572872 | tf_op jit(solution)/shard_map/ppermute | solution.py:403
  16.4 1.9 %collective-permute-start.1 = (f32[64,2,8,128]{3,2,1,0:T(8,128)S(1)}, f32[64,2,8,128]{3,2,1,0:T(8,128)S(1)}, u32[]{:S(2)}, u32[]{:S(2)}) collective-permute-start(f32[64,2,8,128]{3,2,1,0:T(8,128)S(1)} %pad_maximum_fusion.1), channel_id=1, source_target_pairs={{0,30},{32,62},{64,94},{96,126},{128,158},{160,190},{192,222},{224... | collective-permute-start | bytes 1572872 | tf_op jit(solution)/shard_map/ppermute | solution.py:404
  18.4 8.3 %collective-permute-done.lo = f32[64,2,8,128]{3,2,1,0:T(8,128)S(1)} collective-permute-done((f32[64,2,8,128]{3,2,1,0:T(8,128)S(1)}, f32[64,2,8,128]{3,2,1,0:T(8,128)S(1)}, u32[]{:S(2)}, u32[]{:S(2)}) %collective-permute-start) | collective-permute-done | bytes 524320 | tf_op jit(solution)/shard_map/ppermute | solution.py:403
  26.7 3.7 %collective-permute-done.1.hi = f32[64,2,8,128]{3,2,1,0:T(8,128)S(1)} collective-permute-done((f32[64,2,8,128]{3,2,1,0:T(8,128)S(1)}, f32[64,2,8,128]{3,2,1,0:T(8,128)S(1)}, u32[]{:S(2)}, u32[]{:S(2)}) %collective-permute-start.1) | collective-permute-done | bytes 524320 | tf_op jit(solution)/shard_map/ppermute | solution.py:404
  31.7 4.2 %all-gather.1 = f32[88,8,128]{2,1,0:T(8,128)S(1)} all-gather(f32[44,8,128]{2,1,0:T(8,128)S(1)} %pad_maximum_fusion.3), channel_id=3, replica_groups={{0,32},{64,96},{128,160},{192,224},{256,288},{320,352},{384,416},{448,4..., dimensions={0}, use_global_device_ids=true | all-gather | bytes 540672 | tf_op jit(solution)/shard_map/all_gather | solution.py:57
  36.1 10.1 %collective-permute-start.2 = (f32[58,8,128]{2,1,0:T(8,128)S(1)}, f32[58,8,128]{2,1,0:T(8,128)S(1)}, u32[]{:S(2)}, u32[]{:S(2)}) collective-permute-start(f32[58,8,128]{2,1,0:T(8,128)S(1)} %get-tuple-element.59), channel_id=1, source_target_pairs={{0,4},{32,60},{64,68},{96,124},{128,132},{160,188},{192,196},{224,... | collective-permute-start | bytes 712712 | tf_op jit(solution)/shard_map/ppermute | solution.py:428
  46.2 3.0 %collective-permute-start.3 = (f32[26,8,128]{2,1,0:T(8,128)S(1)}, f32[26,8,128]{2,1,0:T(8,128)S(1)}, u32[]{:S(2)}, u32[]{:S(2)}) collective-permute-start(f32[26,8,128]{2,1,0:T(8,128)S(1)} %pad_maximum_fusion.4), channel_id=1, source_target_pairs={{0,6},{32,58},{64,70},{96,122},{128,134},{160,186},{192,198},{224,... | collective-permute-start | bytes 319496 | tf_op jit(solution)/shard_map/ppermute | solution.py:428
  49.2 5.1 %collective-permute-start.4 = (f32[64,8,128]{2,1,0:T(8,128)S(1)}, f32[64,8,128]{2,1,0:T(8,128)S(1)}, u32[]{:S(2)}, u32[]{:S(2)}) collective-permute-start(f32[64,8,128]{2,1,0:T(8,128)S(1)} %get-tuple-element.58), channel_id=1, source_target_pairs={{0,2},{32,62},{64,66},{96,126},{128,130},{160,190},{192,194},{224,... | collective-permute-start | bytes 786440 | tf_op jit(solution)/shard_map/ppermute | solution.py:428
  54.3 1.9 %collective-permute-done.3 = f32[26,8,128]{2,1,0:T(8,128)S(1)} collective-permute-done((f32[26,8,128]{2,1,0:T(8,128)S(1)}, f32[26,8,128]{2,1,0:T(8,128)S(1)}, u32[]{:S(2)}, u32[]{:S(2)}) %collective-permute-start.3) | collective-permute-done | bytes 106528 | tf_op jit(solution)/shard_map/ppermute | solution.py:428
  56.3 3.7 %all-gather.2 = f32[168,8,128]{2,1,0:T(8,128)S(1)} all-gather(f32[84,8,128]{2,1,0:T(8,128)S(1)} %pad_maximum_fusion.2), channel_id=4, replica_groups={{0,32},{64,96},{128,160},{192,224},{256,288},{320,352},{384,416},{448,4..., dimensions={0}, use_global_device_ids=true | all-gather | bytes 1032192 | tf_op jit(solution)/shard_map/all_gather | solution.py:57
  60.1 2.2 %all-gather.3 = f32[128,8,128]{2,1,0:T(8,128)S(1)} all-gather(f32[64,8,128]{2,1,0:T(8,128)S(1)} %collective-permute-done.4), channel_id=5, replica_groups={{0,32},{64,96},{128,160},{192,224},{256,288},{320,352},{384,416},{448,4..., dimensions={0}, use_global_device_ids=true | all-gather | bytes 786432 | tf_op jit(solution)/shard_map/all_gather | solution.py:57
  64.3 2.0 %all-gather.4 = f32[32,2,8,128]{3,2,1,0:T(8,128)S(1)} all-gather(f32[16,2,8,128]{3,2,1,0:T(8,128)S(1)} %collective-permute-done.5), channel_id=6, replica_groups={{0,32},{64,96},{128,160},{192,224},{256,288},{320,352},{384,416},{448,4..., dimensions={0}, use_global_device_ids=true | all-gather | bytes 393216 | tf_op jit(solution)/shard_map/all_gather | solution.py:57
  67.9 2.0 %all-gather.5 = f32[32,2,8,128]{3,2,1,0:T(8,128)S(1)} all-gather(f32[16,2,8,128]{3,2,1,0:T(8,128)S(1)} %collective-permute-done.6), channel_id=7, replica_groups={{0,32},{64,96},{128,160},{192,224},{256,288},{320,352},{384,416},{448,4..., dimensions={0}, use_global_device_ids=true | all-gather | bytes 393216 | tf_op jit(solution)/shard_map/all_gather | solution.py:57
  71.4 2.0 %all-gather.6 = f32[32,2,8,128]{3,2,1,0:T(8,128)S(1)} all-gather(f32[16,2,8,128]{3,2,1,0:T(8,128)S(1)} %collective-permute-done.7), channel_id=8, replica_groups={{0,32},{64,96},{128,160},{192,224},{256,288},{320,352},{384,416},{448,4..., dimensions={0}, use_global_device_ids=true | all-gather | bytes 393216 | tf_op jit(solution)/shard_map/all_gather | solution.py:57
  75.7 2.0 %all-gather.7 = f32[32,2,8,128]{3,2,1,0:T(8,128)S(1)} all-gather(f32[16,2,8,128]{3,2,1,0:T(8,128)S(1)} %collective-permute-done.8), channel_id=9, replica_groups={{0,32},{64,96},{128,160},{192,224},{256,288},{320,352},{384,416},{448,4..., dimensions={0}, use_global_device_ids=true | all-gather | bytes 393216 | tf_op jit(solution)/shard_map/all_gather | solution.py:57
  80.2 2.0 %all-gather.8 = f32[32,2,8,128]{3,2,1,0:T(8,128)S(1)} all-gather(f32[16,2,8,128]{3,2,1,0:T(8,128)S(1)} %collective-permute-done.9), channel_id=10, replica_groups={{0,32},{64,96},{128,160},{192,224},{256,288},{320,352},{384,416},{448,4..., dimensions={0}, use_global_device_ids=true | all-gather | bytes 393216 | tf_op jit(solution)/shard_map/all_gather | solution.py:57
  83.9 1.3 collective-permute-start.12
  85.2 2.8 %all-gather.9 = f32[32,2,8,128]{3,2,1,0:T(8,128)S(1)} all-gather(f32[16,2,8,128]{3,2,1,0:T(8,128)S(1)} %collective-permute-done.10), channel_id=11, replica_groups={{0,32},{64,96},{128,160},{192,224},{256,288},{320,352},{384,416},{448,4..., dimensions={0}, use_global_device_ids=true | all-gather | bytes 393216 | tf_op jit(solution)/shard_map/all_gather | solution.py:57
  88.8 1.3 collective-permute-start.11
  90.2 48.0 %collective-permute-done.11 = f32[16,2,8,128]{3,2,1,0:T(8,128)S(1)} collective-permute-done((f32[16,2,8,128]{3,2,1,0:T(8,128)S(1)}, f32[16,2,8,128]{3,2,1,0:T(8,128)S(1)}, u32[]{:S(2)}, u32[]{:S(2)}) %collective-permute-start.11) | collective-permute-done | bytes 131104 | tf_op jit(solution)/shard_map/ppermute | solution.py:466
  138.2 4.9 %all-gather.10 = f32[32,2,8,128]{3,2,1,0:T(8,128)S(1)} all-gather(f32[16,2,8,128]{3,2,1,0:T(8,128)S(1)} %collective-permute-done.11), channel_id=12, replica_groups={{0,32},{64,96},{128,160},{192,224},{256,288},{320,352},{384,416},{448,4..., dimensions={0}, use_global_device_ids=true | all-gather | bytes 393216 | tf_op jit(solution)/shard_map/all_gather | solution.py:57
  143.2 2.4 %last.1 = f32[1,3,2,4,16,128]{5,4,3,2,1,0:T(8,128)} custom-call(s32[2]{0:T(128)S(1)} %pad_add_fusion.sc, f32[32,2,8,128]{3,2,1,0:T(8,128)S(1)} %broadcast_select_fusion.6.a, f32[28,3,8,128]{3,2,1,0:T(8,128)S(1)} %get-tuple-element.60.p1a, f32[24,3,8,128]{3,2,1,0:T(8,128)S(1)} %get-tuple-element.62.p2a, f32[20,3,8,128]{3,2,1,0:T(8,128)S(1)} %get-tuple-element.61.p1b, ...), custom_call_target="tpu_custom_call" | custom-call | tf_op jit(solution)/shard_map/last/pallas_call | solution.py:471
  (97 shorter events, 13.8 us)
Async XLA Ops:
  12.8 13.8 %collective-permute-start = (f32[64,2,8,128]{3,2,1,0:T(8,128)S(1)}, f32[64,2,8,128]{3,2,1,0:T(8,128)S(1)}, u32[]{:S(2)}, u32[]{:S(2)}) collective-permute-start(f32[64,2,8,128]{3,2,1,0:T(8,128)S(1)} %pad_maximum_fusion), channel_id=1, source_target_pairs={{0,2},{32,34},{64,66},{96,98},{128,130},{160,162},{192,194},{224,2... | collective-permute-start | bytes 1572872 | tf_op jit(solution)/shard_map/ppermute | solution.py:403
  16.4 13.9 %collective-permute-start.1 = (f32[64,2,8,128]{3,2,1,0:T(8,128)S(1)}, f32[64,2,8,128]{3,2,1,0:T(8,128)S(1)}, u32[]{:S(2)}, u32[]{:S(2)}) collective-permute-start(f32[64,2,8,128]{3,2,1,0:T(8,128)S(1)} %pad_maximum_fusion.1), channel_id=1, source_target_pairs={{0,30},{32,62},{64,94},{96,126},{128,158},{160,190},{192,222},{224... | collective-permute-start | bytes 1572872 | tf_op jit(solution)/shard_map/ppermute | solution.py:404
  36.1 20.2 %collective-permute-start.2 = (f32[58,8,128]{2,1,0:T(8,128)S(1)}, f32[58,8,128]{2,1,0:T(8,128)S(1)}, u32[]{:S(2)}, u32[]{:S(2)}) collective-permute-start(f32[58,8,128]{2,1,0:T(8,128)S(1)} %get-tuple-element.59), channel_id=1, source_target_pairs={{0,4},{32,60},{64,68},{96,124},{128,132},{160,188},{192,196},{224,... | collective-permute-start | bytes 712712 | tf_op jit(solution)/shard_map/ppermute | solution.py:428
  46.2 10.1 %collective-permute-start.3 = (f32[26,8,128]{2,1,0:T(8,128)S(1)}, f32[26,8,128]{2,1,0:T(8,128)S(1)}, u32[]{:S(2)}, u32[]{:S(2)}) collective-permute-start(f32[26,8,128]{2,1,0:T(8,128)S(1)} %pad_maximum_fusion.4), channel_id=1, source_target_pairs={{0,6},{32,58},{64,70},{96,122},{128,134},{160,186},{192,198},{224,... | collective-permute-start | bytes 319496 | tf_op jit(solution)/shard_map/ppermute | solution.py:428
  49.2 10.9 %collective-permute-start.4 = (f32[64,8,128]{2,1,0:T(8,128)S(1)}, f32[64,8,128]{2,1,0:T(8,128)S(1)}, u32[]{:S(2)}, u32[]{:S(2)}) collective-permute-start(f32[64,8,128]{2,1,0:T(8,128)S(1)} %get-tuple-element.58), channel_id=1, source_target_pairs={{0,2},{32,62},{64,66},{96,126},{128,130},{160,190},{192,194},{224,... | collective-permute-start | bytes 786440 | tf_op jit(solution)/shard_map/ppermute | solution.py:428
  63.6 0.7 collective-permute-start.5
  67.2 0.7 collective-permute-start.6
  70.7 0.7 collective-permute-start.7
  74.3 0.7 copy-start
  75.0 0.7 collective-permute-start.8
  79.5 0.7 collective-permute-start.9
  83.1 2.1 %collective-permute-start.10 = (f32[16,2,8,128]{3,2,1,0:T(8,128)S(1)}, f32[16,2,8,128]{3,2,1,0:T(8,128)S(1)}, u32[]{:S(2)}, u32[]{:S(2)}) collective-permute-start(f32[16,2,8,128]{3,2,1,0:T(8,128)S(1)} %chain.12), channel_id=1, source_target_pairs={{320,388},{352,445},{321,389},{353,444},{322,390},{354,447},{323,3... | collective-permute-start | bytes 393224 | tf_op jit(solution)/shard_map/ppermute | solution.py:466
  83.9 6.3 %collective-permute-start.12 = (f32[12,2,2,8,128]{4,3,2,1,0:T(8,128)S(1)}, f32[12,2,2,8,128]{4,3,2,1,0:T(8,128)S(1)}, u32[]{:S(2)}, u32[]{:S(2)}) collective-permute-start(f32[12,2,2,8,128]{4,3,2,1,0:T(8,128)S(1)} %constant_dynamic-slice_fusion), channel_id=1, source_target_pairs={{0,32},{1,33},{2,34},{3,35},{4,36},{5,37},{6,38},{7,39},{8,40},{9,... | collective-permute-start | bytes 589832 | tf_op jit(solution)/shard_map/ppermute | solution.py:456
  88.8 49.4 %collective-permute-start.11 = (f32[16,2,8,128]{3,2,1,0:T(8,128)S(1)}, f32[16,2,8,128]{3,2,1,0:T(8,128)S(1)}, u32[]{:S(2)}, u32[]{:S(2)}) collective-permute-start(f32[16,2,8,128]{3,2,1,0:T(8,128)S(1)} %chain.13), channel_id=1, source_target_pairs={{384,452},{416,509},{385,453},{417,508},{386,454},{418,511},{387,4... | collective-permute-start | bytes 393224 | tf_op jit(solution)/shard_map/ppermute | solution.py:466

commit v6 on v5

--- a/solution.py
+++ b/solution.py
@@ -48,9 +48,13 @@
     return [(t * 32 + s, (t + 1) * 32 + s) for t in range(15) for s in range(32)]
 
 
-def turn_pairs(turn):
+def turn_pairs(turn, parity):
     return [(flat(z, h, turn, k), flat(z + (2 if k == 0 else -2), h ^ k, turn + 1, k))
-            for z in range(16) for h in range(2) for k in range(2)]
+            for z in range(parity, 16, 2) for h in range(2) for k in range(2)]
+
+
+def edge_pairs():
+    return [(flat(z, h, c, k), flat(z + (1 if h == 0 else -1), h, c, k)) for z, h, c, k in everyone()]
 
 
 def gather(x, groups):
@@ -126,7 +130,7 @@
 
 
 def sweep_kernel(pair, lo, hi, big, unit, start, rates, v1, v2, b2, xs, xp, cs):
-    segs = ((lo, 2, 6), (pair, 8, 8), (hi, 16, 6))
+    segs = ((lo, 2, 4), (pair, 6, 8), (hi, 14, 4))
 
     def raw(ref, i, f):
         if ref is pair:
@@ -134,10 +138,10 @@
         return jnp.stack([ref[i * 10 + f], ref[i * 10 + 10 + f]])
 
     for s in range(2):
-        v1[0, s] = lo[60 + s]
-        v1[1, s] = lo[62 + s]
-        v1[22, s] = hi[60 + s]
-        v1[23, s] = hi[62 + s]
+        v1[0, s] = lo[40 + s]
+        v1[1, s] = lo[42 + s]
+        v1[18, s] = hi[40 + s]
+        v1[19, s] = hi[42 + s]
 
     for ref, base, count in segs:
         def load_v1(n, _, ref=ref, base=base):
@@ -197,10 +201,10 @@
         big[at, 5] = nv
         return 0
 
-    unrolled(8, node_two)
+    unrolled(6, node_two)
 
     def integrals(n, _):
-        q = 4 + 2 * n
+        q = 2 + 2 * n
         at = pl.ds(q, 2)
         u = [big[at, 2 * j] for j in range(3)]
         v = [big[at, 2 * j + 1] for j in range(3)]
@@ -222,7 +226,7 @@
 
     def coarsen(n, _):
         at = pl.ds(2 * n, 2)
-        for f in range(6):
+        for f in range(6 if 1 <= n <= 6 else 4):
             cs[n, f] = restrict(big[at, f])
         f = restrict(big[at, 6])
         k = restrict(big[at, 7])
@@ -234,16 +238,16 @@
         rates[n, 1] = 1.0 / (1.0 + k)
         return 0
 
-    unrolled(10, coarsen)
+    unrolled(8, coarsen)
 
     def make_unit(n, _):
         for m in range(2):
-            cu, cv = cs[3 + n, 2 * m + 2], cs[3 + n, 2 * m + 3]
-            f, fk = cs[3 + n, 6], cs[3 + n, 7]
+            cu, cv = cs[2 + n, 2 * m + 2], cs[2 + n, 2 * m + 3]
+            f, fk = cs[2 + n, 6], cs[2 + n, 7]
             g = cu * cv * cv
             for s in range(2):
                 fl = fine_lap(xs[pl.ds(2 * n, 6), 2 * m + s], DIFF[s]) + xp[pl.ds(2 * n + 2, 2), 2 * m + s]
-                val = restrict(fl) - coarse_lap(cs[pl.ds(n + 1, 5), 2 * m + s], DIFF[s])[0]
+                val = restrict(fl) - coarse_lap(cs[pl.ds(n, 5), 2 * m + s], DIFF[s])[0]
                 if s == 0:
                     val = val + f * cu + g
                 else:
@@ -283,7 +287,7 @@
     two_slices(a, (p1a, p2a, p1b, p2b, rates), n1, n2, n3, out)
 
 
-def last_kernel(sc, a, p1a, p2a, p1b, p2b, rates, big, prev, res, n1, n2, n3, n4, gs, v1, tp):
+def last_kernel(sc, a, p1a, p2a, p1b, p2b, rates, big, end, prev, res, n1, n2, n3, n4, gs, v1, tp):
     two_slices(a, (p1a, p2a, p1b, p2b, rates), n1, n2, n3, n4)
     core = sc[0]
     yh = sc[1]
@@ -307,11 +311,11 @@
 
     def update(i, _):
         row = 2 * yh + i
-        at = pl.ds(2 + 4 * yh + 2 * i, 2)
+        at = pl.ds(4 * yh + 2 * i, 2)
         to = pl.ds(2 * i, 2)
         new = []
         for f in range(6):
-            x = big[at, f]
+            x = big[at, f] if f < 4 else end[to, f - 4]
             new.append(x + (gs[row, f] - restrict(x))[None, None])
         u, v = new[0::2], new[1::2]
         bu = prev[to, 0]
@@ -345,7 +349,7 @@
     def node_one(n, _):
         i = 2 + 2 * n
         at = pl.ds(i, 2)
-        br = pl.ds(2 + 4 * yh + i, 2)
+        br = pl.ds(4 * yh + i, 2)
         bu = tp[at, 0] + fine_lap(v1[pl.ds(i - 2, 6), 0], DIFF[0])
         bv = tp[at, 1] + fine_lap(v1[pl.ds(i - 2, 6), 1], DIFF[1])
         nu, nv = solve(bu, bv, tp[at, 2], big[br, 8], big[br, 9])
@@ -362,7 +366,7 @@
     for n in range(2):
         i = 4 + 2 * n
         at = pl.ds(i, 2)
-        br = pl.ds(2 + 4 * yh + i, 2)
+        br = pl.ds(4 * yh + i, 2)
         bu = tp[at, 5] + fine_lap(tp[pl.ds(i - 2, 6), 3], DIFF[0])
         bv = tp[at, 6] + fine_lap(tp[pl.ds(i - 2, 6), 4], DIFF[1])
         nu, nv = solve(bu, bv, tp[at, 7], big[br, 8], big[br, 9])
@@ -389,6 +393,7 @@
     chip = t // 2
     yh = lax.axis_index("slab") % 2
     left = core == 0
+    even_z = (lax.axis_index("slab") // 2) % 2 == 0
     own = pl.pallas_call(
         pack_kernel, out_shape=shape(4, 10, 2, 8, 128), in_specs=[VM] * 4, out_specs=VM,
         name="pack",
@@ -398,17 +403,17 @@
     def edge(planes, far):
         w = [far[:, 2 * j:2 * j + 2] for j in range(3)]
         v = first_combo(w, far[:, 6:8])
-        return jnp.concatenate([planes.reshape(60, 2, 8, 128), v.reshape(4, 2, 8, 128)])
-
-    lo = lax.ppermute(edge(pair[2:8], pair[0:2]), AX, z_pairs(1))
-    hi = lax.ppermute(edge(pair[0:6], pair[6:8]), AX, z_pairs(-1))
+        return jnp.concatenate([planes.reshape(40, 2, 8, 128), v.reshape(4, 2, 8, 128)])
+
+    lo = lax.ppermute(edge(pair[4:8], pair[2:4]), AX, z_pairs(1))
+    hi = lax.ppermute(edge(pair[0:4], pair[4:6]), AX, z_pairs(-1))
     big, unit, start, rates = pl.pallas_call(
         sweep_kernel,
-        out_shape=(shape(20, 10, 2, 8, 128), shape(2, 4, 3, 8, 128), shape(10, 2, 8, 128),
-                   shape(10, 2, 8, 128)),
+        out_shape=(shape(16, 10, 2, 8, 128), shape(2, 4, 3, 8, 128), shape(8, 2, 8, 128),
+                   shape(8, 2, 8, 128)),
         in_specs=[VM] * 3, out_specs=(VM, VM, VM, VM),
-        scratch_shapes=[vmem(24, 2, 2, 8, 128), vmem(20, 2, 2, 8, 128), vmem(20, 3, 2, 8, 128),
-                        vmem(12, 4, 2, 8, 128), vmem(12, 4, 2, 8, 128), vmem(10, 8, 8, 128)],
+        scratch_shapes=[vmem(20, 2, 2, 8, 128), vmem(16, 2, 2, 8, 128), vmem(16, 3, 2, 8, 128),
+                        vmem(12, 4, 2, 8, 128), vmem(12, 4, 2, 8, 128), vmem(8, 8, 8, 128)],
         name="sweep", compiler_params=SMALL,
     )(pair, lo, hi)
 
@@ -417,7 +422,7 @@
 
     both = gather(rows([unit, start]), core_groups())
     units = both[:, :24].reshape(2, 2, 4, 3, 8, 128)
-    start = both[0, 24:].reshape(10, 2, 8, 128)
+    start = both[0, 24:].reshape(8, 2, 8, 128)
     (p1a, p2a), (p1b, p2b) = units
 
     def near_planes(x, n):
@@ -427,12 +432,11 @@
         message = rows(parts)
         return lax.ppermute(message, AX, split_pairs(step))
 
-    start4 = jnp.where(left, start[0:4], start[6:10])
-    rates4 = jnp.where(left, rates[0:4], rates[6:10])
+    start4 = jnp.where(left, start[0:4], start[4:8])
+    rates4 = jnp.where(left, rates[0:4], rates[4:8])
     near = send([p1a, p2a, p1b, p2b, start4, rates4], 1)
     mid = send([p1a, p2a, p1b, near_planes(p2b, 2), start4, rates4], 2)
-    far = send([p1a, near_planes(p2a, 2), jnp.where(left, start[1:4], start[6:9]),
-                jnp.where(left, rates[3:4], rates[6:7])], 3)
+    far = send([p1a, near_planes(p2a, 2), start4, jnp.where(left, rates[2:4], rates[4:6])], 3)
     nears = gather(near, core_groups())
     fars = gather(jnp.concatenate([mid, far]), core_groups())
 
@@ -448,13 +452,16 @@
     p2a = window(p2a, (nears, 12, 4), (fars, 12, 4), (fars, 70, 2))
     p1b = window(p1b, (nears, 24, 4), (fars, 24, 4))
     p2b = window(p2b, (nears, 36, 4), (fars, 36, 2))
-    state = window(start, (nears, 48, 4), (fars, 42, 4), (fars, 76, 3))
-    rates = window(rates, (nears, 56, 4), (fars, 50, 4), (fars, 82, 1))
+    state = window(start, (nears, 48, 4), (fars, 42, 4), (fars, 76, 4))
+    rates = window(rates, (nears, 56, 4), (fars, 50, 4), (fars, 84, 2))
     prm = (p1a, p2a, p1b, p2b, rates)
 
-    mine = lax.dynamic_slice_in_dim(big, 2 + 4 * yh, 12, 0)
-    prev = lax.ppermute(mine[:, 4:6], AX, slice_pairs())
-    prev = jnp.where(t == 0, mine[:, 0:2], prev)
+    lower = yh == 0
+    outer = lax.ppermute(jnp.where(lower, big[8:10, 4:6], big[6:8, 4:6]), AX, edge_pairs())
+    end = jnp.where(lower, jnp.concatenate([outer, big[2:12, 4:6]]),
+                    jnp.concatenate([big[4:14, 4:6], outer]))
+    prev = lax.ppermute(end, AX, slice_pairs())
+    prev = jnp.where(t == 0, jnp.where(lower, big[0:12, 0:2], big[4:16, 0:2]), prev)
 
     scratch = [vmem(28, 2, 8, 128), vmem(24, 2, 8, 128), vmem(20, 2, 8, 128)]
 
@@ -463,17 +470,19 @@
             chain_kernel, out_shape=shape(16, 2, 8, 128), in_specs=[VM] * 6, out_specs=VM,
             scratch_shapes=scratch, name="chain", compiler_params=SMALL,
         )(state, *prm)
-        moved = lax.ppermute(out, AX, turn_pairs(turn))
+        even = lax.ppermute(out, AX, turn_pairs(turn, 0))
+        odd = lax.ppermute(out, AX, turn_pairs(turn, 1))
+        moved = jnp.where(even_z, even, odd)
         moved = gather(moved, core_groups()).reshape(32, 2, 8, 128)
         state = jnp.where(chip == turn + 1, moved, state)
 
     scalars = jnp.stack([core, yh]).astype(jnp.int32)
     return pl.pallas_call(
-        last_kernel, out_shape=shape(1, 3, 2, 4, 16, 128), in_specs=[SM] + [VM] * 8, out_specs=VM,
+        last_kernel, out_shape=shape(1, 3, 2, 4, 16, 128), in_specs=[SM] + [VM] * 9, out_specs=VM,
         scratch_shapes=scratch + [
             vmem(16, 2, 8, 128), vmem(8, 6, 8, 128), vmem(12, 2, 2, 8, 128), vmem(12, 12, 2, 8, 128)],
         name="last", compiler_params=SMALL,
-    )(scalars, state, *prm, big, prev)
+    )(scalars, state, *prm, big, end, prev)
 
 
 def solution(mesh):

time: 146 us -> 144 us (0.986)
  the two profiles are of different devices: /device:TPU:47 before, /device:TPU:6 now
where the time goes in v6:
time: 144 us; the launch traced here: 143 us
  waiting for transfers between devices  56.6 us (39%)
  starting transfers between devices  40.5 us (28%)
  blocking collectives  32.3 us (22%)
  Pallas kernels  11.1 us (8%)
    ppermute x7, waiting for transfers between devices, program(): even = lax.ppermute(out, AX, turn_pairs(turn, 0))  43.9 us
    all_gather x11, blocking collectives, gather(): return lax.all_gather(x, AX, axis=0, axis_index_groups=groups, tiled=False)  32.3 us
    ppermute x3, starting transfers between devices, send(): return lax.ppermute(message, AX, split_pairs(step))  12.8 us
    ppermute x1, starting transfers between devices, program(): hi = lax.ppermute(edge(pair[0:4], pair[4:6]), AX, z_pairs(-1))  9.5 us
    ppermute x7, starting transfers between devices, program(): even = lax.ppermute(out, AX, turn_pairs(turn, 0))  5.93 us
    pallas_call x7, Pallas kernels, program(): pl.pallas_call(chain_kernel, out_shape=shape(16, 2, 8, 128), in_specs=[VM...  5.9 us
    ppermute x3, waiting for transfers between devices, send(): return lax.ppermute(message, AX, split_pairs(step))  5.83 us
    ppermute x1, waiting for transfers between devices, program(): lo = lax.ppermute(edge(pair[4:8], pair[2:4]), AX, z_pairs(1))  5.56 us
  transfers between devices with their start and end apart: 21, of which 6 were waited for; matrix products, arithmetic and copies ran while one was open for 0% of the time, Pallas kernels for 1%

profile of v6, /device:TPU:6, one launch (start us, length us, event | category | flops | bytes accessed | tf_op | source)
XLA Modules:
  0.0 142.7 jit_solution(12575202268317692324)
XLA Ops:
  0.0 1.7 %pack.1 = f32[4,10,2,8,128]{4,3,2,1,0:T(8,128)} custom-call(f32[1,3,2,4,16,128]{5,4,3,2,1,0:T(8,128)} %nv.1, f32[1,2,4,16,128]{4,3,2,1,0:T(8,128)} %st.1, f32[4,16,128]{2,1,0:T(8,128)} %fr.1, f32[4,16,128]{2,1,0:T(8,128)} %kr.1), custom_call_target="tpu_custom_call" | custom-call | tf_op jit(solution)/shard_map/pack/pallas_call | solution.py:397
  1.7 11.8 %all-gather.pair = f32[8,10,2,8,128]{4,3,2,1,0:T(8,128)S(1)} all-gather(f32[4,10,2,8,128]{4,3,2,1,0:T(8,128)} %pack.1), channel_id=2, replica_groups={{0,1},{32,33},{64,65},{96,97},{128,129},{160,161},{192,193},{224,225},{..., dimensions={0}, use_global_device_ids=true | all-gather | bytes 983040 | tf_op jit(solution)/shard_map/all_gather | solution.py:61
  13.7 3.8 %collective-permute-start = (f32[44,2,8,128]{3,2,1,0:T(8,128)S(1)}, f32[44,2,8,128]{3,2,1,0:T(8,128)S(1)}, u32[]{:S(2)}, u32[]{:S(2)}) collective-permute-start(f32[44,2,8,128]{3,2,1,0:T(8,128)S(1)} %pad_maximum_fusion), channel_id=1, source_target_pairs={{0,2},{32,34},{64,66},{96,98},{128,130},{160,162},{192,194},{224,2... | collective-permute-start | bytes 1081352 | tf_op jit(solution)/shard_map/ppermute | solution.py:408
  17.5 9.5 %collective-permute-start.1 = (f32[44,2,8,128]{3,2,1,0:T(8,128)S(1)}, f32[44,2,8,128]{3,2,1,0:T(8,128)S(1)}, u32[]{:S(2)}, u32[]{:S(2)}) collective-permute-start(f32[44,2,8,128]{3,2,1,0:T(8,128)S(1)} %pad_maximum_fusion.1), channel_id=1, source_target_pairs={{0,30},{32,62},{64,94},{96,126},{128,158},{160,190},{192,222},{224... | collective-permute-start | bytes 1081352 | tf_op jit(solution)/shard_map/ppermute | solution.py:409
  27.0 5.6 %collective-permute-done.lo = f32[44,2,8,128]{3,2,1,0:T(8,128)S(1)} collective-permute-done((f32[44,2,8,128]{3,2,1,0:T(8,128)S(1)}, f32[44,2,8,128]{3,2,1,0:T(8,128)S(1)}, u32[]{:S(2)}, u32[]{:S(2)}) %collective-permute-start) | collective-permute-done | bytes 360480 | tf_op jit(solution)/shard_map/ppermute | solution.py:408
  35.0 2.0 %all-gather.1 = f32[80,8,128]{2,1,0:T(8,128)S(1)} all-gather(f32[40,8,128]{2,1,0:T(8,128)S(1)} %pad_maximum_fusion.3), channel_id=3, replica_groups={{0,32},{64,96},{128,160},{192,224},{256,288},{320,352},{384,416},{448,4..., dimensions={0}, use_global_device_ids=true | all-gather | bytes 491520 | tf_op jit(solution)/shard_map/all_gather | solution.py:61
  37.2 1.9 %collective-permute-start.2 = (f32[58,8,128]{2,1,0:T(8,128)S(1)}, f32[58,8,128]{2,1,0:T(8,128)S(1)}, u32[]{:S(2)}, u32[]{:S(2)}) collective-permute-start(f32[58,8,128]{2,1,0:T(8,128)S(1)} %get-tuple-element.61), channel_id=1, source_target_pairs={{0,4},{32,60},{64,68},{96,124},{128,132},{160,188},{192,196},{224,... | collective-permute-start | bytes 712712 | tf_op jit(solution)/shard_map/ppermute | solution.py:433
  39.1 5.8 %collective-permute-start.3 = (f32[30,8,128]{2,1,0:T(8,128)S(1)}, f32[30,8,128]{2,1,0:T(8,128)S(1)}, u32[]{:S(2)}, u32[]{:S(2)}) collective-permute-start(f32[30,8,128]{2,1,0:T(8,128)S(1)} %pad_maximum_fusion.4), channel_id=1, source_target_pairs={{0,6},{32,58},{64,70},{96,122},{128,134},{160,186},{192,198},{224,... | collective-permute-start | bytes 368648 | tf_op jit(solution)/shard_map/ppermute | solution.py:433
  45.0 5.0 %collective-permute-start.4 = (f32[64,8,128]{2,1,0:T(8,128)S(1)}, f32[64,8,128]{2,1,0:T(8,128)S(1)}, u32[]{:S(2)}, u32[]{:S(2)}) collective-permute-start(f32[64,8,128]{2,1,0:T(8,128)S(1)} %get-tuple-element.60), channel_id=1, source_target_pairs={{0,2},{32,62},{64,66},{96,126},{128,130},{160,190},{192,194},{224,... | collective-permute-start | bytes 786440 | tf_op jit(solution)/shard_map/ppermute | solution.py:433
  50.0 5.8 %collective-permute-done.3 = f32[30,8,128]{2,1,0:T(8,128)S(1)} collective-permute-done((f32[30,8,128]{2,1,0:T(8,128)S(1)}, f32[30,8,128]{2,1,0:T(8,128)S(1)}, u32[]{:S(2)}, u32[]{:S(2)}) %collective-permute-start.3) | collective-permute-done | bytes 122912 | tf_op jit(solution)/shard_map/ppermute | solution.py:433
  55.9 2.3 %all-gather.2 = f32[176,8,128]{2,1,0:T(8,128)S(1)} all-gather(f32[88,8,128]{2,1,0:T(8,128)S(1)} %pad_maximum_fusion.2), channel_id=4, replica_groups={{0,32},{64,96},{128,160},{192,224},{256,288},{320,352},{384,416},{448,4..., dimensions={0}, use_global_device_ids=true | all-gather | bytes 1081344 | tf_op jit(solution)/shard_map/all_gather | solution.py:61
  58.4 2.2 %all-gather.3 = f32[128,8,128]{2,1,0:T(8,128)S(1)} all-gather(f32[64,8,128]{2,1,0:T(8,128)S(1)} %collective-permute-done.4), channel_id=5, replica_groups={{0,32},{64,96},{128,160},{192,224},{256,288},{320,352},{384,416},{448,4..., dimensions={0}, use_global_device_ids=true | all-gather | bytes 786432 | tf_op jit(solution)/shard_map/all_gather | solution.py:61
  63.3 2.0 %all-gather.4 = f32[32,2,8,128]{3,2,1,0:T(8,128)S(1)} all-gather(f32[16,2,8,128]{3,2,1,0:T(8,128)S(1)} %broadcast_select_fusion.13), channel_id=6, replica_groups={{0,32},{64,96},{128,160},{192,224},{256,288},{320,352},{384,416},{448,4..., dimensions={0}, use_global_device_ids=true | all-gather | bytes 393216 | tf_op jit(solution)/shard_map/all_gather | solution.py:61
  67.6 2.0 %all-gather.5 = f32[32,2,8,128]{3,2,1,0:T(8,128)S(1)} all-gather(f32[16,2,8,128]{3,2,1,0:T(8,128)S(1)} %broadcast_select_fusion.12), channel_id=7, replica_groups={{0,32},{64,96},{128,160},{192,224},{256,288},{320,352},{384,416},{448,4..., dimensions={0}, use_global_device_ids=true | all-gather | bytes 393216 | tf_op jit(solution)/shard_map/all_gather | solution.py:61
  71.8 2.0 %all-gather.6 = f32[32,2,8,128]{3,2,1,0:T(8,128)S(1)} all-gather(f32[16,2,8,128]{3,2,1,0:T(8,128)S(1)} %broadcast_select_fusion.11), channel_id=8, replica_groups={{0,32},{64,96},{128,160},{192,224},{256,288},{320,352},{384,416},{448,4..., dimensions={0}, use_global_device_ids=true | all-gather | bytes 393216 | tf_op jit(solution)/shard_map/all_gather | solution.py:61
  76.2 2.0 %all-gather.7 = f32[32,2,8,128]{3,2,1,0:T(8,128)S(1)} all-gather(f32[16,2,8,128]{3,2,1,0:T(8,128)S(1)} %broadcast_select_fusion.10), channel_id=9, replica_groups={{0,32},{64,96},{128,160},{192,224},{256,288},{320,352},{384,416},{448,4..., dimensions={0}, use_global_device_ids=true | all-gather | bytes 393216 | tf_op jit(solution)/shard_map/all_gather | solution.py:61
  80.5 1.9 %collective-permute-start.19 = (f32[2,2,2,8,128]{4,3,2,1,0:T(8,128)S(1)}, f32[2,2,2,8,128]{4,3,2,1,0:T(8,128)S(1)}, u32[]{:S(2)}, u32[]{:S(2)}) collective-permute-start(f32[2,2,2,8,128]{4,3,2,1,0:T(8,128)S(1)} %slice_select_fusion.1), channel_id=1, source_target_pairs={{0,2},{32,34},{64,66},{96,98},{128,130},{160,162},{192,194},{224,2... | collective-permute-start | bytes 98312 | tf_op jit(solution)/shard_map/ppermute | solution.py:460
  82.4 2.0 %all-gather.8 = f32[32,2,8,128]{3,2,1,0:T(8,128)S(1)} all-gather(f32[16,2,8,128]{3,2,1,0:T(8,128)S(1)} %broadcast_select_fusion.9), channel_id=10, replica_groups={{0,32},{64,96},{128,160},{192,224},{256,288},{320,352},{384,416},{448,4..., dimensions={0}, use_global_device_ids=true | all-gather | bytes 393216 | tf_op jit(solution)/shard_map/all_gather | solution.py:61
  87.5 1.9 %collective-permute-start.20 = (f32[12,2,2,8,128]{4,3,2,1,0:T(8,128)S(1)}, f32[12,2,2,8,128]{4,3,2,1,0:T(8,128)S(1)}, u32[]{:S(2)}, u32[]{:S(2)}) collective-permute-start(f32[12,2,2,8,128]{4,3,2,1,0:T(8,128)S(1)} %maximum_select_fusion.end), channel_id=1, source_target_pairs={{0,32},{1,33},{2,34},{3,35},{4,36},{5,37},{6,38},{7,39},{8,40},{9,... | collective-permute-start | bytes 589832 | tf_op jit(solution)/shard_map/ppermute | solution.py:463
  89.5 41.0 %collective-permute-done.15 = f32[16,2,8,128]{3,2,1,0:T(8,128)S(1)} collective-permute-done((f32[16,2,8,128]{3,2,1,0:T(8,128)S(1)}, f32[16,2,8,128]{3,2,1,0:T(8,128)S(1)}, u32[]{:S(2)}, u32[]{:S(2)}) %collective-permute-start.15) | collective-permute-done | bytes 131104 | tf_op jit(solution)/shard_map/ppermute | solution.py:473
  130.5 2.0 %all-gather.9 = f32[32,2,8,128]{3,2,1,0:T(8,128)S(1)} all-gather(f32[16,2,8,128]{3,2,1,0:T(8,128)S(1)} %broadcast_select_fusion.8), channel_id=11, replica_groups={{0,32},{64,96},{128,160},{192,224},{256,288},{320,352},{384,416},{448,4..., dimensions={0}, use_global_device_ids=true | all-gather | bytes 393216 | tf_op jit(solution)/shard_map/all_gather | solution.py:61
  135.4 2.9 %collective-permute-done.17 = f32[16,2,8,128]{3,2,1,0:T(8,128)S(1)} collective-permute-done((f32[16,2,8,128]{3,2,1,0:T(8,128)S(1)}, f32[16,2,8,128]{3,2,1,0:T(8,128)S(1)}, u32[]{:S(2)}, u32[]{:S(2)}) %collective-permute-start.17) | collective-permute-done | bytes 131104 | tf_op jit(solution)/shard_map/ppermute | solution.py:473
  138.3 2.0 %all-gather.10 = f32[32,2,8,128]{3,2,1,0:T(8,128)S(1)} all-gather(f32[16,2,8,128]{3,2,1,0:T(8,128)S(1)} %broadcast_select_fusion.7), channel_id=12, replica_groups={{0,32},{64,96},{128,160},{192,224},{256,288},{320,352},{384,416},{448,4..., dimensions={0}, use_global_device_ids=true | all-gather | bytes 393216 | tf_op jit(solution)/shard_map/all_gather | solution.py:61
  140.3 2.4 %last.1 = f32[1,3,2,4,16,128]{5,4,3,2,1,0:T(8,128)} custom-call(s32[2]{0:T(128)S(1)} %pad_add_fusion.sc, f32[32,2,8,128]{3,2,1,0:T(8,128)S(1)} %broadcast_select_fusion.6.a, f32[28,3,8,128]{3,2,1,0:T(8,128)S(1)} %get-tuple-element.62.p1a, f32[24,3,8,128]{3,2,1,0:T(8,128)S(1)} %get-tuple-element.64.p2a, f32[20,3,8,128]{3,2,1,0:T(8,128)S(1)} %get-tuple-element.63.p1b, ...), custom_call_target="tpu_custom_call" | custom-call | tf_op jit(solution)/shard_map/last/pallas_call | solution.py:480
  (122 shorter events, 20.1 us)
Async XLA Ops:
  13.7 18.9 %collective-permute-start = (f32[44,2,8,128]{3,2,1,0:T(8,128)S(1)}, f32[44,2,8,128]{3,2,1,0:T(8,128)S(1)}, u32[]{:S(2)}, u32[]{:S(2)}) collective-permute-start(f32[44,2,8,128]{3,2,1,0:T(8,128)S(1)} %pad_maximum_fusion), channel_id=1, source_target_pairs={{0,2},{32,34},{64,66},{96,98},{128,130},{160,162},{192,194},{224,2... | collective-permute-start | bytes 1081352 | tf_op jit(solution)/shard_map/ppermute | solution.py:408
  17.5 16.3 %collective-permute-start.1 = (f32[44,2,8,128]{3,2,1,0:T(8,128)S(1)}, f32[44,2,8,128]{3,2,1,0:T(8,128)S(1)}, u32[]{:S(2)}, u32[]{:S(2)}) collective-permute-start(f32[44,2,8,128]{3,2,1,0:T(8,128)S(1)} %pad_maximum_fusion.1), channel_id=1, source_target_pairs={{0,30},{32,62},{64,94},{96,126},{128,158},{160,190},{192,222},{224... | collective-permute-start | bytes 1081352 | tf_op jit(solution)/shard_map/ppermute | solution.py:409
  37.2 18.6 %collective-permute-start.2 = (f32[58,8,128]{2,1,0:T(8,128)S(1)}, f32[58,8,128]{2,1,0:T(8,128)S(1)}, u32[]{:S(2)}, u32[]{:S(2)}) collective-permute-start(f32[58,8,128]{2,1,0:T(8,128)S(1)} %get-tuple-element.61), channel_id=1, source_target_pairs={{0,4},{32,60},{64,68},{96,124},{128,132},{160,188},{192,196},{224,... | collective-permute-start | bytes 712712 | tf_op jit(solution)/shard_map/ppermute | solution.py:433
  39.1 16.7 %collective-permute-start.3 = (f32[30,8,128]{2,1,0:T(8,128)S(1)}, f32[30,8,128]{2,1,0:T(8,128)S(1)}, u32[]{:S(2)}, u32[]{:S(2)}) collective-permute-start(f32[30,8,128]{2,1,0:T(8,128)S(1)} %pad_maximum_fusion.4), channel_id=1, source_target_pairs={{0,6},{32,58},{64,70},{96,122},{128,134},{160,186},{192,198},{224,... | collective-permute-start | bytes 368648 | tf_op jit(solution)/shard_map/ppermute | solution.py:433
  45.0 13.4 %collective-permute-start.4 = (f32[64,8,128]{2,1,0:T(8,128)S(1)}, f32[64,8,128]{2,1,0:T(8,128)S(1)}, u32[]{:S(2)}, u32[]{:S(2)}) collective-permute-start(f32[64,8,128]{2,1,0:T(8,128)S(1)} %get-tuple-element.60), channel_id=1, source_target_pairs={{0,2},{32,62},{64,66},{96,126},{128,130},{160,190},{192,194},{224,... | collective-permute-start | bytes 786440 | tf_op jit(solution)/shard_map/ppermute | solution.py:433
  61.8 1.4 collective-permute-start.6
  62.5 0.7 collective-permute-start.5
  66.2 1.4 collective-permute-start.8
  66.8 0.7 collective-permute-start.7
  70.4 1.4 collective-permute-start.10
  71.1 0.7 collective-permute-start.9
  74.7 1.5 %collective-permute-start.12 = (f32[16,2,8,128]{3,2,1,0:T(8,128)S(1)}, f32[16,2,8,128]{3,2,1,0:T(8,128)S(1)}, u32[]{:S(2)}, u32[]{:S(2)}) collective-permute-start(f32[16,2,8,128]{3,2,1,0:T(8,128)S(1)} %chain.10), channel_id=1, source_target_pairs={{194,262},{226,319},{195,263},{227,318},{198,266},{230,291},{199,2... | collective-permute-start | bytes 393224 | tf_op jit(solution)/shard_map/ppermute | solution.py:474
  75.4 0.8 collective-permute-start.11
  79.1 3.3 %collective-permute-start.14 = (f32[16,2,8,128]{3,2,1,0:T(8,128)S(1)}, f32[16,2,8,128]{3,2,1,0:T(8,128)S(1)}, u32[]{:S(2)}, u32[]{:S(2)}) collective-permute-start(f32[16,2,8,128]{3,2,1,0:T(8,128)S(1)} %chain.11), channel_id=1, source_target_pairs={{258,326},{290,383},{259,327},{291,382},{262,330},{294,355},{263,3... | collective-permute-start | bytes 393224 | tf_op jit(solution)/shard_map/ppermute | solution.py:474
  79.8 2.6 %collective-permute-start.13 = (f32[16,2,8,128]{3,2,1,0:T(8,128)S(1)}, f32[16,2,8,128]{3,2,1,0:T(8,128)S(1)}, u32[]{:S(2)}, u32[]{:S(2)}) collective-permute-start(f32[16,2,8,128]{3,2,1,0:T(8,128)S(1)} %chain.11), channel_id=1, source_target_pairs={{256,324},{288,381},{257,325},{289,380},{260,328},{292,353},{261,3... | collective-permute-start | bytes 393224 | tf_op jit(solution)/shard_map/ppermute | solution.py:473
  80.5 7.0 %collective-permute-start.19 = (f32[2,2,2,8,128]{4,3,2,1,0:T(8,128)S(1)}, f32[2,2,2,8,128]{4,3,2,1,0:T(8,128)S(1)}, u32[]{:S(2)}, u32[]{:S(2)}) collective-permute-start(f32[2,2,2,8,128]{4,3,2,1,0:T(8,128)S(1)} %slice_select_fusion.1), channel_id=1, source_target_pairs={{0,2},{32,34},{64,66},{96,98},{128,130},{160,162},{192,194},{224,2... | collective-permute-start | bytes 98312 | tf_op jit(solution)/shard_map/ppermute | solution.py:460
  85.3 4.1 %collective-permute-start.16 = (f32[16,2,8,128]{3,2,1,0:T(8,128)S(1)}, f32[16,2,8,128]{3,2,1,0:T(8,128)S(1)}, u32[]{:S(2)}, u32[]{:S(2)}) collective-permute-start(f32[16,2,8,128]{3,2,1,0:T(8,128)S(1)} %chain.12), channel_id=1, source_target_pairs={{322,390},{354,447},{323,391},{355,446},{326,394},{358,419},{327,3... | collective-permute-start | bytes 393224 | tf_op jit(solution)/shard_map/ppermute | solution.py:474
  86.0 44.4 %collective-permute-start.15 = (f32[16,2,8,128]{3,2,1,0:T(8,128)S(1)}, f32[16,2,8,128]{3,2,1,0:T(8,128)S(1)}, u32[]{:S(2)}, u32[]{:S(2)}) collective-permute-start(f32[16,2,8,128]{3,2,1,0:T(8,128)S(1)} %chain.12), channel_id=1, source_target_pairs={{320,388},{352,445},{321,389},{353,444},{324,392},{356,417},{325,3... | collective-permute-start | bytes 393224 | tf_op jit(solution)/shard_map/ppermute | solution.py:473
  87.5 47.8 %collective-permute-start.20 = (f32[12,2,2,8,128]{4,3,2,1,0:T(8,128)S(1)}, f32[12,2,2,8,128]{4,3,2,1,0:T(8,128)S(1)}, u32[]{:S(2)}, u32[]{:S(2)}) collective-permute-start(f32[12,2,2,8,128]{4,3,2,1,0:T(8,128)S(1)} %maximum_select_fusion.end), channel_id=1, source_target_pairs={{0,32},{1,33},{2,34},{3,35},{4,36},{5,37},{6,38},{7,39},{8,40},{9,... | collective-permute-start | bytes 589832 | tf_op jit(solution)/shard_map/ppermute | solution.py:463
  133.4 2.0 %collective-permute-start.18 = (f32[16,2,8,128]{3,2,1,0:T(8,128)S(1)}, f32[16,2,8,128]{3,2,1,0:T(8,128)S(1)}, u32[]{:S(2)}, u32[]{:S(2)}) collective-permute-start(f32[16,2,8,128]{3,2,1,0:T(8,128)S(1)} %chain.13), channel_id=1, source_target_pairs={{386,454},{418,511},{387,455},{419,510},{390,458},{422,483},{391,4... | collective-permute-start | bytes 393224 | tf_op jit(solution)/shard_map/ppermute | solution.py:474
  134.0 4.2 %collective-permute-start.17 = (f32[16,2,8,128]{3,2,1,0:T(8,128)S(1)}, f32[16,2,8,128]{3,2,1,0:T(8,128)S(1)}, u32[]{:S(2)}, u32[]{:S(2)}) collective-permute-start(f32[16,2,8,128]{3,2,1,0:T(8,128)S(1)} %chain.13), channel_id=1, source_target_pairs={{384,452},{416,509},{385,453},{417,508},{388,456},{420,481},{389,4... | collective-permute-start | bytes 393224 | tf_op jit(solution)/shard_map/ppermute | solution.py:473

commit v7 on v6

--- a/solution.py
+++ b/solution.py
@@ -48,9 +48,9 @@
     return [(t * 32 + s, (t + 1) * 32 + s) for t in range(15) for s in range(32)]
 
 
-def turn_pairs(turn, parity):
+def turn_pairs(turn):
     return [(flat(z, h, turn, k), flat(z + (2 if k == 0 else -2), h ^ k, turn + 1, k))
-            for z in range(parity, 16, 2) for h in range(2) for k in range(2)]
+            for z in range(16) for h in range(2) for k in range(2)]
 
 
 def edge_pairs():
@@ -393,7 +393,6 @@
     chip = t // 2
     yh = lax.axis_index("slab") % 2
     left = core == 0
-    even_z = (lax.axis_index("slab") // 2) % 2 == 0
     own = pl.pallas_call(
         pack_kernel, out_shape=shape(4, 10, 2, 8, 128), in_specs=[VM] * 4, out_specs=VM,
         name="pack",
@@ -470,9 +469,9 @@
             chain_kernel, out_shape=shape(16, 2, 8, 128), in_specs=[VM] * 6, out_specs=VM,
             scratch_shapes=scratch, name="chain", compiler_params=SMALL,
         )(state, *prm)
-        even = lax.ppermute(out, AX, turn_pairs(turn, 0))
-        odd = lax.ppermute(out, AX, turn_pairs(turn, 1))
-        moved = jnp.where(even_z, even, odd)
+        first = lax.ppermute(out[:8], AX, turn_pairs(turn))
+        rest = lax.ppermute(out[8:], AX, turn_pairs(turn))
+        moved = jnp.concatenate([first, rest])
         moved = gather(moved, core_groups()).reshape(32, 2, 8, 128)
         state = jnp.where(chip == turn + 1, moved, state)
 

time: 144 us -> 144 us (level)
  the two profiles are of different devices: /device:TPU:6 before, /device:TPU:15 now
where the time goes in v7:
time: 144 us
  waiting for transfers between devices  50.4 us (35%)
  blocking collectives  40.1 us (28%)
  starting transfers between devices  40 us (28%)
  Pallas kernels  11.2 us (8%)
    ppermute x7, waiting for transfers between devices, program(): first = lax.ppermute(out[:8], AX, turn_pairs(turn))  40.9 us
    all_gather x11, blocking collectives, gather(): return lax.all_gather(x, AX, axis=0, axis_index_groups=groups, tiled=False)  40.1 us
    ppermute x3, starting transfers between devices, send(): return lax.ppermute(message, AX, split_pairs(step))  13.1 us
    ppermute x1, starting transfers between devices, program(): hi = lax.ppermute(edge(pair[0:4], pair[4:6]), AX, z_pairs(-1))  9.5 us
    pallas_call x7, Pallas kernels, program(): pl.pallas_call(chain_kernel, out_shape=shape(16, 2, 8, 128), in_specs=[VM...  5.92 us
    ppermute x7, starting transfers between devices, program(): first = lax.ppermute(out[:8], AX, turn_pairs(turn))  5.28 us
    ppermute x7, starting transfers between devices, program(): rest = lax.ppermute(out[8:], AX, turn_pairs(turn))  5.28 us
    ppermute x1, waiting for transfers between devices, program(): lo = lax.ppermute(edge(pair[4:8], pair[2:4]), AX, z_pairs(1))  5.26 us
  transfers between devices with their start and end apart: 21, of which 5 were waited for; matrix products, arithmetic and copies ran while one was open for 0% of the time, Pallas kernels for 1%

profile of v7, /device:TPU:15, one launch (start us, length us, event | category | flops | bytes accessed | tf_op | source)
XLA Modules:
  0.0 143.8 jit_solution(3463489760895250938)
XLA Ops:
  0.0 1.7 %pack.1 = f32[4,10,2,8,128]{4,3,2,1,0:T(8,128)} custom-call(f32[1,3,2,4,16,128]{5,4,3,2,1,0:T(8,128)} %nv.1, f32[1,2,4,16,128]{4,3,2,1,0:T(8,128)} %st.1, f32[4,16,128]{2,1,0:T(8,128)} %fr.1, f32[4,16,128]{2,1,0:T(8,128)} %kr.1), custom_call_target="tpu_custom_call" | custom-call | tf_op jit(solution)/shard_map/pack/pallas_call | solution.py:396
  1.7 11.0 %all-gather.pair = f32[8,10,2,8,128]{4,3,2,1,0:T(8,128)S(1)} all-gather(f32[4,10,2,8,128]{4,3,2,1,0:T(8,128)} %pack.1), channel_id=2, replica_groups={{0,1},{32,33},{64,65},{96,97},{128,129},{160,161},{192,193},{224,225},{..., dimensions={0}, use_global_device_ids=true | all-gather | bytes 983040 | tf_op jit(solution)/shard_map/all_gather | solution.py:61
  12.8 3.5 %collective-permute-start = (f32[44,2,8,128]{3,2,1,0:T(8,128)S(1)}, f32[44,2,8,128]{3,2,1,0:T(8,128)S(1)}, u32[]{:S(2)}, u32[]{:S(2)}) collective-permute-start(f32[44,2,8,128]{3,2,1,0:T(8,128)S(1)} %pad_maximum_fusion), channel_id=1, source_target_pairs={{0,2},{32,34},{64,66},{96,98},{128,130},{160,162},{192,194},{224,2... | collective-permute-start | bytes 1081352 | tf_op jit(solution)/shard_map/ppermute | solution.py:407
  16.4 9.5 %collective-permute-start.1 = (f32[44,2,8,128]{3,2,1,0:T(8,128)S(1)}, f32[44,2,8,128]{3,2,1,0:T(8,128)S(1)}, u32[]{:S(2)}, u32[]{:S(2)}) collective-permute-start(f32[44,2,8,128]{3,2,1,0:T(8,128)S(1)} %pad_maximum_fusion.1), channel_id=1, source_target_pairs={{0,30},{32,62},{64,94},{96,126},{128,158},{160,190},{192,222},{224... | collective-permute-start | bytes 1081352 | tf_op jit(solution)/shard_map/ppermute | solution.py:408
  25.9 5.3 %collective-permute-done.lo = f32[44,2,8,128]{3,2,1,0:T(8,128)S(1)} collective-permute-done((f32[44,2,8,128]{3,2,1,0:T(8,128)S(1)}, f32[44,2,8,128]{3,2,1,0:T(8,128)S(1)}, u32[]{:S(2)}, u32[]{:S(2)}) %collective-permute-start) | collective-permute-done | bytes 360480 | tf_op jit(solution)/shard_map/ppermute | solution.py:407
  33.3 4.1 %all-gather.1 = f32[80,8,128]{2,1,0:T(8,128)S(1)} all-gather(f32[40,8,128]{2,1,0:T(8,128)S(1)} %pad_maximum_fusion.3), channel_id=3, replica_groups={{0,32},{64,96},{128,160},{192,224},{256,288},{320,352},{384,416},{448,4..., dimensions={0}, use_global_device_ids=true | all-gather | bytes 491520 | tf_op jit(solution)/shard_map/all_gather | solution.py:61
  37.5 5.3 %collective-permute-start.2 = (f32[58,8,128]{2,1,0:T(8,128)S(1)}, f32[58,8,128]{2,1,0:T(8,128)S(1)}, u32[]{:S(2)}, u32[]{:S(2)}) collective-permute-start(f32[58,8,128]{2,1,0:T(8,128)S(1)} %get-tuple-element.75), channel_id=1, source_target_pairs={{0,4},{32,60},{64,68},{96,124},{128,132},{160,188},{192,196},{224,... | collective-permute-start | bytes 712712 | tf_op jit(solution)/shard_map/ppermute | solution.py:432
  42.8 5.9 %collective-permute-start.3 = (f32[30,8,128]{2,1,0:T(8,128)S(1)}, f32[30,8,128]{2,1,0:T(8,128)S(1)}, u32[]{:S(2)}, u32[]{:S(2)}) collective-permute-start(f32[30,8,128]{2,1,0:T(8,128)S(1)} %pad_maximum_fusion.11), channel_id=1, source_target_pairs={{0,6},{32,58},{64,70},{96,122},{128,134},{160,186},{192,198},{224,... | collective-permute-start | bytes 368648 | tf_op jit(solution)/shard_map/ppermute | solution.py:432
  48.8 1.9 %collective-permute-start.4 = (f32[64,8,128]{2,1,0:T(8,128)S(1)}, f32[64,8,128]{2,1,0:T(8,128)S(1)}, u32[]{:S(2)}, u32[]{:S(2)}) collective-permute-start(f32[64,8,128]{2,1,0:T(8,128)S(1)} %get-tuple-element.74), channel_id=1, source_target_pairs={{0,2},{32,62},{64,66},{96,126},{128,130},{160,190},{192,194},{224,... | collective-permute-start | bytes 786440 | tf_op jit(solution)/shard_map/ppermute | solution.py:432
  50.7 1.6 %collective-permute-done.3 = f32[30,8,128]{2,1,0:T(8,128)S(1)} collective-permute-done((f32[30,8,128]{2,1,0:T(8,128)S(1)}, f32[30,8,128]{2,1,0:T(8,128)S(1)}, u32[]{:S(2)}, u32[]{:S(2)}) %collective-permute-start.3) | collective-permute-done | bytes 122912 | tf_op jit(solution)/shard_map/ppermute | solution.py:432
  52.3 6.1 %all-gather.2 = f32[176,8,128]{2,1,0:T(8,128)S(1)} all-gather(f32[88,8,128]{2,1,0:T(8,128)S(1)} %pad_maximum_fusion.2), channel_id=4, replica_groups={{0,32},{64,96},{128,160},{192,224},{256,288},{320,352},{384,416},{448,4..., dimensions={0}, use_global_device_ids=true | all-gather | bytes 1081344 | tf_op jit(solution)/shard_map/all_gather | solution.py:61
  58.7 2.2 %all-gather.3 = f32[128,8,128]{2,1,0:T(8,128)S(1)} all-gather(f32[64,8,128]{2,1,0:T(8,128)S(1)} %collective-permute-done.4), channel_id=5, replica_groups={{0,32},{64,96},{128,160},{192,224},{256,288},{320,352},{384,416},{448,4..., dimensions={0}, use_global_device_ids=true | all-gather | bytes 786432 | tf_op jit(solution)/shard_map/all_gather | solution.py:61
  63.6 2.0 %all-gather.4 = f32[32,2,8,128]{3,2,1,0:T(8,128)S(1)} all-gather(f32[16,2,8,128]{3,2,1,0:T(8,128)S(1)} %pad_maximum_fusion.4), channel_id=6, replica_groups={{0,32},{64,96},{128,160},{192,224},{256,288},{320,352},{384,416},{448,4..., dimensions={0}, use_global_device_ids=true | all-gather | bytes 393216 | tf_op jit(solution)/shard_map/all_gather | solution.py:61
  67.9 2.0 %all-gather.5 = f32[32,2,8,128]{3,2,1,0:T(8,128)S(1)} all-gather(f32[16,2,8,128]{3,2,1,0:T(8,128)S(1)} %pad_maximum_fusion.5), channel_id=7, replica_groups={{0,32},{64,96},{128,160},{192,224},{256,288},{320,352},{384,416},{448,4..., dimensions={0}, use_global_device_ids=true | all-gather | bytes 393216 | tf_op jit(solution)/shard_map/all_gather | solution.py:61
  72.2 2.0 %all-gather.6 = f32[32,2,8,128]{3,2,1,0:T(8,128)S(1)} all-gather(f32[16,2,8,128]{3,2,1,0:T(8,128)S(1)} %pad_maximum_fusion.6), channel_id=8, replica_groups={{0,32},{64,96},{128,160},{192,224},{256,288},{320,352},{384,416},{448,4..., dimensions={0}, use_global_device_ids=true | all-gather | bytes 393216 | tf_op jit(solution)/shard_map/all_gather | solution.py:61
  76.6 2.0 %all-gather.7 = f32[32,2,8,128]{3,2,1,0:T(8,128)S(1)} all-gather(f32[16,2,8,128]{3,2,1,0:T(8,128)S(1)} %pad_maximum_fusion.7), channel_id=9, replica_groups={{0,32},{64,96},{128,160},{192,224},{256,288},{320,352},{384,416},{448,4..., dimensions={0}, use_global_device_ids=true | all-gather | bytes 393216 | tf_op jit(solution)/shard_map/all_gather | solution.py:61
  80.8 1.9 %collective-permute-start.19 = (f32[2,2,2,8,128]{4,3,2,1,0:T(8,128)S(1)}, f32[2,2,2,8,128]{4,3,2,1,0:T(8,128)S(1)}, u32[]{:S(2)}, u32[]{:S(2)}) collective-permute-start(f32[2,2,2,8,128]{4,3,2,1,0:T(8,128)S(1)} %slice_select_fusion.1), channel_id=1, source_target_pairs={{0,2},{32,34},{64,66},{96,98},{128,130},{160,162},{192,194},{224,2... | collective-permute-start | bytes 98312 | tf_op jit(solution)/shard_map/ppermute | solution.py:459
  82.8 2.0 %all-gather.8 = f32[32,2,8,128]{3,2,1,0:T(8,128)S(1)} all-gather(f32[16,2,8,128]{3,2,1,0:T(8,128)S(1)} %pad_maximum_fusion.8), channel_id=10, replica_groups={{0,32},{64,96},{128,160},{192,224},{256,288},{320,352},{384,416},{448,4..., dimensions={0}, use_global_device_ids=true | all-gather | bytes 393216 | tf_op jit(solution)/shard_map/all_gather | solution.py:61
  87.1 1.3 collective-permute-start.20
  88.4 3.4 %all-gather.9 = f32[32,2,8,128]{3,2,1,0:T(8,128)S(1)} all-gather(f32[16,2,8,128]{3,2,1,0:T(8,128)S(1)} %pad_maximum_fusion.9), channel_id=11, replica_groups={{0,32},{64,96},{128,160},{192,224},{256,288},{320,352},{384,416},{448,4..., dimensions={0}, use_global_device_ids=true | all-gather | bytes 393216 | tf_op jit(solution)/shard_map/all_gather | solution.py:61
  95.4 40.9 %collective-permute-done.17 = f32[8,2,8,128]{3,2,1,0:T(8,128)S(1)} collective-permute-done((f32[8,2,8,128]{3,2,1,0:T(8,128)S(1)}, f32[8,2,8,128]{3,2,1,0:T(8,128)S(1)}, u32[]{:S(2)}, u32[]{:S(2)}) %collective-permute-start.17) | collective-permute-done | bytes 65568 | tf_op jit(solution)/shard_map/ppermute | solution.py:472
  136.3 1.7 %collective-permute-done.18 = f32[8,2,8,128]{3,2,1,0:T(8,128)S(1)} collective-permute-done((f32[8,2,8,128]{3,2,1,0:T(8,128)S(1)}, f32[8,2,8,128]{3,2,1,0:T(8,128)S(1)}, u32[]{:S(2)}, u32[]{:S(2)}) %collective-permute-start.18) | collective-permute-done | bytes 65568 | tf_op jit(solution)/shard_map/ppermute | solution.py:473
  138.0 3.3 %all-gather.10 = f32[32,2,8,128]{3,2,1,0:T(8,128)S(1)} all-gather(f32[16,2,8,128]{3,2,1,0:T(8,128)S(1)} %pad_maximum_fusion.10), channel_id=12, replica_groups={{0,32},{64,96},{128,160},{192,224},{256,288},{320,352},{384,416},{448,4..., dimensions={0}, use_global_device_ids=true | all-gather | bytes 393216 | tf_op jit(solution)/shard_map/all_gather | solution.py:61
  141.4 2.4 %last.1 = f32[1,3,2,4,16,128]{5,4,3,2,1,0:T(8,128)} custom-call(s32[2]{0:T(128)S(1)} %pad_add_fusion.sc, f32[32,2,8,128]{3,2,1,0:T(8,128)S(1)} %broadcast_select_fusion.6.a, f32[28,3,8,128]{3,2,1,0:T(8,128)S(1)} %get-tuple-element.76.p1a, f32[24,3,8,128]{3,2,1,0:T(8,128)S(1)} %get-tuple-element.78.p2a, f32[20,3,8,128]{3,2,1,0:T(8,128)S(1)} %get-tuple-element.77.p1b, ...), custom_call_target="tpu_custom_call" | custom-call | tf_op jit(solution)/shard_map/last/pallas_call | solution.py:479
  (129 shorter events, 19.7 us)
Async XLA Ops:
  12.8 18.4 %collective-permute-start = (f32[44,2,8,128]{3,2,1,0:T(8,128)S(1)}, f32[44,2,8,128]{3,2,1,0:T(8,128)S(1)}, u32[]{:S(2)}, u32[]{:S(2)}) collective-permute-start(f32[44,2,8,128]{3,2,1,0:T(8,128)S(1)} %pad_maximum_fusion), channel_id=1, source_target_pairs={{0,2},{32,34},{64,66},{96,98},{128,130},{160,162},{192,194},{224,2... | collective-permute-start | bytes 1081352 | tf_op jit(solution)/shard_map/ppermute | solution.py:407
  16.4 15.7 %collective-permute-start.1 = (f32[44,2,8,128]{3,2,1,0:T(8,128)S(1)}, f32[44,2,8,128]{3,2,1,0:T(8,128)S(1)}, u32[]{:S(2)}, u32[]{:S(2)}) collective-permute-start(f32[44,2,8,128]{3,2,1,0:T(8,128)S(1)} %pad_maximum_fusion.1), channel_id=1, source_target_pairs={{0,30},{32,62},{64,94},{96,126},{128,158},{160,190},{192,222},{224... | collective-permute-start | bytes 1081352 | tf_op jit(solution)/shard_map/ppermute | solution.py:408
  37.5 14.8 %collective-permute-start.2 = (f32[58,8,128]{2,1,0:T(8,128)S(1)}, f32[58,8,128]{2,1,0:T(8,128)S(1)}, u32[]{:S(2)}, u32[]{:S(2)}) collective-permute-start(f32[58,8,128]{2,1,0:T(8,128)S(1)} %get-tuple-element.75), channel_id=1, source_target_pairs={{0,4},{32,60},{64,68},{96,124},{128,132},{160,188},{192,196},{224,... | collective-permute-start | bytes 712712 | tf_op jit(solution)/shard_map/ppermute | solution.py:432
  42.8 9.5 %collective-permute-start.3 = (f32[30,8,128]{2,1,0:T(8,128)S(1)}, f32[30,8,128]{2,1,0:T(8,128)S(1)}, u32[]{:S(2)}, u32[]{:S(2)}) collective-permute-start(f32[30,8,128]{2,1,0:T(8,128)S(1)} %pad_maximum_fusion.11), channel_id=1, source_target_pairs={{0,6},{32,58},{64,70},{96,122},{128,134},{160,186},{192,198},{224,... | collective-permute-start | bytes 368648 | tf_op jit(solution)/shard_map/ppermute | solution.py:432
  48.8 9.9 %collective-permute-start.4 = (f32[64,8,128]{2,1,0:T(8,128)S(1)}, f32[64,8,128]{2,1,0:T(8,128)S(1)}, u32[]{:S(2)}, u32[]{:S(2)}) collective-permute-start(f32[64,8,128]{2,1,0:T(8,128)S(1)} %get-tuple-element.74), channel_id=1, source_target_pairs={{0,2},{32,62},{64,66},{96,126},{128,130},{160,190},{192,194},{224,... | collective-permute-start | bytes 786440 | tf_op jit(solution)/shard_map/ppermute | solution.py:432
  62.2 1.4 collective-permute-start.5
  62.8 0.7 collective-permute-start.6
  66.5 1.4 collective-permute-start.7
  67.1 0.7 collective-permute-start.8
  70.8 1.4 collective-permute-start.9
  71.5 0.8 collective-permute-start.10
  75.1 1.4 collective-permute-start.11
  75.8 0.7 collective-permute-start.12
  79.5 3.3 %collective-permute-start.13 = (f32[8,2,8,128]{3,2,1,0:T(8,128)S(1)}, f32[8,2,8,128]{3,2,1,0:T(8,128)S(1)}, u32[]{:S(2)}, u32[]{:S(2)}) collective-permute-start(f32[8,2,8,128]{3,2,1,0:T(8,128)S(1)} %get-tuple-element.64), channel_id=1, source_target_pairs={{256,324},{288,381},{257,325},{289,380},{258,326},{290,383},{259,3... | collective-permute-start | bytes 196616 | tf_op jit(solution)/shard_map/ppermute | solution.py:472
  80.1 2.6 %collective-permute-start.14 = (f32[8,2,8,128]{3,2,1,0:T(8,128)S(1)}, f32[8,2,8,128]{3,2,1,0:T(8,128)S(1)}, u32[]{:S(2)}, u32[]{:S(2)}) collective-permute-start(f32[8,2,8,128]{3,2,1,0:T(8,128)S(1)} %get-tuple-element.65), channel_id=1, source_target_pairs={{256,324},{288,381},{257,325},{289,380},{258,326},{290,383},{259,3... | collective-permute-start | bytes 196616 | tf_op jit(solution)/shard_map/ppermute | solution.py:473
  80.8 6.2 %collective-permute-start.19 = (f32[2,2,2,8,128]{4,3,2,1,0:T(8,128)S(1)}, f32[2,2,2,8,128]{4,3,2,1,0:T(8,128)S(1)}, u32[]{:S(2)}, u32[]{:S(2)}) collective-permute-start(f32[2,2,2,8,128]{4,3,2,1,0:T(8,128)S(1)} %slice_select_fusion.1), channel_id=1, source_target_pairs={{0,2},{32,34},{64,66},{96,98},{128,130},{160,162},{192,194},{224,2... | collective-permute-start | bytes 98312 | tf_op jit(solution)/shard_map/ppermute | solution.py:459
  85.7 2.7 %collective-permute-start.15 = (f32[8,2,8,128]{3,2,1,0:T(8,128)S(1)}, f32[8,2,8,128]{3,2,1,0:T(8,128)S(1)}, u32[]{:S(2)}, u32[]{:S(2)}) collective-permute-start(f32[8,2,8,128]{3,2,1,0:T(8,128)S(1)} %get-tuple-element.62), channel_id=1, source_target_pairs={{320,388},{352,445},{321,389},{353,444},{322,390},{354,447},{323,3... | collective-permute-start | bytes 196616 | tf_op jit(solution)/shard_map/ppermute | solution.py:472
  86.4 2.0 %collective-permute-start.16 = (f32[8,2,8,128]{3,2,1,0:T(8,128)S(1)}, f32[8,2,8,128]{3,2,1,0:T(8,128)S(1)}, u32[]{:S(2)}, u32[]{:S(2)}) collective-permute-start(f32[8,2,8,128]{3,2,1,0:T(8,128)S(1)} %get-tuple-element.63), channel_id=1, source_target_pairs={{320,388},{352,445},{321,389},{353,444},{322,390},{354,447},{323,3... | collective-permute-start | bytes 196616 | tf_op jit(solution)/shard_map/ppermute | solution.py:473
  87.1 8.3 %collective-permute-start.20 = (f32[12,2,2,8,128]{4,3,2,1,0:T(8,128)S(1)}, f32[12,2,2,8,128]{4,3,2,1,0:T(8,128)S(1)}, u32[]{:S(2)}, u32[]{:S(2)}) collective-permute-start(f32[12,2,2,8,128]{4,3,2,1,0:T(8,128)S(1)} %maximum_select_fusion.end), channel_id=1, source_target_pairs={{0,32},{1,33},{2,34},{3,35},{4,36},{5,37},{6,38},{7,39},{8,40},{9,... | collective-permute-start | bytes 589832 | tf_op jit(solution)/shard_map/ppermute | solution.py:462
  92.8 43.5 %collective-permute-start.17 = (f32[8,2,8,128]{3,2,1,0:T(8,128)S(1)}, f32[8,2,8,128]{3,2,1,0:T(8,128)S(1)}, u32[]{:S(2)}, u32[]{:S(2)}) collective-permute-start(f32[8,2,8,128]{3,2,1,0:T(8,128)S(1)} %get-tuple-element.60), channel_id=1, source_target_pairs={{384,452},{416,509},{385,453},{417,508},{386,454},{418,511},{387,4... | collective-permute-start | bytes 196616 | tf_op jit(solution)/shard_map/ppermute | solution.py:472
  94.1 43.9 %collective-permute-start.18 = (f32[8,2,8,128]{3,2,1,0:T(8,128)S(1)}, f32[8,2,8,128]{3,2,1,0:T(8,128)S(1)}, u32[]{:S(2)}, u32[]{:S(2)}) collective-permute-start(f32[8,2,8,128]{3,2,1,0:T(8,128)S(1)} %get-tuple-element.61), channel_id=1, source_target_pairs={{384,452},{416,509},{385,453},{417,508},{386,454},{418,511},{387,4... | collective-permute-start | bytes 196616 | tf_op jit(solution)/shard_map/ppermute | solution.py:473

commit v8 on v7

--- a/solution.py
+++ b/solution.py
@@ -51,10 +51,6 @@
 def turn_pairs(turn):
     return [(flat(z, h, turn, k), flat(z + (2 if k == 0 else -2), h ^ k, turn + 1, k))
             for z in range(16) for h in range(2) for k in range(2)]
-
-
-def edge_pairs():
-    return [(flat(z, h, c, k), flat(z + (1 if h == 0 else -1), h, c, k)) for z, h, c, k in everyone()]
 
 
 def gather(x, groups):
@@ -419,9 +415,12 @@
     def rows(parts):
         return jnp.concatenate([x.reshape(-1, 8, 128) for x in parts])
 
-    both = gather(rows([unit, start]), core_groups())
+    lower = yh == 0
+    outer = jnp.where(lower, big[8:10, 4:6], big[6:8, 4:6])
+    both = gather(rows([unit, start, outer]), core_groups())
+    outer = both[:, 40:]
     units = both[:, :24].reshape(2, 2, 4, 3, 8, 128)
-    start = both[0, 24:].reshape(8, 2, 8, 128)
+    start = both[0, 24:40].reshape(8, 2, 8, 128)
     (p1a, p2a), (p1b, p2b) = units
 
     def near_planes(x, n):
@@ -433,11 +432,12 @@
 
     start4 = jnp.where(left, start[0:4], start[4:8])
     rates4 = jnp.where(left, rates[0:4], rates[4:8])
-    near = send([p1a, p2a, p1b, p2b, start4, rates4], 1)
+    near = send([p1a, p2a, p1b, p2b, start4, rates4, outer], 1)
     mid = send([p1a, p2a, p1b, near_planes(p2b, 2), start4, rates4], 2)
     far = send([p1a, near_planes(p2a, 2), start4, jnp.where(left, rates[2:4], rates[4:6])], 3)
     nears = gather(near, core_groups())
-    fars = gather(jnp.concatenate([mid, far]), core_groups())
+    far_rows = jnp.concatenate([mid, far])
+    fars = gather(far_rows, core_groups())
 
     def pick(part, side, first, planes, fields):
         return part[side, first:first + planes * fields].reshape(planes, fields, 8, 128)
@@ -455,8 +455,8 @@
     rates = window(rates, (nears, 56, 4), (fars, 50, 4), (fars, 84, 2))
     prm = (p1a, p2a, p1b, p2b, rates)
 
-    lower = yh == 0
-    outer = lax.ppermute(jnp.where(lower, big[8:10, 4:6], big[6:8, 4:6]), AX, edge_pairs())
+    outer = jnp.where(lower, nears[0, 64:], nears[1, 64:])
+    outer = jnp.where(left, outer[:8], outer[8:]).reshape(2, 2, 2, 8, 128)
     end = jnp.where(lower, jnp.concatenate([outer, big[2:12, 4:6]]),
                     jnp.concatenate([big[4:14, 4:6], outer]))
     prev = lax.ppermute(end, AX, slice_pairs())
@@ -469,9 +469,7 @@
             chain_kernel, out_shape=shape(16, 2, 8, 128), in_specs=[VM] * 6, out_specs=VM,
             scratch_shapes=scratch, name="chain", compiler_params=SMALL,
         )(state, *prm)
-        first = lax.ppermute(out[:8], AX, turn_pairs(turn))
-        rest = lax.ppermute(out[8:], AX, turn_pairs(turn))
-        moved = jnp.concatenate([first, rest])
+        moved = lax.ppermute(out, AX, turn_pairs(turn))
         moved = gather(moved, core_groups()).reshape(32, 2, 8, 128)
         state = jnp.where(chip == turn + 1, moved, state)
 

time: 144 us -> 143 us (level)
  the two profiles are of different devices: /device:TPU:15 before, /device:TPU:31 now
where the time goes in v8:
time: 143 us
  waiting for transfers between devices  57.2 us (40%)
  blocking collectives  38.2 us (27%)
  starting transfers between devices  32.8 us (23%)
  Pallas kernels  11.1 us (8%)
  other arithmetic  1.43 us (1%)
    ppermute x7, waiting for transfers between devices, program(): moved = lax.ppermute(out, AX, turn_pairs(turn))  49.4 us
    all_gather x11, blocking collectives, gather(): return lax.all_gather(x, AX, axis=0, axis_index_groups=groups, tiled=False)  38.2 us
    ppermute x3, starting transfers between devices, send(): return lax.ppermute(message, AX, split_pairs(step))  13.1 us
    ppermute x1, starting transfers between devices, program(): hi = lax.ppermute(edge(pair[0:4], pair[4:6]), AX, z_pairs(-1))  9.5 us
    pallas_call x7, Pallas kernels, program(): pl.pallas_call(chain_kernel, out_shape=shape(16, 2, 8, 128), in_specs=[VM...  5.92 us
    ppermute x7, starting transfers between devices, program(): moved = lax.ppermute(out, AX, turn_pairs(turn))  5.31 us
    ppermute x1, waiting for transfers between devices, program(): lo = lax.ppermute(edge(pair[4:8], pair[2:4]), AX, z_pairs(1))  5.25 us
    ppermute x1, starting transfers between devices, program(): lo = lax.ppermute(edge(pair[4:8], pair[2:4]), AX, z_pairs(1))  3.55 us
  transfers between devices with their start and end apart: 13, of which 4 were waited for; matrix products, arithmetic and copies ran while one was open for 1% of the time, Pallas kernels for 1%

profile of v8, /device:TPU:31, one launch (start us, length us, event | category | flops | bytes accessed | tf_op | source)
XLA Modules:
  0.0 142.6 jit_solution(9519387777110882413)
XLA Ops:
  0.0 1.7 %pack.1 = f32[4,10,2,8,128]{4,3,2,1,0:T(8,128)} custom-call(f32[1,3,2,4,16,128]{5,4,3,2,1,0:T(8,128)} %nv.1, f32[1,2,4,16,128]{4,3,2,1,0:T(8,128)} %st.1, f32[4,16,128]{2,1,0:T(8,128)} %fr.1, f32[4,16,128]{2,1,0:T(8,128)} %kr.1), custom_call_target="tpu_custom_call" | custom-call | tf_op jit(solution)/shard_map/pack/pallas_call | solution.py:392
  1.7 11.0 %all-gather.pair = f32[8,10,2,8,128]{4,3,2,1,0:T(8,128)S(1)} all-gather(f32[4,10,2,8,128]{4,3,2,1,0:T(8,128)} %pack.1), channel_id=2, replica_groups={{0,1},{32,33},{64,65},{96,97},{128,129},{160,161},{192,193},{224,225},{..., dimensions={0}, use_global_device_ids=true | all-gather | bytes 983040 | tf_op jit(solution)/shard_map/all_gather | solution.py:57
  12.8 3.5 %collective-permute-start = (f32[44,2,8,128]{3,2,1,0:T(8,128)S(1)}, f32[44,2,8,128]{3,2,1,0:T(8,128)S(1)}, u32[]{:S(2)}, u32[]{:S(2)}) collective-permute-start(f32[44,2,8,128]{3,2,1,0:T(8,128)S(1)} %pad_maximum_fusion), channel_id=1, source_target_pairs={{0,2},{32,34},{64,66},{96,98},{128,130},{160,162},{192,194},{224,2... | collective-permute-start | bytes 1081352 | tf_op jit(solution)/shard_map/ppermute | solution.py:403
  16.4 9.5 %collective-permute-start.1 = (f32[44,2,8,128]{3,2,1,0:T(8,128)S(1)}, f32[44,2,8,128]{3,2,1,0:T(8,128)S(1)}, u32[]{:S(2)}, u32[]{:S(2)}) collective-permute-start(f32[44,2,8,128]{3,2,1,0:T(8,128)S(1)} %pad_maximum_fusion.1), channel_id=1, source_target_pairs={{0,30},{32,62},{64,94},{96,126},{128,158},{160,190},{192,222},{224... | collective-permute-start | bytes 1081352 | tf_op jit(solution)/shard_map/ppermute | solution.py:404
  25.9 5.3 %collective-permute-done.lo = f32[44,2,8,128]{3,2,1,0:T(8,128)S(1)} collective-permute-done((f32[44,2,8,128]{3,2,1,0:T(8,128)S(1)}, f32[44,2,8,128]{3,2,1,0:T(8,128)S(1)}, u32[]{:S(2)}, u32[]{:S(2)}) %collective-permute-start) | collective-permute-done | bytes 360480 | tf_op jit(solution)/shard_map/ppermute | solution.py:403
  32.1 1.1 sweep.1
  33.3 4.1 %all-gather.1 = f32[96,8,128]{2,1,0:T(8,128)S(1)} all-gather(f32[48,8,128]{2,1,0:T(8,128)S(1)} %pad_maximum_fusion.3), channel_id=3, replica_groups={{0,32},{64,96},{128,160},{192,224},{256,288},{320,352},{384,416},{448,4..., dimensions={0}, use_global_device_ids=true | all-gather | bytes 589824 | tf_op jit(solution)/shard_map/all_gather | solution.py:57
  37.5 5.3 %collective-permute-start.2 = (f32[58,8,128]{2,1,0:T(8,128)S(1)}, f32[58,8,128]{2,1,0:T(8,128)S(1)}, u32[]{:S(2)}, u32[]{:S(2)}) collective-permute-start(f32[58,8,128]{2,1,0:T(8,128)S(1)} %get-tuple-element.61), channel_id=1, source_target_pairs={{0,4},{32,60},{64,68},{96,124},{128,132},{160,188},{192,196},{224,... | collective-permute-start | bytes 712712 | tf_op jit(solution)/shard_map/ppermute | solution.py:431
  42.8 5.9 %collective-permute-start.3 = (f32[30,8,128]{2,1,0:T(8,128)S(1)}, f32[30,8,128]{2,1,0:T(8,128)S(1)}, u32[]{:S(2)}, u32[]{:S(2)}) collective-permute-start(f32[30,8,128]{2,1,0:T(8,128)S(1)} %pad_maximum_fusion.4), channel_id=1, source_target_pairs={{0,6},{32,58},{64,70},{96,122},{128,134},{160,186},{192,198},{224,... | collective-permute-start | bytes 368648 | tf_op jit(solution)/shard_map/ppermute | solution.py:431
  48.8 1.9 %collective-permute-start.4 = (f32[80,8,128]{2,1,0:T(8,128)S(1)}, f32[80,8,128]{2,1,0:T(8,128)S(1)}, u32[]{:S(2)}, u32[]{:S(2)}) collective-permute-start(f32[80,8,128]{2,1,0:T(8,128)S(1)} %constant_dynamic-update-slice_fusion.6), channel_id=1, source_target_pairs={{0,2},{32,62},{64,66},{96,126},{128,130},{160,190},{192,194},{224,... | collective-permute-start | bytes 983048 | tf_op jit(solution)/shard_map/ppermute | solution.py:431
  50.8 1.6 %collective-permute-done.3 = f32[30,8,128]{2,1,0:T(8,128)S(1)} collective-permute-done((f32[30,8,128]{2,1,0:T(8,128)S(1)}, f32[30,8,128]{2,1,0:T(8,128)S(1)}, u32[]{:S(2)}, u32[]{:S(2)}) %collective-permute-start.3) | collective-permute-done | bytes 122912 | tf_op jit(solution)/shard_map/ppermute | solution.py:431
  52.4 6.1 %all-gather.2 = f32[176,8,128]{2,1,0:T(8,128)S(1)} all-gather(f32[88,8,128]{2,1,0:T(8,128)S(1)} %pad_maximum_fusion.2), channel_id=4, replica_groups={{0,32},{64,96},{128,160},{192,224},{256,288},{320,352},{384,416},{448,4..., dimensions={0}, use_global_device_ids=true | all-gather | bytes 1081344 | tf_op jit(solution)/shard_map/all_gather | solution.py:57
  58.7 2.3 %all-gather.3 = f32[160,8,128]{2,1,0:T(8,128)S(1)} all-gather(f32[80,8,128]{2,1,0:T(8,128)S(1)} %collective-permute-done.4), channel_id=5, replica_groups={{0,32},{64,96},{128,160},{192,224},{256,288},{320,352},{384,416},{448,4..., dimensions={0}, use_global_device_ids=true | all-gather | bytes 983040 | tf_op jit(solution)/shard_map/all_gather | solution.py:57
  63.5 2.0 %all-gather.4 = f32[32,2,8,128]{3,2,1,0:T(8,128)S(1)} all-gather(f32[16,2,8,128]{3,2,1,0:T(8,128)S(1)} %collective-permute-done.5), channel_id=6, replica_groups={{0,32},{64,96},{128,160},{192,224},{256,288},{320,352},{384,416},{448,4..., dimensions={0}, use_global_device_ids=true | all-gather | bytes 393216 | tf_op jit(solution)/shard_map/all_gather | solution.py:57
  67.1 2.0 %all-gather.5 = f32[32,2,8,128]{3,2,1,0:T(8,128)S(1)} all-gather(f32[16,2,8,128]{3,2,1,0:T(8,128)S(1)} %collective-permute-done.6), channel_id=7, replica_groups={{0,32},{64,96},{128,160},{192,224},{256,288},{320,352},{384,416},{448,4..., dimensions={0}, use_global_device_ids=true | all-gather | bytes 393216 | tf_op jit(solution)/shard_map/all_gather | solution.py:57
  70.7 2.0 %all-gather.6 = f32[32,2,8,128]{3,2,1,0:T(8,128)S(1)} all-gather(f32[16,2,8,128]{3,2,1,0:T(8,128)S(1)} %collective-permute-done.7), channel_id=8, replica_groups={{0,32},{64,96},{128,160},{192,224},{256,288},{320,352},{384,416},{448,4..., dimensions={0}, use_global_device_ids=true | all-gather | bytes 393216 | tf_op jit(solution)/shard_map/all_gather | solution.py:57
  74.3 2.0 %all-gather.7 = f32[32,2,8,128]{3,2,1,0:T(8,128)S(1)} all-gather(f32[16,2,8,128]{3,2,1,0:T(8,128)S(1)} %collective-permute-done.8), channel_id=9, replica_groups={{0,32},{64,96},{128,160},{192,224},{256,288},{320,352},{384,416},{448,4..., dimensions={0}, use_global_device_ids=true | all-gather | bytes 393216 | tf_op jit(solution)/shard_map/all_gather | solution.py:57
  78.8 2.0 %all-gather.8 = f32[32,2,8,128]{3,2,1,0:T(8,128)S(1)} all-gather(f32[16,2,8,128]{3,2,1,0:T(8,128)S(1)} %collective-permute-done.9), channel_id=10, replica_groups={{0,32},{64,96},{128,160},{192,224},{256,288},{320,352},{384,416},{448,4..., dimensions={0}, use_global_device_ids=true | all-gather | bytes 393216 | tf_op jit(solution)/shard_map/all_gather | solution.py:57
  82.4 1.3 collective-permute-start.12
  83.7 2.8 %all-gather.9 = f32[32,2,8,128]{3,2,1,0:T(8,128)S(1)} all-gather(f32[16,2,8,128]{3,2,1,0:T(8,128)S(1)} %collective-permute-done.10), channel_id=11, replica_groups={{0,32},{64,96},{128,160},{192,224},{256,288},{320,352},{384,416},{448,4..., dimensions={0}, use_global_device_ids=true | all-gather | bytes 393216 | tf_op jit(solution)/shard_map/all_gather | solution.py:57
  87.4 1.3 collective-permute-start.11
  88.7 49.4 %collective-permute-done.11 = f32[16,2,8,128]{3,2,1,0:T(8,128)S(1)} collective-permute-done((f32[16,2,8,128]{3,2,1,0:T(8,128)S(1)}, f32[16,2,8,128]{3,2,1,0:T(8,128)S(1)}, u32[]{:S(2)}, u32[]{:S(2)}) %collective-permute-start.11) | collective-permute-done | bytes 131104 | tf_op jit(solution)/shard_map/ppermute | solution.py:472
  138.2 2.0 %all-gather.10 = f32[32,2,8,128]{3,2,1,0:T(8,128)S(1)} all-gather(f32[16,2,8,128]{3,2,1,0:T(8,128)S(1)} %collective-permute-done.11), channel_id=12, replica_groups={{0,32},{64,96},{128,160},{192,224},{256,288},{320,352},{384,416},{448,4..., dimensions={0}, use_global_device_ids=true | all-gather | bytes 393216 | tf_op jit(solution)/shard_map/all_gather | solution.py:57
  140.2 2.4 %last.1 = f32[1,3,2,4,16,128]{5,4,3,2,1,0:T(8,128)} custom-call(s32[2]{0:T(128)S(1)} %pad_add_fusion.sc, f32[32,2,8,128]{3,2,1,0:T(8,128)S(1)} %broadcast_select_fusion.6.a, f32[28,3,8,128]{3,2,1,0:T(8,128)S(1)} %get-tuple-element.62.p1a, f32[24,3,8,128]{3,2,1,0:T(8,128)S(1)} %get-tuple-element.64.p2a, f32[20,3,8,128]{3,2,1,0:T(8,128)S(1)} %get-tuple-element.63.p1b, ...), custom_call_target="tpu_custom_call" | custom-call | tf_op jit(solution)/shard_map/last/pallas_call | solution.py:477
  (105 shorter events, 13.3 us)
Async XLA Ops:
  12.8 18.4 %collective-permute-start = (f32[44,2,8,128]{3,2,1,0:T(8,128)S(1)}, f32[44,2,8,128]{3,2,1,0:T(8,128)S(1)}, u32[]{:S(2)}, u32[]{:S(2)}) collective-permute-start(f32[44,2,8,128]{3,2,1,0:T(8,128)S(1)} %pad_maximum_fusion), channel_id=1, source_target_pairs={{0,2},{32,34},{64,66},{96,98},{128,130},{160,162},{192,194},{224,2... | collective-permute-start | bytes 1081352 | tf_op jit(solution)/shard_map/ppermute | solution.py:403
  16.4 15.7 %collective-permute-start.1 = (f32[44,2,8,128]{3,2,1,0:T(8,128)S(1)}, f32[44,2,8,128]{3,2,1,0:T(8,128)S(1)}, u32[]{:S(2)}, u32[]{:S(2)}) collective-permute-start(f32[44,2,8,128]{3,2,1,0:T(8,128)S(1)} %pad_maximum_fusion.1), channel_id=1, source_target_pairs={{0,30},{32,62},{64,94},{96,126},{128,158},{160,190},{192,222},{224... | collective-permute-start | bytes 1081352 | tf_op jit(solution)/shard_map/ppermute | solution.py:404
  37.5 14.8 %collective-permute-start.2 = (f32[58,8,128]{2,1,0:T(8,128)S(1)}, f32[58,8,128]{2,1,0:T(8,128)S(1)}, u32[]{:S(2)}, u32[]{:S(2)}) collective-permute-start(f32[58,8,128]{2,1,0:T(8,128)S(1)} %get-tuple-element.61), channel_id=1, source_target_pairs={{0,4},{32,60},{64,68},{96,124},{128,132},{160,188},{192,196},{224,... | collective-permute-start | bytes 712712 | tf_op jit(solution)/shard_map/ppermute | solution.py:431
  42.8 9.5 %collective-permute-start.3 = (f32[30,8,128]{2,1,0:T(8,128)S(1)}, f32[30,8,128]{2,1,0:T(8,128)S(1)}, u32[]{:S(2)}, u32[]{:S(2)}) collective-permute-start(f32[30,8,128]{2,1,0:T(8,128)S(1)} %pad_maximum_fusion.4), channel_id=1, source_target_pairs={{0,6},{32,58},{64,70},{96,122},{128,134},{160,186},{192,198},{224,... | collective-permute-start | bytes 368648 | tf_op jit(solution)/shard_map/ppermute | solution.py:431
  48.8 9.9 %collective-permute-start.4 = (f32[80,8,128]{2,1,0:T(8,128)S(1)}, f32[80,8,128]{2,1,0:T(8,128)S(1)}, u32[]{:S(2)}, u32[]{:S(2)}) collective-permute-start(f32[80,8,128]{2,1,0:T(8,128)S(1)} %constant_dynamic-update-slice_fusion.6), channel_id=1, source_target_pairs={{0,2},{32,62},{64,66},{96,126},{128,130},{160,190},{192,194},{224,... | collective-permute-start | bytes 983048 | tf_op jit(solution)/shard_map/ppermute | solution.py:431
  61.0 0.8 copy-start
  62.8 0.7 collective-permute-start.5
  66.4 0.7 collective-permute-start.6
  70.0 0.8 collective-permute-start.7
  73.6 0.7 collective-permute-start.8
  77.2 1.6 %collective-permute-start.9 = (f32[16,2,8,128]{3,2,1,0:T(8,128)S(1)}, f32[16,2,8,128]{3,2,1,0:T(8,128)S(1)}, u32[]{:S(2)}, u32[]{:S(2)}) collective-permute-start(f32[16,2,8,128]{3,2,1,0:T(8,128)S(1)} %chain.11), channel_id=1, source_target_pairs={{256,324},{288,381},{257,325},{289,380},{258,326},{290,383},{259,3... | collective-permute-start | bytes 393224 | tf_op jit(solution)/shard_map/ppermute | solution.py:472
  81.7 2.0 %collective-permute-start.10 = (f32[16,2,8,128]{3,2,1,0:T(8,128)S(1)}, f32[16,2,8,128]{3,2,1,0:T(8,128)S(1)}, u32[]{:S(2)}, u32[]{:S(2)}) collective-permute-start(f32[16,2,8,128]{3,2,1,0:T(8,128)S(1)} %chain.12), channel_id=1, source_target_pairs={{320,388},{352,445},{321,389},{353,444},{322,390},{354,447},{323,3... | collective-permute-start | bytes 393224 | tf_op jit(solution)/shard_map/ppermute | solution.py:472
  82.4 6.3 %collective-permute-start.12 = (f32[12,2,2,8,128]{4,3,2,1,0:T(8,128)S(1)}, f32[12,2,2,8,128]{4,3,2,1,0:T(8,128)S(1)}, u32[]{:S(2)}, u32[]{:S(2)}) collective-permute-start(f32[12,2,2,8,128]{4,3,2,1,0:T(8,128)S(1)} %maximum_select_fusion.end), channel_id=1, source_target_pairs={{0,32},{1,33},{2,34},{3,35},{4,36},{5,37},{6,38},{7,39},{8,40},{9,... | collective-permute-start | bytes 589832 | tf_op jit(solution)/shard_map/ppermute | solution.py:462
  87.4 50.8 %collective-permute-start.11 = (f32[16,2,8,128]{3,2,1,0:T(8,128)S(1)}, f32[16,2,8,128]{3,2,1,0:T(8,128)S(1)}, u32[]{:S(2)}, u32[]{:S(2)}) collective-permute-start(f32[16,2,8,128]{3,2,1,0:T(8,128)S(1)} %chain.13), channel_id=1, source_target_pairs={{384,452},{416,509},{385,453},{417,508},{386,454},{418,511},{387,4... | collective-permute-start | bytes 393224 | tf_op jit(solution)/shard_map/ppermute | solution.py:472
